TPU v7x, 32 devices: a whole 2x2x4 slice. The times are simulated.
32 devices in a mesh: dp: 2 (over y), fsdp: 2 (over x), expert: 8 (over z, core).
Axes of the slice: x: 2, y: 2, z: 4, core: 2. Of those that a mesh axis runs over, the one named last changes fastest.
Arguments:
- tokens: bfloat16 [8192, 2048], P(('dp', 'fsdp', 'expert')), may hold values from -6 to 6
- expert_ids: int32 [8192, 8], P(('dp', 'fsdp', 'expert')), may hold values from 0 to 127, all different within a row; in each aligned block of 256 rows (0 to 255, 256 to 511, ...) at most 24 rows name the same one
- gate_units: int32 [8192, 8], P(('dp', 'fsdp', 'expert')), may hold values from 1 to 256
- expert_weights: bfloat16 [8, 2048, 3, 768], P('expert', ('dp', 'fsdp')), may hold values from -0.125 to 0.125
- out_grad: bfloat16 [8192, 2048], P(('dp', 'fsdp', 'expert')), may hold values from -6 to 6
Outputs:
- moe_out: bfloat16 [8192, 2048], P(('dp', 'fsdp', 'expert'))
- token_grad: bfloat16 [8192, 2048], P(('dp', 'fsdp', 'expert'))
- weight_grad: bfloat16 [8, 2048, 3, 768], P('expert', ('dp', 'fsdp'))
Inputs may be any that keep to these rules, and one draw needn't show every extreme that they name: `expert_ids`: each row names 8 different experts; the 256 rows of one device name one expert at most 24 times.
All inputs are finite; a program needn't handle non-finite values.
Results may differ from a plain program's by a relative error of at most 0.018.
Values may be sent and summed in bfloat16 or wider, within the bound.
No kernel may reach another device: no remote copies, remote signals or barrier semaphores. Data moves between devices by JAX's collectives and lax.ppermute only.
A program may use at most 128 MiB of HBM per device.

v0:
```python
import jax
import jax.numpy as jnp
from jax import lax
from jax.sharding import PartitionSpec as P


CAP = 24
ALL = ("dp", "fsdp", "expert")
F32 = jnp.float32
BF16 = jnp.bfloat16


def route_tables(expert_ids, gate_units, slot_expert, slot_rank):
    tok_count, _ = expert_ids.shape
    same = expert_ids[:, :, None] == slot_expert[None, None, :]
    named = jnp.sum(same.astype(F32), axis=1)
    gates = jnp.sum(jnp.where(same, gate_units.astype(F32)[:, :, None], 0.0), axis=1)
    order = jnp.arange(tok_count, dtype=jnp.int32)
    earlier = (order[:, None] > order[None, :]).astype(BF16)
    before = jnp.dot(earlier, named.astype(BF16), preferred_element_type=F32)
    hit = (named > 0.5) & (before == slot_rank.astype(F32)[None, :])
    dispatch = hit.astype(BF16)
    combine = jnp.where(hit, gates / 256.0, 0.0).astype(BF16)
    return dispatch, combine


def contract(left, right, left_dim, right_dim):
    return lax.dot_general(
        left, right, (((left_dim,), (right_dim,)), ((), ())), preferred_element_type=F32
    )


class Moves:
    def __init__(self, dp, fsdp, experts):
        self.shape = (dp, fsdp, experts)

    def move(self, value, where):
        dp, fsdp, experts = self.shape
        pairs = []
        for d in range(dp):
            for f in range(fsdp):
                for e in range(experts):
                    nd, nf, ne = where(d, f, e)
                    pairs.append(((d * fsdp + f) * experts + e, (nd * fsdp + nf) * experts + ne))
        return lax.ppermute(value, ALL, pairs)

    def core(self, value):
        return self.move(value, lambda d, f, e: (d, f, e ^ 1))

    def weight_pair(self, value):
        return self.move(value, lambda d, f, e: (d, 1 - f, e) if e % 2 == 0 else (1 - d, f, e))

    def column_pair(self, value):
        return self.move(value, lambda d, f, e: (1 - d, f, e) if e % 2 == 0 else (d, 1 - f, e))

    def along_z(self, value, step):
        return self.move(value, lambda d, f, e: (d, f, e ^ (2 * step)))


def z_order(steps):
    return sorted(range(1, steps), key=lambda step: (step < 2, step))


def paired(tokens, expert_ids, gate_units, expert_weights, out_grad):
    return paired_body(tokens, expert_ids, gate_units, expert_weights, out_grad)


def paired_body(tokens, expert_ids, gate_units, expert_weights, out_grad):
    moves = Moves(*(lax.axis_size(name) for name in ALL))
    steps = moves.shape[2] // 2
    model_width = tokens.shape[1]
    quarter_width = model_width // 4
    half_width = model_width // 2
    hidden = expert_weights.shape[3]
    own_e = lax.axis_index("expert")
    own_z, own_c = own_e // 2, own_e % 2
    own_q = lax.axis_index("dp") * 2 + lax.axis_index("fsdp")
    quarter = (own_q, own_q ^ (1 + own_c), own_q ^ (2 - own_c), own_q ^ 3)
    half = steps * CAP

    weights_own = expert_weights[0]
    weights_far = moves.weight_pair(weights_own)
    pair = (weights_own, weights_far)

    slot = jnp.arange(2 * half, dtype=jnp.int32)
    slot_expert = ((slot % half // CAP) ^ own_z) * 2 + ((slot // half) ^ own_c)
    dispatch, combine = route_tables(expert_ids, gate_units, slot_expert, slot % CAP)

    def interleaved(first, second):
        width = first.shape[1]
        both = (first.reshape(steps, CAP, width), second.reshape(steps, CAP, width))
        return jnp.stack(both, axis=1).reshape(2 * half, width)

    def cut(array, *which):
        return jnp.concatenate(
            [array[:, i * quarter_width : (i + 1) * quarter_width] for i in which], axis=1
        )

    def send_local(table, source):
        ordered = jnp.concatenate(
            [
                lax.dynamic_slice_in_dim(source, index * quarter_width, quarter_width, 1)
                for index in quarter
            ],
            axis=1,
        )
        other = contract(table[:, half:], ordered, 0, 0).astype(BF16)
        came = moves.core(other)
        same = contract(table[:, :half], ordered, 0, 0).astype(BF16)
        own = interleaved(cut(same, 0, 1), cut(came, 0, 2))
        out = interleaved(cut(same, 2, 3), cut(came, 1, 3))
        return own, moves.column_pair(out)

    def by_z(rows):
        parts = [value.shape[0] // steps for value in rows]
        order = z_order(steps)
        pieces = []
        fenced = lax.optimization_barrier(tuple(rows))
        for step in order:
            piece = [v[step * n : (step + 1) * n] for v, n in zip(fenced, parts)]
            pieces.append(jnp.concatenate(piece) if len(piece) > 1 else piece[0])
        pieces = lax.optimization_barrier(tuple(pieces))
        got = {0: jnp.concatenate([v[:n] for v, n in zip(rows, parts)])}
        for step, piece in zip(order, pieces):
            got[step] = moves.along_z(piece, step)
        whole, low = [], 0
        for n in parts:
            whole.append(jnp.concatenate([got[i][low : low + n] for i in range(steps)]))
            low += n
        return whole

    def give_back_in(table, own, near):
        out = moves.column_pair(near)

        def source(array, index):
            return array.reshape(steps, 2, CAP, half_width)[:, index].reshape(half, half_width)

        other = jnp.concatenate([source(own, 1), source(out, 1)], axis=1)
        came = moves.core(other)
        same = jnp.concatenate([source(own, 0), source(out, 0)], axis=1)
        rows = jnp.concatenate([same, cut(came, 0, 2, 1, 3)])
        result = contract(table, rows, 1, 0).astype(BF16)
        answer = jnp.zeros((table.shape[0], model_width), BF16)
        for index in range(4):
            answer = lax.dynamic_update_slice_in_dim(
                answer,
                result[:, index * quarter_width : (index + 1) * quarter_width],
                quarter[index] * quarter_width,
                1,
            )
        return answer

    def inward(rows, which):
        return contract(rows[:, :quarter_width], pair[0][:, which], 1, 0) + contract(
            rows[:, quarter_width:], pair[1][:, which], 1, 0
        )

    def outward(terms):
        return jnp.concatenate(
            [
                sum(contract(value, pair[i][:, which], 1, 1) for value, which in terms)
                for i in (0, 1)
            ],
            axis=1,
        ).astype(BF16)

    def wide(rows, *which):
        return jnp.concatenate([inward(rows, i) for i in which], axis=1)

    rows_own, rows_near = send_local(dispatch, tokens)
    (rows_own,) = by_z([rows_own])
    (rows_near,) = by_z([rows_near])
    scaled_own, scaled_near = by_z(send_local(combine, out_grad))

    part_own = wide(rows_own, 0, 1)
    message = part_own.astype(BF16)
    near_extra = moves.column_pair(message)
    part_near = wide(rows_near, 0, 1)
    message = part_near.astype(BF16)
    own_extra = moves.column_pair(message)

    def act(part, extra):
        total = part + extra.astype(F32)
        gate_act, up_act = total[:, :hidden], total[:, hidden:]
        sigmoid_gate = jax.nn.sigmoid(gate_act)
        swish_gate = gate_act * sigmoid_gate
        slope = up_act * sigmoid_gate * (1.0 + gate_act * (1.0 - sigmoid_gate))
        return lax.optimization_barrier(((swish_gate * up_act).astype(BF16), slope, swish_gate))

    act_near, slope_near, swish_near = act(part_near, near_extra)
    out_near = outward([(act_near, 2)])
    act_own, slope_own, swish_own = act(part_own, own_extra)
    out_own = outward([(act_own, 2)])
    back_near, back_own = by_z([out_near, out_own])

    hid_own, hid_near = wide(scaled_own, 2), wide(scaled_near, 2)
    message = jnp.concatenate([hid_near, hid_own]).astype(BF16)
    extra = moves.column_pair(message)
    hid_own = hid_own + extra[: 2 * half].astype(F32)
    hid_near = hid_near + extra[2 * half :].astype(F32)
    gg_near, ug_near = (hid_near * slope_near).astype(BF16), (hid_near * swish_near).astype(BF16)
    gg_own, ug_own = (hid_own * slope_own).astype(BF16), (hid_own * swish_own).astype(BF16)

    rows = jnp.concatenate([rows_own, rows_near])
    scaled = jnp.concatenate([scaled_own, scaled_near])
    activation = jnp.concatenate([act_own, act_near])
    gate_grad = jnp.concatenate([gg_own, gg_near])
    up_grad = jnp.concatenate([ug_own, ug_near])
    first, second = slice(0, quarter_width), slice(quarter_width, half_width)
    down_far = contract(scaled[:, second], activation, 0, 0).astype(BF16)
    down_far = moves.weight_pair(down_far)
    grad_near = outward([(gg_near, 0), (ug_near, 1)])
    (grad_near,) = by_z([grad_near])
    in_far = jnp.stack(
        [contract(rows[:, second], value, 0, 0) for value in (gate_grad, up_grad)]
    ).astype(BF16)
    in_far = moves.weight_pair(in_far)
    grad_own = outward([(gg_own, 0), (ug_own, 1)])
    (grad_own,) = by_z([grad_own])
    moe_out = give_back_in(combine, back_own, back_near)
    token_grad = give_back_in(dispatch, grad_own, grad_near)
    weight_grad = jnp.stack(
        [
            contract(rows[:, first], gate_grad, 0, 0) + in_far[0].astype(F32),
            contract(rows[:, first], up_grad, 0, 0) + in_far[1].astype(F32),
            contract(scaled[:, first], activation, 0, 0) + down_far.astype(F32),
        ],
        axis=1,
    ).astype(BF16)[None]
    return moe_out, token_grad, weight_grad


def gathered(tokens, expert_ids, gate_units, expert_weights, out_grad):
    experts = lax.axis_size("expert")
    slots = experts * CAP
    width = tokens.shape[1]
    hidden = expert_weights.shape[3]
    slot = jnp.arange(slots, dtype=jnp.int32)
    dispatch, combine = route_tables(expert_ids, gate_units, slot // CAP, slot % CAP)

    def exchange(rows):
        return lax.all_to_all(
            rows.reshape(experts, CAP, width), "expert", split_axis=0, concat_axis=0, tiled=True
        ).reshape(slots, width)

    slot_rows = exchange(contract(dispatch, tokens, 0, 0).astype(BF16))
    scaled = exchange(contract(combine, out_grad, 0, 0).astype(BF16))
    full = lax.all_gather(expert_weights, ("dp", "fsdp"), axis=1, tiled=True)[0]
    gate_act = contract(slot_rows, full[:, 0], 1, 0)
    up_act = contract(slot_rows, full[:, 1], 1, 0)
    sigmoid_gate = jax.nn.sigmoid(gate_act)
    swish_gate = gate_act * sigmoid_gate
    activation = (swish_gate * up_act).astype(BF16)
    result = contract(activation, full[:, 2], 1, 1).astype(BF16)
    moe_out = contract(combine, exchange(result), 1, 0).astype(BF16)
    hidden_grad = contract(scaled, full[:, 2], 1, 0)
    gate_grad = (
        hidden_grad * up_act * sigmoid_gate * (1.0 + gate_act * (1.0 - sigmoid_gate))
    ).astype(BF16)
    up_grad = (hidden_grad * swish_gate).astype(BF16)
    row_grad = (
        contract(gate_grad, full[:, 0], 1, 1) + contract(up_grad, full[:, 1], 1, 1)
    ).astype(BF16)
    token_grad = contract(dispatch, exchange(row_grad), 1, 0).astype(BF16)
    term = jnp.stack(
        [
            contract(slot_rows, gate_grad, 0, 0),
            contract(slot_rows, up_grad, 0, 0),
            contract(scaled, activation, 0, 0),
        ],
        axis=1,
    ).astype(BF16)
    summed = lax.psum_scatter(term, ("dp", "fsdp"), scatter_dimension=0, tiled=True)
    return moe_out, token_grad, summed.reshape(1, -1, 3, hidden)


def solution(mesh):
    placed = P(ALL, None)
    weights = P("expert", ("dp", "fsdp"), None, None)
    sizes = mesh.shape
    steps = sizes["expert"] // 2
    small = sizes["dp"] == 2 and sizes["fsdp"] == 2 and steps > 1
    small = small and sizes["expert"] % 2 == 0 and steps & (steps - 1) == 0
    return jax.shard_map(
        paired if small else gathered,
        mesh=mesh,
        in_specs=(placed, placed, placed, weights, placed),
        out_specs=(placed, placed, weights),
        check_vma=False,
    )
```

profile of v0, /device:TPU:0, one launch (start us, length us, event | category | flops | bytes accessed | tf_op | source)
XLA Modules:
  0.0 136.6 jit_solution(317712680071620495)
XLA Ops:
  0.7 0.7 convert_element_type.110
  1.4 1.0 fusion.1
  2.7 1.7 %constant_dynamic-slice_fusion.3 = (bf16[256,512]{1,0:T(8,128)(2,1)S(1)}, bf16[256,512]{1,0:T(8,128)(2,1)S(1)}, bf16[256,512]{1,0:T(8,128)(2,1)S(1)}, bf16[256,5...) fusion(bf16[256,2048]{1,0:T(8,128)(2,1)} %param.9, ...), kind=kLoop, calls=%fused_computation.210 | loop fusion | bytes 4194320 | tf_op jit(solution)/shard_map/dynamic_slice | solution.py:102
  4.7 0.6 collective-permute-start
  5.6 0.7 copy-done
  6.3 3.0 %collective-permute-start.4 = (bf16[512,3,768]{2,0,1:T(8,128)(2,1)S(1)}, bf16[512,3,768]{2,0,1:T(8,128)(2,1)S(1)}, u32[]{:S(2)}, u32[]{:S(2)}) collective-permute-start(bf16[512,3,768]{2,0,1:T(8,128)(2,1)S(1)} %bitcast.119), channel_id=1, source_target_pairs={{0,8},{1,17},{2,10},{3,19},{4,12},{5,21},{6,14},{7,23},{8,0},{9,25... | collective-permute-start | bytes 7077896 | tf_op jit(solution)/shard_map/ppermute | solution.py:45
  10.3 1.6 %collective-permute-start.1 = (bf16[48,1024]{1,0:T(8,128)(2,1)S(1)}, bf16[48,1024]{1,0:T(8,128)(2,1)S(1)}, u32[]{:S(2)}, u32[]{:S(2)}) collective-permute-start(bf16[48,1024]{1,0:T(8,128)(2,1)S(1)} %get-tuple-element.31), channel_id=1, source_target_pairs={{0,2},{1,3},{2,0},{3,1},{4,6},{5,7},{6,4},{7,5},{8,10},{9,11},{10,... | collective-permute-start | bytes 294920 | tf_op jit(solution)/shard_map/ppermute | solution.py:45
  12.0 2.6 %collective-permute-start.2 = (bf16[48,1024]{1,0:T(8,128)(2,1)S(1)}, bf16[48,1024]{1,0:T(8,128)(2,1)S(1)}, u32[]{:S(2)}, u32[]{:S(2)}) collective-permute-start(bf16[48,1024]{1,0:T(8,128)(2,1)S(1)} %get-tuple-element.32), channel_id=1, source_target_pairs={{0,4},{1,5},{2,6},{3,7},{4,0},{5,1},{6,2},{7,3},{8,12},{9,13},{10,... | collective-permute-start | bytes 294920 | tf_op jit(solution)/shard_map/ppermute | solution.py:45
  14.8 1.6 %collective-permute-start.5 = (bf16[192,1024]{1,0:T(8,128)(2,1)S(1)}, bf16[192,1024]{1,0:T(8,128)(2,1)S(1)}, u32[]{:S(2)}, u32[]{:S(2)}) collective-permute-start(bf16[192,1024]{1,0:T(8,128)(2,1)S(1)} %bitcast.158), channel_id=1, source_target_pairs={{0,16},{1,9},{2,18},{3,11},{4,20},{5,13},{6,22},{7,15},{8,24},{9,1... | collective-permute-start | bytes 1179656 | tf_op jit(solution)/shard_map/ppermute | solution.py:45
  16.5 0.9 collective-permute-start.17
  17.4 4.7 %collective-permute-done.2 = bf16[48,1024]{1,0:T(8,128)(2,1)S(1)} collective-permute-done((bf16[48,1024]{1,0:T(8,128)(2,1)S(1)}, bf16[48,1024]{1,0:T(8,128)(2,1)S(1)}, u32[]{:S(2)}, u32[]{:S(2)}) %collective-permute-start.2) | collective-permute-done | bytes 98336 | tf_op jit(solution)/shard_map/ppermute | solution.py:45
  22.2 4.7 %collective-permute-done.5 = bf16[192,1024]{1,0:T(8,128)(2,1)S(1)} collective-permute-done((bf16[192,1024]{1,0:T(8,128)(2,1)S(1)}, bf16[192,1024]{1,0:T(8,128)(2,1)S(1)}, u32[]{:S(2)}, u32[]{:S(2)}) %collective-permute-start.5) | collective-permute-done | bytes 393248 | tf_op jit(solution)/shard_map/ppermute | solution.py:45
  26.9 0.7 collective-permute-start.6
  27.7 3.5 %collective-permute-start.7 = (bf16[48,1024]{1,0:T(8,128)(2,1)S(1)}, bf16[48,1024]{1,0:T(8,128)(2,1)S(1)}, u32[]{:S(2)}, u32[]{:S(2)}) collective-permute-start(bf16[48,1024]{1,0:T(8,128)(2,1)S(1)} %get-tuple-element.35), channel_id=1, source_target_pairs={{0,4},{1,5},{2,6},{3,7},{4,0},{5,1},{6,2},{7,3},{8,12},{9,13},{10,... | collective-permute-start | bytes 294920 | tf_op jit(solution)/shard_map/ppermute | solution.py:45
  31.4 3.9 %collective-permute-done.17 = bf16[192,1024]{1,0:T(8,128)(2,1)S(1)} collective-permute-done((bf16[192,1024]{1,0:T(8,128)(2,1)S(1)}, bf16[192,1024]{1,0:T(8,128)(2,1)S(1)}, u32[]{:S(2)}, u32[]{:S(2)}) %collective-permute-start.17) | collective-permute-done | bytes 393248 | tf_op jit(solution)/shard_map/ppermute | solution.py:45
  35.5 0.7 collective-permute-start.18
  36.2 3.5 %collective-permute-start.19 = (bf16[96,1024]{1,0:T(8,128)(2,1)S(1)}, bf16[96,1024]{1,0:T(8,128)(2,1)S(1)}, u32[]{:S(2)}, u32[]{:S(2)}) collective-permute-start(bf16[96,1024]{1,0:T(8,128)(2,1)S(1)} %pad_maximum_fusion.38), channel_id=1, source_target_pairs={{0,4},{1,5},{2,6},{3,7},{4,0},{5,1},{6,2},{7,3},{8,12},{9,13},{10,... | collective-permute-start | bytes 589832 | tf_op jit(solution)/shard_map/ppermute | solution.py:45
  40.1 5.0 %collective-permute-done.18 = bf16[96,1024]{1,0:T(8,128)(2,1)S(1)} collective-permute-done((bf16[96,1024]{1,0:T(8,128)(2,1)S(1)}, bf16[96,1024]{1,0:T(8,128)(2,1)S(1)}, u32[]{:S(2)}, u32[]{:S(2)}) %collective-permute-start.18) | collective-permute-done | bytes 196640 | tf_op jit(solution)/shard_map/ppermute | solution.py:45
  45.2 7.8 %collective-permute-done.19 = bf16[96,1024]{1,0:T(8,128)(2,1)S(1)} collective-permute-done((bf16[96,1024]{1,0:T(8,128)(2,1)S(1)}, bf16[96,1024]{1,0:T(8,128)(2,1)S(1)}, u32[]{:S(2)}, u32[]{:S(2)}) %collective-permute-start.19) | collective-permute-done | bytes 196640 | tf_op jit(solution)/shard_map/ppermute | solution.py:45
  54.6 1.2 collective-permute-start.21
  56.1 0.3 convolution_add_fusion.3
  56.7 0.3 convolution_add_fusion.2
  57.1 1.0 collective-permute-start.9
  59.6 1.2 collective-permute-start.10
  60.7 10.1 %collective-permute-done.9 = bf16[192,1536]{1,0:T(8,128)(2,1)S(1)} collective-permute-done((bf16[192,1536]{1,0:T(8,128)(2,1)S(1)}, bf16[192,1536]{1,0:T(8,128)(2,1)S(1)}, u32[]{:S(2)}, u32[]{:S(2)}) %collective-permute-start.9) | collective-permute-done | bytes 589856 | tf_op jit(solution)/shard_map/ppermute | solution.py:45
  71.3 5.9 %collective-permute-done.10 = bf16[192,1536]{1,0:T(8,128)(2,1)S(1)} collective-permute-done((bf16[192,1536]{1,0:T(8,128)(2,1)S(1)}, bf16[192,1536]{1,0:T(8,128)(2,1)S(1)}, u32[]{:S(2)}, u32[]{:S(2)}) %collective-permute-start.10) | collective-permute-done | bytes 589856 | tf_op jit(solution)/shard_map/ppermute | solution.py:45
  77.9 0.4 fusion.41
  78.3 0.4 fusion.9
  78.7 0.4 fusion.45
  79.2 0.4 fusion.10
  79.6 0.4 fusion.40
  80.0 0.6 fusion.4
  80.7 0.6 fusion.5
  81.3 0.4 fusion.11
  81.7 0.4 fusion.44
  82.1 0.4 fusion.12
  82.6 0.4 convolution_convert_fusion.12
  83.0 0.4 convolution_convert_fusion.11
  83.6 1.6 %collective-permute-start.30 = (bf16[2,512,768]{2,1,0:T(8,128)(2,1)S(1)}, bf16[2,512,768]{2,1,0:T(8,128)(2,1)S(1)}, u32[]{:S(2)}, u32[]{:S(2)}) collective-permute-start(bf16[2,512,768]{2,1,0:T(8,128)(2,1)S(1)} %pad_maximum_fusion.1), channel_id=1, source_target_pairs={{0,8},{1,17},{2,10},{3,19},{4,12},{5,21},{6,14},{7,23},{8,0},{9,25... | collective-permute-start | bytes 4718600 | tf_op jit(solution)/shard_map/ppermute | solution.py:45
  85.2 0.4 convolution_convert_fusion.10
  85.6 0.6 convolution_convert_fusion.6
  86.3 0.6 collective-permute-start.31
  86.9 3.0 %collective-permute-start.22 = (bf16[48,1024]{1,0:T(8,128)(2,1)S(1)}, bf16[48,1024]{1,0:T(8,128)(2,1)S(1)}, u32[]{:S(2)}, u32[]{:S(2)}) collective-permute-start(bf16[48,1024]{1,0:T(8,128)(2,1)S(1)} %get-tuple-element.51), channel_id=1, source_target_pairs={{0,2},{1,3},{2,0},{3,1},{4,6},{5,7},{6,4},{7,5},{8,10},{9,11},{10,... | collective-permute-start | bytes 294920 | tf_op jit(solution)/shard_map/ppermute | solution.py:45
  89.9 1.0 collective-permute-start.23
  90.9 1.4 %collective-permute-start.24 = (bf16[48,1024]{1,0:T(8,128)(2,1)S(1)}, bf16[48,1024]{1,0:T(8,128)(2,1)S(1)}, u32[]{:S(2)}, u32[]{:S(2)}) collective-permute-start(bf16[48,1024]{1,0:T(8,128)(2,1)S(1)} %get-tuple-element.53), channel_id=1, source_target_pairs={{0,6},{1,7},{2,4},{3,5},{4,2},{5,3},{6,0},{7,1},{8,14},{9,15},{10,... | collective-permute-start | bytes 294920 | tf_op jit(solution)/shard_map/ppermute | solution.py:45
  92.3 0.4 convolution_convert_fusion.9
  92.9 1.2 collective-permute-done.22
  94.1 1.1 collective-permute-start.25
  95.2 5.5 %collective-permute-done.23 = bf16[48,1024]{1,0:T(8,128)(2,1)S(1)} collective-permute-done((bf16[48,1024]{1,0:T(8,128)(2,1)S(1)}, bf16[48,1024]{1,0:T(8,128)(2,1)S(1)}, u32[]{:S(2)}, u32[]{:S(2)}) %collective-permute-start.23) | collective-permute-done | bytes 98336 | tf_op jit(solution)/shard_map/ppermute | solution.py:45
  100.8 2.1 %collective-permute-start.27 = (bf16[48,1024]{1,0:T(8,128)(2,1)S(1)}, bf16[48,1024]{1,0:T(8,128)(2,1)S(1)}, u32[]{:S(2)}, u32[]{:S(2)}) collective-permute-start(bf16[48,1024]{1,0:T(8,128)(2,1)S(1)} %get-tuple-element.58), channel_id=1, source_target_pairs={{0,6},{1,7},{2,4},{3,5},{4,2},{5,3},{6,0},{7,1},{8,14},{9,15},{10,... | collective-permute-start | bytes 294920 | tf_op jit(solution)/shard_map/ppermute | solution.py:45
  102.9 1.8 %collective-permute-start.11 = (bf16[96,1024]{1,0:T(8,128)(2,1)S(1)}, bf16[96,1024]{1,0:T(8,128)(2,1)S(1)}, u32[]{:S(2)}, u32[]{:S(2)}) collective-permute-start(bf16[96,1024]{1,0:T(8,128)(2,1)S(1)} %pad_maximum_fusion.35), channel_id=1, source_target_pairs={{0,2},{1,3},{2,0},{3,1},{4,6},{5,7},{6,4},{7,5},{8,10},{9,11},{10,... | collective-permute-start | bytes 589832 | tf_op jit(solution)/shard_map/ppermute | solution.py:45
  104.6 7.9 %collective-permute-done.26 = bf16[48,1024]{1,0:T(8,128)(2,1)S(1)} collective-permute-done((bf16[48,1024]{1,0:T(8,128)(2,1)S(1)}, bf16[48,1024]{1,0:T(8,128)(2,1)S(1)}, u32[]{:S(2)}, u32[]{:S(2)}) %collective-permute-start.26) | collective-permute-done | bytes 98336 | tf_op jit(solution)/shard_map/ppermute | solution.py:45
  112.6 1.2 collective-permute-start.13
  113.8 1.0 collective-permute-done.11
  114.8 0.9 collective-permute-start.28
  115.7 7.2 %collective-permute-done.12 = bf16[96,1024]{1,0:T(8,128)(2,1)S(1)} collective-permute-done((bf16[96,1024]{1,0:T(8,128)(2,1)S(1)}, bf16[96,1024]{1,0:T(8,128)(2,1)S(1)}, u32[]{:S(2)}, u32[]{:S(2)}) %collective-permute-start.12) | collective-permute-done | bytes 196640 | tf_op jit(solution)/shard_map/ppermute | solution.py:45
  123.0 0.6 collective-permute-start.14
  123.9 7.0 %collective-permute-done.14 = bf16[192,1024]{1,0:T(8,128)(2,1)S(1)} collective-permute-done((bf16[192,1024]{1,0:T(8,128)(2,1)S(1)}, bf16[192,1024]{1,0:T(8,128)(2,1)S(1)}, u32[]{:S(2)}, u32[]{:S(2)}) %collective-permute-start.14) | collective-permute-done | bytes 393248 | tf_op jit(solution)/shard_map/ppermute | solution.py:45
  131.0 0.6 fusion.6
  131.7 0.5 convolution_convert_fusion
  132.8 0.5 convolution_convert_fusion.1
  133.7 0.6 fusion.7
  134.3 0.6 fusion.8
  134.9 1.7 %pad_maximum_fusion = bf16[1,512,3,768]{3,1,2,0:T(8,128)(2,1)} fusion(bf16[1,512,1,768]{3,1,2,0:T(8,128)(2,1)S(1)} %fusion.6, bf16[1,512,1,768]{3,1,2,0:T(8,128)(2,1)S(1)} %fusion.8, bf16[1,512,1,768]{3,1,2,0:T(8,128)(2,1)S(1)} %fusion.7), kind=kLoop, calls=%fused_computation.2 | loop fusion | flops 2359296 | bytes 4718592 | tf_op jit(solution)/shard_map/stack | solution.py:222
  (140 shorter events, 9.7 us)
Async XLA Ops:
  4.7 1.7 %copy-start = (bf16[1,512,3,768]{3,1,2,0:T(8,128)(2,1)S(1)}, bf16[1,512,3,768]{3,1,2,0:T(8,128)(2,1)}, u32[]{:S(2)}) copy-start(bf16[1,512,3,768]{3,1,2,0:T(8,128)(2,1)} %param.8) | copy-start | bytes 7077892
  4.7 5.3 %collective-permute-start = (bf16[96,2048]{1,0:T(8,128)(2,1)S(1)}, bf16[96,2048]{1,0:T(8,128)(2,1)S(1)}, u32[]{:S(2)}, u32[]{:S(2)}) collective-permute-start(bf16[96,2048]{1,0:T(8,128)(2,1)S(1)} %convolution_convert_fusion.4), channel_id=1, source_target_pairs={{0,1},{1,0},{2,3},{3,2},{4,5},{5,4},{6,7},{7,6},{8,9},{9,8},{10,11... | collective-permute-start | bytes 1179656 | tf_op jit(solution)/shard_map/ppermute | solution.py:45
  5.5 4.6 %collective-permute-start.16 = (bf16[96,2048]{1,0:T(8,128)(2,1)S(1)}, bf16[96,2048]{1,0:T(8,128)(2,1)S(1)}, u32[]{:S(2)}, u32[]{:S(2)}) collective-permute-start(bf16[96,2048]{1,0:T(8,128)(2,1)S(1)} %convolution_convert_fusion.2), channel_id=1, source_target_pairs={{0,1},{1,0},{2,3},{3,2},{4,5},{5,4},{6,7},{7,6},{8,9},{9,8},{10,11... | collective-permute-start | bytes 1179656 | tf_op jit(solution)/shard_map/ppermute | solution.py:45
  6.3 46.8 %collective-permute-start.4 = (bf16[512,3,768]{2,0,1:T(8,128)(2,1)S(1)}, bf16[512,3,768]{2,0,1:T(8,128)(2,1)S(1)}, u32[]{:S(2)}, u32[]{:S(2)}) collective-permute-start(bf16[512,3,768]{2,0,1:T(8,128)(2,1)S(1)} %bitcast.119), channel_id=1, source_target_pairs={{0,8},{1,17},{2,10},{3,19},{4,12},{5,21},{6,14},{7,23},{8,0},{9,25... | collective-permute-start | bytes 7077896 | tf_op jit(solution)/shard_map/ppermute | solution.py:45
  10.3 6.2 %collective-permute-start.1 = (bf16[48,1024]{1,0:T(8,128)(2,1)S(1)}, bf16[48,1024]{1,0:T(8,128)(2,1)S(1)}, u32[]{:S(2)}, u32[]{:S(2)}) collective-permute-start(bf16[48,1024]{1,0:T(8,128)(2,1)S(1)} %get-tuple-element.31), channel_id=1, source_target_pairs={{0,2},{1,3},{2,0},{3,1},{4,6},{5,7},{6,4},{7,5},{8,10},{9,11},{10,... | collective-permute-start | bytes 294920 | tf_op jit(solution)/shard_map/ppermute | solution.py:45
  12.0 10.2 %collective-permute-start.2 = (bf16[48,1024]{1,0:T(8,128)(2,1)S(1)}, bf16[48,1024]{1,0:T(8,128)(2,1)S(1)}, u32[]{:S(2)}, u32[]{:S(2)}) collective-permute-start(bf16[48,1024]{1,0:T(8,128)(2,1)S(1)} %get-tuple-element.32), channel_id=1, source_target_pairs={{0,4},{1,5},{2,6},{3,7},{4,0},{5,1},{6,2},{7,3},{8,12},{9,13},{10,... | collective-permute-start | bytes 294920 | tf_op jit(solution)/shard_map/ppermute | solution.py:45
  14.6 7.6 %collective-permute-start.3 = (bf16[48,1024]{1,0:T(8,128)(2,1)S(1)}, bf16[48,1024]{1,0:T(8,128)(2,1)S(1)}, u32[]{:S(2)}, u32[]{:S(2)}) collective-permute-start(bf16[48,1024]{1,0:T(8,128)(2,1)S(1)} %get-tuple-element.33), channel_id=1, source_target_pairs={{0,6},{1,7},{2,4},{3,5},{4,2},{5,3},{6,0},{7,1},{8,14},{9,15},{10,... | collective-permute-start | bytes 294920 | tf_op jit(solution)/shard_map/ppermute | solution.py:45
  14.8 12.1 %collective-permute-start.5 = (bf16[192,1024]{1,0:T(8,128)(2,1)S(1)}, bf16[192,1024]{1,0:T(8,128)(2,1)S(1)}, u32[]{:S(2)}, u32[]{:S(2)}) collective-permute-start(bf16[192,1024]{1,0:T(8,128)(2,1)S(1)} %bitcast.158), channel_id=1, source_target_pairs={{0,16},{1,9},{2,18},{3,11},{4,20},{5,13},{6,22},{7,15},{8,24},{9,1... | collective-permute-start | bytes 1179656 | tf_op jit(solution)/shard_map/ppermute | solution.py:45
  16.5 18.8 %collective-permute-start.17 = (bf16[192,1024]{1,0:T(8,128)(2,1)S(1)}, bf16[192,1024]{1,0:T(8,128)(2,1)S(1)}, u32[]{:S(2)}, u32[]{:S(2)}) collective-permute-start(bf16[192,1024]{1,0:T(8,128)(2,1)S(1)} %bitcast.156), channel_id=1, source_target_pairs={{0,16},{1,9},{2,18},{3,11},{4,20},{5,13},{6,22},{7,15},{8,24},{9,1... | collective-permute-start | bytes 1179656 | tf_op jit(solution)/shard_map/ppermute | solution.py:45
  26.9 9.3 %collective-permute-start.6 = (bf16[48,1024]{1,0:T(8,128)(2,1)S(1)}, bf16[48,1024]{1,0:T(8,128)(2,1)S(1)}, u32[]{:S(2)}, u32[]{:S(2)}) collective-permute-start(bf16[48,1024]{1,0:T(8,128)(2,1)S(1)} %get-tuple-element.34), channel_id=1, source_target_pairs={{0,2},{1,3},{2,0},{3,1},{4,6},{5,7},{6,4},{7,5},{8,10},{9,11},{10,... | collective-permute-start | bytes 294920 | tf_op jit(solution)/shard_map/ppermute | solution.py:45
  27.7 12.1 %collective-permute-start.7 = (bf16[48,1024]{1,0:T(8,128)(2,1)S(1)}, bf16[48,1024]{1,0:T(8,128)(2,1)S(1)}, u32[]{:S(2)}, u32[]{:S(2)}) collective-permute-start(bf16[48,1024]{1,0:T(8,128)(2,1)S(1)} %get-tuple-element.35), channel_id=1, source_target_pairs={{0,4},{1,5},{2,6},{3,7},{4,0},{5,1},{6,2},{7,3},{8,12},{9,13},{10,... | collective-permute-start | bytes 294920 | tf_op jit(solution)/shard_map/ppermute | solution.py:45
  31.2 8.9 %collective-permute-start.8 = (bf16[48,1024]{1,0:T(8,128)(2,1)S(1)}, bf16[48,1024]{1,0:T(8,128)(2,1)S(1)}, u32[]{:S(2)}, u32[]{:S(2)}) collective-permute-start(bf16[48,1024]{1,0:T(8,128)(2,1)S(1)} %get-tuple-element.36), channel_id=1, source_target_pairs={{0,6},{1,7},{2,4},{3,5},{4,2},{5,3},{6,0},{7,1},{8,14},{9,15},{10,... | collective-permute-start | bytes 294920 | tf_op jit(solution)/shard_map/ppermute | solution.py:45
  35.5 9.7 %collective-permute-start.18 = (bf16[96,1024]{1,0:T(8,128)(2,1)S(1)}, bf16[96,1024]{1,0:T(8,128)(2,1)S(1)}, u32[]{:S(2)}, u32[]{:S(2)}) collective-permute-start(bf16[96,1024]{1,0:T(8,128)(2,1)S(1)} %pad_maximum_fusion.40), channel_id=1, source_target_pairs={{0,2},{1,3},{2,0},{3,1},{4,6},{5,7},{6,4},{7,5},{8,10},{9,11},{10,... | collective-permute-start | bytes 589832 | tf_op jit(solution)/shard_map/ppermute | solution.py:45
  36.2 16.7 %collective-permute-start.19 = (bf16[96,1024]{1,0:T(8,128)(2,1)S(1)}, bf16[96,1024]{1,0:T(8,128)(2,1)S(1)}, u32[]{:S(2)}, u32[]{:S(2)}) collective-permute-start(bf16[96,1024]{1,0:T(8,128)(2,1)S(1)} %pad_maximum_fusion.38), channel_id=1, source_target_pairs={{0,4},{1,5},{2,6},{3,7},{4,0},{5,1},{6,2},{7,3},{8,12},{9,13},{10,... | collective-permute-start | bytes 589832 | tf_op jit(solution)/shard_map/ppermute | solution.py:45
  39.8 13.2 %collective-permute-start.20 = (bf16[96,1024]{1,0:T(8,128)(2,1)S(1)}, bf16[96,1024]{1,0:T(8,128)(2,1)S(1)}, u32[]{:S(2)}, u32[]{:S(2)}) collective-permute-start(bf16[96,1024]{1,0:T(8,128)(2,1)S(1)} %pad_maximum_fusion.39), channel_id=1, source_target_pairs={{0,6},{1,7},{2,4},{3,5},{4,2},{5,3},{6,0},{7,1},{8,14},{9,15},{10,... | collective-permute-start | bytes 589832 | tf_op jit(solution)/shard_map/ppermute | solution.py:45
  54.6 23.0 %collective-permute-start.21 = (bf16[384,768]{1,0:T(8,128)(2,1)S(1)}, bf16[384,768]{1,0:T(8,128)(2,1)S(1)}, u32[]{:S(2)}, u32[]{:S(2)}) collective-permute-start(bf16[384,768]{1,0:T(8,128)(2,1)S(1)} %pad_maximum_fusion.6), channel_id=1, source_target_pairs={{0,16},{1,9},{2,18},{3,11},{4,20},{5,13},{6,22},{7,15},{8,24},{9,1... | collective-permute-start | bytes 1769480 | tf_op jit(solution)/shard_map/ppermute | solution.py:45
  57.1 13.7 %collective-permute-start.9 = (bf16[192,1536]{1,0:T(8,128)(2,1)S(1)}, bf16[192,1536]{1,0:T(8,128)(2,1)S(1)}, u32[]{:S(2)}, u32[]{:S(2)}) collective-permute-start(bf16[192,1536]{1,0:T(8,128)(2,1)S(1)} %fusion.14), channel_id=1, source_target_pairs={{0,16},{1,9},{2,18},{3,11},{4,20},{5,13},{6,22},{7,15},{8,24},{9,1... | collective-permute-start | bytes 1769480 | tf_op jit(solution)/shard_map/ppermute | solution.py:45
  59.6 17.6 %collective-permute-start.10 = (bf16[192,1536]{1,0:T(8,128)(2,1)S(1)}, bf16[192,1536]{1,0:T(8,128)(2,1)S(1)}, u32[]{:S(2)}, u32[]{:S(2)}) collective-permute-start(bf16[192,1536]{1,0:T(8,128)(2,1)S(1)} %fusion.15), channel_id=1, source_target_pairs={{0,16},{1,9},{2,18},{3,11},{4,20},{5,13},{6,22},{7,15},{8,24},{9,1... | collective-permute-start | bytes 1769480 | tf_op jit(solution)/shard_map/ppermute | solution.py:45
  83.6 50.0 %collective-permute-start.30 = (bf16[2,512,768]{2,1,0:T(8,128)(2,1)S(1)}, bf16[2,512,768]{2,1,0:T(8,128)(2,1)S(1)}, u32[]{:S(2)}, u32[]{:S(2)}) collective-permute-start(bf16[2,512,768]{2,1,0:T(8,128)(2,1)S(1)} %pad_maximum_fusion.1), channel_id=1, source_target_pairs={{0,8},{1,17},{2,10},{3,19},{4,12},{5,21},{6,14},{7,23},{8,0},{9,25... | collective-permute-start | bytes 4718600 | tf_op jit(solution)/shard_map/ppermute | solution.py:45
  86.3 44.8 %collective-permute-start.31 = (bf16[512,768]{1,0:T(8,128)(2,1)S(1)}, bf16[512,768]{1,0:T(8,128)(2,1)S(1)}, u32[]{:S(2)}, u32[]{:S(2)}) collective-permute-start(bf16[512,768]{1,0:T(8,128)(2,1)S(1)} %convolution_convert_fusion.6), channel_id=1, source_target_pairs={{0,8},{1,17},{2,10},{3,19},{4,12},{5,21},{6,14},{7,23},{8,0},{9,25... | collective-permute-start | bytes 2359304 | tf_op jit(solution)/shard_map/ppermute | solution.py:45
  86.9 7.3 %collective-permute-start.22 = (bf16[48,1024]{1,0:T(8,128)(2,1)S(1)}, bf16[48,1024]{1,0:T(8,128)(2,1)S(1)}, u32[]{:S(2)}, u32[]{:S(2)}) collective-permute-start(bf16[48,1024]{1,0:T(8,128)(2,1)S(1)} %get-tuple-element.51), channel_id=1, source_target_pairs={{0,2},{1,3},{2,0},{3,1},{4,6},{5,7},{6,4},{7,5},{8,10},{9,11},{10,... | collective-permute-start | bytes 294920 | tf_op jit(solution)/shard_map/ppermute | solution.py:45
  89.9 10.9 %collective-permute-start.23 = (bf16[48,1024]{1,0:T(8,128)(2,1)S(1)}, bf16[48,1024]{1,0:T(8,128)(2,1)S(1)}, u32[]{:S(2)}, u32[]{:S(2)}) collective-permute-start(bf16[48,1024]{1,0:T(8,128)(2,1)S(1)} %get-tuple-element.52), channel_id=1, source_target_pairs={{0,4},{1,5},{2,6},{3,7},{4,0},{5,1},{6,2},{7,3},{8,12},{9,13},{10,... | collective-permute-start | bytes 294920 | tf_op jit(solution)/shard_map/ppermute | solution.py:45
  90.9 9.9 %collective-permute-start.24 = (bf16[48,1024]{1,0:T(8,128)(2,1)S(1)}, bf16[48,1024]{1,0:T(8,128)(2,1)S(1)}, u32[]{:S(2)}, u32[]{:S(2)}) collective-permute-start(bf16[48,1024]{1,0:T(8,128)(2,1)S(1)} %get-tuple-element.53), channel_id=1, source_target_pairs={{0,6},{1,7},{2,4},{3,5},{4,2},{5,3},{6,0},{7,1},{8,14},{9,15},{10,... | collective-permute-start | bytes 294920 | tf_op jit(solution)/shard_map/ppermute | solution.py:45
  94.1 8.7 %collective-permute-start.25 = (bf16[48,1024]{1,0:T(8,128)(2,1)S(1)}, bf16[48,1024]{1,0:T(8,128)(2,1)S(1)}, u32[]{:S(2)}, u32[]{:S(2)}) collective-permute-start(bf16[48,1024]{1,0:T(8,128)(2,1)S(1)} %get-tuple-element.56), channel_id=1, source_target_pairs={{0,2},{1,3},{2,0},{3,1},{4,6},{5,7},{6,4},{7,5},{8,10},{9,11},{10,... | collective-permute-start | bytes 294920 | tf_op jit(solution)/shard_map/ppermute | solution.py:45
  100.8 11.8 %collective-permute-start.26 = (bf16[48,1024]{1,0:T(8,128)(2,1)S(1)}, bf16[48,1024]{1,0:T(8,128)(2,1)S(1)}, u32[]{:S(2)}, u32[]{:S(2)}) collective-permute-start(bf16[48,1024]{1,0:T(8,128)(2,1)S(1)} %get-tuple-element.57), channel_id=1, source_target_pairs={{0,4},{1,5},{2,6},{3,7},{4,0},{5,1},{6,2},{7,3},{8,12},{9,13},{10,... | collective-permute-start | bytes 294920 | tf_op jit(solution)/shard_map/ppermute | solution.py:45
  100.8 11.8 %collective-permute-start.27 = (bf16[48,1024]{1,0:T(8,128)(2,1)S(1)}, bf16[48,1024]{1,0:T(8,128)(2,1)S(1)}, u32[]{:S(2)}, u32[]{:S(2)}) collective-permute-start(bf16[48,1024]{1,0:T(8,128)(2,1)S(1)} %get-tuple-element.58), channel_id=1, source_target_pairs={{0,6},{1,7},{2,4},{3,5},{4,2},{5,3},{6,0},{7,1},{8,14},{9,15},{10,... | collective-permute-start | bytes 294920 | tf_op jit(solution)/shard_map/ppermute | solution.py:45
  102.9 12.0 %collective-permute-start.11 = (bf16[96,1024]{1,0:T(8,128)(2,1)S(1)}, bf16[96,1024]{1,0:T(8,128)(2,1)S(1)}, u32[]{:S(2)}, u32[]{:S(2)}) collective-permute-start(bf16[96,1024]{1,0:T(8,128)(2,1)S(1)} %pad_maximum_fusion.35), channel_id=1, source_target_pairs={{0,2},{1,3},{2,0},{3,1},{4,6},{5,7},{6,4},{7,5},{8,10},{9,11},{10,... | collective-permute-start | bytes 589832 | tf_op jit(solution)/shard_map/ppermute | solution.py:45
  112.6 10.4 %collective-permute-start.12 = (bf16[96,1024]{1,0:T(8,128)(2,1)S(1)}, bf16[96,1024]{1,0:T(8,128)(2,1)S(1)}, u32[]{:S(2)}, u32[]{:S(2)}) collective-permute-start(bf16[96,1024]{1,0:T(8,128)(2,1)S(1)} %pad_maximum_fusion.33), channel_id=1, source_target_pairs={{0,4},{1,5},{2,6},{3,7},{4,0},{5,1},{6,2},{7,3},{8,12},{9,13},{10,... | collective-permute-start | bytes 589832 | tf_op jit(solution)/shard_map/ppermute | solution.py:45
  112.6 10.4 %collective-permute-start.13 = (bf16[96,1024]{1,0:T(8,128)(2,1)S(1)}, bf16[96,1024]{1,0:T(8,128)(2,1)S(1)}, u32[]{:S(2)}, u32[]{:S(2)}) collective-permute-start(bf16[96,1024]{1,0:T(8,128)(2,1)S(1)} %pad_maximum_fusion.34), channel_id=1, source_target_pairs={{0,6},{1,7},{2,4},{3,5},{4,2},{5,3},{6,0},{7,1},{8,14},{9,15},{10,... | collective-permute-start | bytes 589832 | tf_op jit(solution)/shard_map/ppermute | solution.py:45
  114.8 8.9 %collective-permute-start.28 = (bf16[192,1024]{1,0:T(8,128)(2,1)S(1)}, bf16[192,1024]{1,0:T(8,128)(2,1)S(1)}, u32[]{:S(2)}, u32[]{:S(2)}) collective-permute-start(bf16[192,1024]{1,0:T(8,128)(2,1)S(1)} %pad_maximum_fusion.25), channel_id=1, source_target_pairs={{0,16},{1,9},{2,18},{3,11},{4,20},{5,13},{6,22},{7,15},{8,24},{9,1... | collective-permute-start | bytes 1179656 | tf_op jit(solution)/shard_map/ppermute | solution.py:45
  123.0 7.8 %collective-permute-start.14 = (bf16[192,1024]{1,0:T(8,128)(2,1)S(1)}, bf16[192,1024]{1,0:T(8,128)(2,1)S(1)}, u32[]{:S(2)}, u32[]{:S(2)}) collective-permute-start(bf16[192,1024]{1,0:T(8,128)(2,1)S(1)} %pad_maximum_fusion.19), channel_id=1, source_target_pairs={{0,16},{1,9},{2,18},{3,11},{4,20},{5,13},{6,22},{7,15},{8,24},{9,1... | collective-permute-start | bytes 1179656 | tf_op jit(solution)/shard_map/ppermute | solution.py:45
  123.8 7.8 %collective-permute-start.29 = (bf16[96,2048]{1,0:T(8,128)(2,1)S(1)}, bf16[96,2048]{1,0:T(8,128)(2,1)S(1)}, u32[]{:S(2)}, u32[]{:S(2)}) collective-permute-start(bf16[96,2048]{1,0:T(8,128)(2,1)S(1)} %pad_maximum_fusion.26), channel_id=1, source_target_pairs={{0,1},{1,0},{2,3},{3,2},{4,5},{5,4},{6,7},{7,6},{8,9},{9,8},{10,11... | collective-permute-start | bytes 1179656 | tf_op jit(solution)/shard_map/ppermute | solution.py:45
  131.0 1.8 %collective-permute-start.15 = (bf16[96,2048]{1,0:T(8,128)(2,1)S(1)}, bf16[96,2048]{1,0:T(8,128)(2,1)S(1)}, u32[]{:S(2)}, u32[]{:S(2)}) collective-permute-start(bf16[96,2048]{1,0:T(8,128)(2,1)S(1)} %pad_maximum_fusion.20), channel_id=1, source_target_pairs={{0,1},{1,0},{2,3},{3,2},{4,5},{5,4},{6,7},{7,6},{8,9},{9,8},{10,11... | collective-permute-start | bytes 1179656 | tf_op jit(solution)/shard_map/ppermute | solution.py:45
  132.4 1.0 copy-start.2
  133.7 1.2 copy-start.1
where the time goes:
time: 137 us
  waiting for transfers between devices  72.3 us (53%)
  starting transfers between devices  38.3 us (28%)
  matrix products  14.9 us (11%)
  other arithmetic  5.72 us (4%)
  local copies, waits for them, and re-layouts  3.73 us (3%)
  between operations  1.7 us (1%)
    ppermute x32, waiting for transfers between devices, move(): return lax.ppermute(value, ALL, pairs)  72.3 us
    ppermute x32, starting transfers between devices, move(): return lax.ppermute(value, ALL, pairs)  38.3 us
    dot_general x36, matrix products, contract(): lax.dot_general(left, right, (((left_dim,), (right_dim,)), ((), ())), pre...  14.7 us
  transfers between devices with their start and end apart: 32, of which 14 were waited for; matrix products, arithmetic and copies ran while one was open for 7% of the time, Pallas kernels for 0%

commit v1 on v0

--- a/solution.py
+++ b/solution.py
@@ -79,8 +79,12 @@
     half = steps * CAP
 
     weights_own = expert_weights[0]
-    weights_far = moves.weight_pair(weights_own)
-    pair = (weights_own, weights_far)
+    gates_far = moves.weight_pair(weights_own[:, :2])
+    down_far = moves.weight_pair(weights_own[:, 2])
+    pair = (
+        (weights_own[:, 0], weights_own[:, 1], weights_own[:, 2]),
+        (gates_far[:, 0], gates_far[:, 1], down_far),
+    )
 
     slot = jnp.arange(2 * half, dtype=jnp.int32)
     slot_expert = ((slot % half // CAP) ^ own_z) * 2 + ((slot // half) ^ own_c)
@@ -91,24 +95,31 @@
         both = (first.reshape(steps, CAP, width), second.reshape(steps, CAP, width))
         return jnp.stack(both, axis=1).reshape(2 * half, width)
 
-    def cut(array, *which):
+    def taken(array, *which):
         return jnp.concatenate(
-            [array[:, i * quarter_width : (i + 1) * quarter_width] for i in which], axis=1
-        )
-
-    def send_local(table, source):
-        ordered = jnp.concatenate(
             [
-                lax.dynamic_slice_in_dim(source, index * quarter_width, quarter_width, 1)
-                for index in quarter
+                lax.dynamic_slice_in_dim(array, quarter[i] * quarter_width, quarter_width, 1)
+                for i in which
             ],
             axis=1,
         )
-        other = contract(table[:, half:], ordered, 0, 0).astype(BF16)
+
+    def placed(own, out):
+        whole = jnp.zeros((own.shape[0], model_width), BF16)
+        for index in range(4):
+            part = (own, out)[index // 2]
+            low = index % 2 * quarter_width
+            whole = lax.dynamic_update_slice_in_dim(
+                whole, part[:, low : low + quarter_width], quarter[index] * quarter_width, 1
+            )
+        return whole
+
+    def send_local(table, source):
+        other = contract(table[:, half:], source, 0, 0).astype(BF16)
         came = moves.core(other)
-        same = contract(table[:, :half], ordered, 0, 0).astype(BF16)
-        own = interleaved(cut(same, 0, 1), cut(came, 0, 2))
-        out = interleaved(cut(same, 2, 3), cut(came, 1, 3))
+        same = contract(table[:, :half], source, 0, 0).astype(BF16)
+        own = interleaved(taken(same, 0, 1), taken(came, 0, 1))
+        out = interleaved(taken(same, 2, 3), taken(came, 2, 3))
         return own, moves.column_pair(out)
 
     def by_z(rows):
@@ -135,30 +146,19 @@
         def source(array, index):
             return array.reshape(steps, 2, CAP, half_width)[:, index].reshape(half, half_width)
 
-        other = jnp.concatenate([source(own, 1), source(out, 1)], axis=1)
-        came = moves.core(other)
-        same = jnp.concatenate([source(own, 0), source(out, 0)], axis=1)
-        rows = jnp.concatenate([same, cut(came, 0, 2, 1, 3)])
-        result = contract(table, rows, 1, 0).astype(BF16)
-        answer = jnp.zeros((table.shape[0], model_width), BF16)
-        for index in range(4):
-            answer = lax.dynamic_update_slice_in_dim(
-                answer,
-                result[:, index * quarter_width : (index + 1) * quarter_width],
-                quarter[index] * quarter_width,
-                1,
-            )
-        return answer
+        came = moves.core(placed(source(own, 1), source(out, 1)))
+        rows = jnp.concatenate([placed(source(own, 0), source(out, 0)), came])
+        return contract(table, rows, 1, 0).astype(BF16)
 
     def inward(rows, which):
-        return contract(rows[:, :quarter_width], pair[0][:, which], 1, 0) + contract(
-            rows[:, quarter_width:], pair[1][:, which], 1, 0
+        return contract(rows[:, :quarter_width], pair[0][which], 1, 0) + contract(
+            rows[:, quarter_width:], pair[1][which], 1, 0
         )
 
     def outward(terms):
         return jnp.concatenate(
             [
-                sum(contract(value, pair[i][:, which], 1, 1) for value, which in terms)
+                sum(contract(value, pair[i][which], 1, 1) for value, which in terms)
                 for i in (0, 1)
             ],
             axis=1,
@@ -207,27 +207,26 @@
     gate_grad = jnp.concatenate([gg_own, gg_near])
     up_grad = jnp.concatenate([ug_own, ug_near])
     first, second = slice(0, quarter_width), slice(quarter_width, half_width)
-    down_far = contract(scaled[:, second], activation, 0, 0).astype(BF16)
-    down_far = moves.weight_pair(down_far)
+    term_far = contract(scaled[:, second], activation, 0, 0).astype(BF16)
+    arrived_down = moves.weight_pair(term_far)
     grad_near = outward([(gg_near, 0), (ug_near, 1)])
     (grad_near,) = by_z([grad_near])
-    in_far = jnp.stack(
+    terms_far = jnp.stack(
         [contract(rows[:, second], value, 0, 0) for value in (gate_grad, up_grad)]
     ).astype(BF16)
-    in_far = moves.weight_pair(in_far)
+    arrived_in = moves.weight_pair(terms_far)
     grad_own = outward([(gg_own, 0), (ug_own, 1)])
     (grad_own,) = by_z([grad_own])
     moe_out = give_back_in(combine, back_own, back_near)
     token_grad = give_back_in(dispatch, grad_own, grad_near)
-    weight_grad = jnp.stack(
-        [
-            contract(rows[:, first], gate_grad, 0, 0) + in_far[0].astype(F32),
-            contract(rows[:, first], up_grad, 0, 0) + in_far[1].astype(F32),
-            contract(scaled[:, first], activation, 0, 0) + down_far.astype(F32),
-        ],
-        axis=1,
-    ).astype(BF16)[None]
-    return moe_out, token_grad, weight_grad
+    term_down = contract(scaled[:, first], activation, 0, 0) + arrived_down.astype(F32)
+    term_down = term_down.astype(BF16)
+    terms = [
+        contract(rows[:, first], value, 0, 0) + arrived_in[i].astype(F32)
+        for i, value in enumerate((gate_grad, up_grad))
+    ]
+    weight_grad = jnp.stack([*(term.astype(BF16) for term in terms), term_down], axis=1)
+    return moe_out, token_grad, weight_grad[None]
 
 
 def gathered(tokens, expert_ids, gate_units, expert_weights, out_grad):

time: 137 us -> 178 us (1.30)
  matrix products: 14.9 us -> 32.9 us
  waiting for transfers between devices: 72.3 us -> 84 us
  starting transfers between devices: 38.3 us -> 46.9 us
  local copies, waits for them, and re-layouts: 3.73 us -> 7.64 us
    dot_general x36, matrix products: 14.7 us -> 32.6 us  [contract(): lax.dot_general(left, right, (((left_dim,), (right_dim,)), ((), ())), pre...]
    ppermute x32 -> x33, waiting for transfers between devices: 72.3 us -> 84 us  [move(): return lax.ppermute(value, ALL, pairs)]
    ppermute x32 -> x33, starting transfers between devices: 38.3 us -> 46.9 us  [move(): return lax.ppermute(value, ALL, pairs)]
    slice x4 -> x1, local copies, waits for them, and re-layouts: 0.11 us -> 2.74 us  [paired_body(): gates_far = moves.weight_pair(weights_own[:, :2])]
  transfers between devices with their start and end apart: 32 -> 33, of which waited for: 14 -> 15; matrix products, arithmetic and copies ran while one was open for 7% -> 19% of each run, Pallas kernels for 0% -> 0%
where the time goes in v1:
time: 178 us; the launch traced here: 177 us
  waiting for transfers between devices  84 us (47%)
  starting transfers between devices  46.9 us (26%)
  matrix products  32.9 us (18%)
  local copies, waits for them, and re-layouts  7.64 us (4%)
  other arithmetic  4.29 us (2%)
    ppermute x33, waiting for transfers between devices, move(): return lax.ppermute(value, ALL, pairs)  84 us
    ppermute x33, starting transfers between devices, move(): return lax.ppermute(value, ALL, pairs)  46.9 us
    dot_general x36, matrix products, contract(): lax.dot_general(left, right, (((left_dim,), (right_dim,)), ((), ())), pre...  32.6 us
  transfers between devices with their start and end apart: 33, of which 15 were waited for; matrix products, arithmetic and copies ran while one was open for 19% of the time, Pallas kernels for 0%

profile of v1, /device:TPU:0, one launch (start us, length us, event | category | flops | bytes accessed | tf_op | source)
XLA Modules:
  0.0 177.5 jit_solution(5906994898307735142)
XLA Ops:
  0.7 2.7 %slice.417 = bf16[512,2,768]{2,0,1:T(8,128)(2,1)} slice(bf16[512,3,768]{2,0,1:T(8,128)(2,1)} %bitcast.123), slice={[0:512], [0:2], [0:768]} | slice | bytes 3145728 | tf_op jit(solution)/shard_map/slice | solution.py:82
  3.4 3.0 %collective-permute-start.4 = (bf16[512,2,768]{2,0,1:T(8,128)(2,1)}, bf16[512,2,768]{2,0,1:T(8,128)(2,1)}, u32[]{:S(2)}, u32[]{:S(2)}) collective-permute-start(bf16[512,2,768]{2,0,1:T(8,128)(2,1)} %slice.417), channel_id=1, source_target_pairs={{0,8},{1,17},{2,10},{3,19},{4,12},{5,21},{6,14},{7,23},{8,0},{9,25... | collective-permute-start | bytes 4718600 | tf_op jit(solution)/shard_map/ppermute | solution.py:45
  7.0 1.1 convolution_convert_fusion.4
  8.1 0.9 slice_bitcast_fusion.2
  9.0 1.1 collective-permute-start.10
  10.1 1.1 convolution_convert_fusion.2
  11.1 0.7 collective-permute-start.17
  11.8 1.1 convolution_convert_fusion.5
  13.4 0.7 copy-done.5
  14.2 1.1 constant_dynamic-slice_fusion.9
  15.4 1.1 constant_dynamic-slice_fusion.1
  16.6 3.7 %collective-permute-start.3 = (bf16[48,1024]{1,0:T(8,128)(2,1)S(1)}, bf16[48,1024]{1,0:T(8,128)(2,1)S(1)}, u32[]{:S(2)}, u32[]{:S(2)}) collective-permute-start(bf16[48,1024]{1,0:T(8,128)(2,1)S(1)} %get-tuple-element.33), channel_id=1, source_target_pairs={{0,6},{1,7},{2,4},{3,5},{4,2},{5,3},{6,0},{7,1},{8,14},{9,15},{10,... | collective-permute-start | bytes 294920 | tf_op jit(solution)/shard_map/ppermute | solution.py:45
  20.3 0.8 collective-permute-start.1
  21.2 5.5 %collective-permute-done.1 = bf16[48,1024]{1,0:T(8,128)(2,1)S(1)} collective-permute-done((bf16[48,1024]{1,0:T(8,128)(2,1)S(1)}, bf16[48,1024]{1,0:T(8,128)(2,1)S(1)}, u32[]{:S(2)}, u32[]{:S(2)}) %collective-permute-start.1) | collective-permute-done | bytes 98336 | tf_op jit(solution)/shard_map/ppermute | solution.py:45
  26.8 0.8 collective-permute-start.5
  27.6 1.1 collective-permute-done.2
  28.7 0.8 collective-permute-start.18
  29.6 7.2 %collective-permute-done.5 = bf16[192,1024]{1,0:T(8,128)(2,1)S(1)} collective-permute-done((bf16[192,1024]{1,0:T(8,128)(2,1)S(1)}, bf16[192,1024]{1,0:T(8,128)(2,1)S(1)}, u32[]{:S(2)}, u32[]{:S(2)}) %collective-permute-start.5) | collective-permute-done | bytes 393248 | tf_op jit(solution)/shard_map/ppermute | solution.py:45
  36.8 3.9 %collective-permute-start.8 = (bf16[48,1024]{1,0:T(8,128)(2,1)S(1)}, bf16[48,1024]{1,0:T(8,128)(2,1)S(1)}, u32[]{:S(2)}, u32[]{:S(2)}) collective-permute-start(bf16[48,1024]{1,0:T(8,128)(2,1)S(1)} %get-tuple-element.36), channel_id=1, source_target_pairs={{0,6},{1,7},{2,4},{3,5},{4,2},{5,3},{6,0},{7,1},{8,14},{9,15},{10,... | collective-permute-start | bytes 294920 | tf_op jit(solution)/shard_map/ppermute | solution.py:45
  41.0 1.8 %collective-permute-start.6 = (bf16[48,1024]{1,0:T(8,128)(2,1)S(1)}, bf16[48,1024]{1,0:T(8,128)(2,1)S(1)}, u32[]{:S(2)}, u32[]{:S(2)}) collective-permute-start(bf16[48,1024]{1,0:T(8,128)(2,1)S(1)} %get-tuple-element.34), channel_id=1, source_target_pairs={{0,2},{1,3},{2,0},{3,1},{4,6},{5,7},{6,4},{7,5},{8,10},{9,11},{10,... | collective-permute-start | bytes 294920 | tf_op jit(solution)/shard_map/ppermute | solution.py:45
  42.9 4.2 %collective-permute-done.6 = bf16[48,1024]{1,0:T(8,128)(2,1)S(1)} collective-permute-done((bf16[48,1024]{1,0:T(8,128)(2,1)S(1)}, bf16[48,1024]{1,0:T(8,128)(2,1)S(1)}, u32[]{:S(2)}, u32[]{:S(2)}) %collective-permute-start.6) | collective-permute-done | bytes 98336 | tf_op jit(solution)/shard_map/ppermute | solution.py:45
  47.1 2.5 %collective-permute-start.19 = (bf16[96,1024]{1,0:T(8,128)(2,1)S(1)}, bf16[96,1024]{1,0:T(8,128)(2,1)S(1)}, u32[]{:S(2)}, u32[]{:S(2)}) collective-permute-start(bf16[96,1024]{1,0:T(8,128)(2,1)S(1)} %pad_maximum_fusion.39), channel_id=1, source_target_pairs={{0,2},{1,3},{2,0},{3,1},{4,6},{5,7},{6,4},{7,5},{8,10},{9,11},{10,... | collective-permute-start | bytes 589832 | tf_op jit(solution)/shard_map/ppermute | solution.py:45
  50.1 2.7 %collective-permute-start.20 = (bf16[96,1024]{1,0:T(8,128)(2,1)S(1)}, bf16[96,1024]{1,0:T(8,128)(2,1)S(1)}, u32[]{:S(2)}, u32[]{:S(2)}) collective-permute-start(bf16[96,1024]{1,0:T(8,128)(2,1)S(1)} %pad_maximum_fusion.37), channel_id=1, source_target_pairs={{0,4},{1,5},{2,6},{3,7},{4,0},{5,1},{6,2},{7,3},{8,12},{9,13},{10,... | collective-permute-start | bytes 589832 | tf_op jit(solution)/shard_map/ppermute | solution.py:45
  53.0 4.7 %collective-permute-done.19 = bf16[96,1024]{1,0:T(8,128)(2,1)S(1)} collective-permute-done((bf16[96,1024]{1,0:T(8,128)(2,1)S(1)}, bf16[96,1024]{1,0:T(8,128)(2,1)S(1)}, u32[]{:S(2)}, u32[]{:S(2)}) %collective-permute-start.19) | collective-permute-done | bytes 196640 | tf_op jit(solution)/shard_map/ppermute | solution.py:45
  57.7 9.5 %collective-permute-done.20 = bf16[96,1024]{1,0:T(8,128)(2,1)S(1)} collective-permute-done((bf16[96,1024]{1,0:T(8,128)(2,1)S(1)}, bf16[96,1024]{1,0:T(8,128)(2,1)S(1)}, u32[]{:S(2)}, u32[]{:S(2)}) %collective-permute-start.20) | collective-permute-done | bytes 196640 | tf_op jit(solution)/shard_map/ppermute | solution.py:45
  67.4 1.5 fusion.38
  68.9 1.5 fusion.41
  71.1 1.3 collective-permute-start.22
  72.4 1.5 fusion.31
  74.2 1.5 fusion.27
  76.1 0.8 collective-permute-start.11
  76.9 1.5 fusion.30
  78.7 1.5 fusion.26
  80.6 1.3 collective-permute-start.9
  81.9 5.5 %collective-permute-done.11 = bf16[192,1536]{1,0:T(8,128)(2,1)S(1)} collective-permute-done((bf16[192,1536]{1,0:T(8,128)(2,1)S(1)}, bf16[192,1536]{1,0:T(8,128)(2,1)S(1)}, u32[]{:S(2)}, u32[]{:S(2)}) %collective-permute-start.11) | collective-permute-done | bytes 589856 | tf_op jit(solution)/shard_map/ppermute | solution.py:45
  88.2 5.5 %collective-permute-done.9 = bf16[192,1536]{1,0:T(8,128)(2,1)S(1)} collective-permute-done((bf16[192,1536]{1,0:T(8,128)(2,1)S(1)}, bf16[192,1536]{1,0:T(8,128)(2,1)S(1)}, u32[]{:S(2)}, u32[]{:S(2)}) %collective-permute-start.9) | collective-permute-done | bytes 589856 | tf_op jit(solution)/shard_map/ppermute | solution.py:45
  94.5 1.5 convolution_convert_fusion.11
  96.1 1.5 convolution_convert_fusion.9
  98.9 1.5 fusion.29
  100.5 1.5 fusion.10
  102.2 2.3 %collective-permute-start.14 = (bf16[96,1024]{1,0:T(8,128)(2,1)S(1)}, bf16[96,1024]{1,0:T(8,128)(2,1)S(1)}, u32[]{:S(2)}, u32[]{:S(2)}) collective-permute-start(bf16[96,1024]{1,0:T(8,128)(2,1)S(1)} %pad_maximum_fusion.31), channel_id=1, source_target_pairs={{0,6},{1,7},{2,4},{3,5},{4,2},{5,3},{6,0},{7,1},{8,14},{9,15},{10,... | collective-permute-start | bytes 589832 | tf_op jit(solution)/shard_map/ppermute | solution.py:45
  104.5 3.1 %collective-permute-start.13 = (bf16[96,1024]{1,0:T(8,128)(2,1)S(1)}, bf16[96,1024]{1,0:T(8,128)(2,1)S(1)}, u32[]{:S(2)}, u32[]{:S(2)}) collective-permute-start(bf16[96,1024]{1,0:T(8,128)(2,1)S(1)} %pad_maximum_fusion.30), channel_id=1, source_target_pairs={{0,4},{1,5},{2,6},{3,7},{4,0},{5,1},{6,2},{7,3},{8,12},{9,13},{10,... | collective-permute-start | bytes 589832 | tf_op jit(solution)/shard_map/ppermute | solution.py:45
  107.7 2.3 %collective-permute-start.25 = (bf16[48,1024]{1,0:T(8,128)(2,1)S(1)}, bf16[48,1024]{1,0:T(8,128)(2,1)S(1)}, u32[]{:S(2)}, u32[]{:S(2)}) collective-permute-start(bf16[48,1024]{1,0:T(8,128)(2,1)S(1)} %get-tuple-element.53), channel_id=1, source_target_pairs={{0,6},{1,7},{2,4},{3,5},{4,2},{5,3},{6,0},{7,1},{8,14},{9,15},{10,... | collective-permute-start | bytes 294920 | tf_op jit(solution)/shard_map/ppermute | solution.py:45
  109.9 2.2 %collective-permute-start.23 = (bf16[48,1024]{1,0:T(8,128)(2,1)S(1)}, bf16[48,1024]{1,0:T(8,128)(2,1)S(1)}, u32[]{:S(2)}, u32[]{:S(2)}) collective-permute-start(bf16[48,1024]{1,0:T(8,128)(2,1)S(1)} %get-tuple-element.51), channel_id=1, source_target_pairs={{0,2},{1,3},{2,0},{3,1},{4,6},{5,7},{6,4},{7,5},{8,10},{9,11},{10,... | collective-permute-start | bytes 294920 | tf_op jit(solution)/shard_map/ppermute | solution.py:45
  114.2 1.7 fusion.28
  115.9 1.5 fusion.12
  117.5 0.6 convolution_convert_fusion.6
  118.3 2.3 %collective-permute-start.28 = (bf16[48,1024]{1,0:T(8,128)(2,1)S(1)}, bf16[48,1024]{1,0:T(8,128)(2,1)S(1)}, u32[]{:S(2)}, u32[]{:S(2)}) collective-permute-start(bf16[48,1024]{1,0:T(8,128)(2,1)S(1)} %get-tuple-element.58), channel_id=1, source_target_pairs={{0,6},{1,7},{2,4},{3,5},{4,2},{5,3},{6,0},{7,1},{8,14},{9,15},{10,... | collective-permute-start | bytes 294920 | tf_op jit(solution)/shard_map/ppermute | solution.py:45
  120.6 12.1 %collective-permute-done.24 = bf16[48,1024]{1,0:T(8,128)(2,1)S(1)} collective-permute-done((bf16[48,1024]{1,0:T(8,128)(2,1)S(1)}, bf16[48,1024]{1,0:T(8,128)(2,1)S(1)}, u32[]{:S(2)}, u32[]{:S(2)}) %collective-permute-start.24) | collective-permute-done | bytes 98336 | tf_op jit(solution)/shard_map/ppermute | solution.py:45
  132.9 2.6 %collective-permute-start.26 = (bf16[48,1024]{1,0:T(8,128)(2,1)S(1)}, bf16[48,1024]{1,0:T(8,128)(2,1)S(1)}, u32[]{:S(2)}, u32[]{:S(2)}) collective-permute-start(bf16[48,1024]{1,0:T(8,128)(2,1)S(1)} %get-tuple-element.56), channel_id=1, source_target_pairs={{0,2},{1,3},{2,0},{3,1},{4,6},{5,7},{6,4},{7,5},{8,10},{9,11},{10,... | collective-permute-start | bytes 294920 | tf_op jit(solution)/shard_map/ppermute | solution.py:45
  135.7 1.8 %collective-permute-start.12 = (bf16[96,1024]{1,0:T(8,128)(2,1)S(1)}, bf16[96,1024]{1,0:T(8,128)(2,1)S(1)}, u32[]{:S(2)}, u32[]{:S(2)}) collective-permute-start(bf16[96,1024]{1,0:T(8,128)(2,1)S(1)} %pad_maximum_fusion.32), channel_id=1, source_target_pairs={{0,2},{1,3},{2,0},{3,1},{4,6},{5,7},{6,4},{7,5},{8,10},{9,11},{10,... | collective-permute-start | bytes 589832 | tf_op jit(solution)/shard_map/ppermute | solution.py:45
  137.5 1.6 collective-permute-done.27
  139.1 1.3 collective-permute-start.32
  140.4 1.1 collective-permute-start.31
  141.6 1.8 %collective-permute-start.29 = (bf16[192,1024]{1,0:T(8,128)(2,1)S(1)}, bf16[192,1024]{1,0:T(8,128)(2,1)S(1)}, u32[]{:S(2)}, u32[]{:S(2)}) collective-permute-start(bf16[192,1024]{1,0:T(8,128)(2,1)S(1)} %pad_maximum_fusion.21), channel_id=1, source_target_pairs={{0,16},{1,9},{2,18},{3,11},{4,20},{5,13},{6,22},{7,15},{8,24},{9,1... | collective-permute-start | bytes 1179656 | tf_op jit(solution)/shard_map/ppermute | solution.py:45
  143.7 0.6 collective-permute-start.15
  144.4 9.3 %collective-permute-done.29 = bf16[192,1024]{1,0:T(8,128)(2,1)S(1)} collective-permute-done((bf16[192,1024]{1,0:T(8,128)(2,1)S(1)}, bf16[192,1024]{1,0:T(8,128)(2,1)S(1)}, u32[]{:S(2)}, u32[]{:S(2)}) %collective-permute-start.29) | collective-permute-done | bytes 393248 | tf_op jit(solution)/shard_map/ppermute | solution.py:45
  153.8 8.2 %collective-permute-done.15 = bf16[192,1024]{1,0:T(8,128)(2,1)S(1)} collective-permute-done((bf16[192,1024]{1,0:T(8,128)(2,1)S(1)}, bf16[192,1024]{1,0:T(8,128)(2,1)S(1)}, u32[]{:S(2)}, u32[]{:S(2)}) %collective-permute-start.15) | collective-permute-done | bytes 393248 | tf_op jit(solution)/shard_map/ppermute | solution.py:45
  162.3 0.6 fusion.6
  162.9 1.5 convolution_convert_fusion
  164.4 1.4 convolution_convert_fusion.1
  165.8 8.8 %collective-permute-done.31 = bf16[2,512,768]{2,1,0:T(8,128)(2,1)S(1)} collective-permute-done((bf16[2,512,768]{2,1,0:T(8,128)(2,1)S(1)}, bf16[2,512,768]{2,1,0:T(8,128)(2,1)S(1)}, u32[]{:S(2)}, u32[]{:S(2)}) %collective-permute-start.31) | collective-permute-done | bytes 1572896 | tf_op jit(solution)/shard_map/ppermute | solution.py:45
  175.2 0.6 fusion.7
  175.8 1.7 maximum_bitcast_fusion
  (163 shorter events, 11.7 us)
Async XLA Ops:
  0.6 6.4 %copy-start = (bf16[256,2048]{1,0:T(8,128)(2,1)S(1)}, bf16[256,2048]{1,0:T(8,128)(2,1)}, u32[]{:S(2)}) copy-start(bf16[256,2048]{1,0:T(8,128)(2,1)} %param.5) | copy-start | bytes 3145732
  0.6 5.7 %copy-start.7 = (s32[256,8]{0,1:T(8,128)S(1)}, s32[256,8]{0,1:T(8,128)}, u32[]{:S(2)}) copy-start(s32[256,8]{0,1:T(8,128)} %param.7) | copy-start | bytes 24580
  0.7 5.7 %copy-start.6 = (s32[256,8]{0,1:T(8,128)S(1)}, s32[256,8]{0,1:T(8,128)}, u32[]{:S(2)}) copy-start(s32[256,8]{0,1:T(8,128)} %param.6) | copy-start | bytes 24580
  3.4 4.7 %copy-start.2 = (bf16[1,512,3,768]{3,1,2,0:T(8,128)(2,1)S(1)}, bf16[1,512,3,768]{3,1,2,0:T(8,128)(2,1)}, u32[]{:S(2)}) copy-start(bf16[1,512,3,768]{3,1,2,0:T(8,128)(2,1)} %param.8) | copy-start | bytes 7077892
  3.4 69.0 %collective-permute-start.4 = (bf16[512,2,768]{2,0,1:T(8,128)(2,1)}, bf16[512,2,768]{2,0,1:T(8,128)(2,1)}, u32[]{:S(2)}, u32[]{:S(2)}) collective-permute-start(bf16[512,2,768]{2,0,1:T(8,128)(2,1)} %slice.417), channel_id=1, source_target_pairs={{0,8},{1,17},{2,10},{3,19},{4,12},{5,21},{6,14},{7,23},{8,0},{9,25... | collective-permute-start | bytes 4718600 | tf_op jit(solution)/shard_map/ppermute | solution.py:45
  7.0 3.1 %copy-start.3 = (bf16[256,2048]{1,0:T(8,128)(2,1)S(1)}, bf16[256,2048]{1,0:T(8,128)(2,1)}, u32[]{:S(2)}) copy-start(bf16[256,2048]{1,0:T(8,128)(2,1)} %param.9) | copy-start | bytes 3145732
  8.1 6.1 %collective-permute-start = (bf16[96,2048]{1,0:T(8,128)(2,1)}, bf16[96,2048]{1,0:T(8,128)(2,1)}, u32[]{:S(2)}, u32[]{:S(2)}) collective-permute-start(bf16[96,2048]{1,0:T(8,128)(2,1)} %convolution_convert_fusion.4), channel_id=1, source_target_pairs={{0,1},{1,0},{2,3},{3,2},{4,5},{5,4},{6,7},{7,6},{8,9},{9,8},{10,11... | collective-permute-start | bytes 1179656 | tf_op jit(solution)/shard_map/ppermute | solution.py:45
  9.0 58.4 %collective-permute-start.10 = (bf16[512,768]{1,0:T(8,128)(2,1)}, bf16[512,768]{1,0:T(8,128)(2,1)}, u32[]{:S(2)}, u32[]{:S(2)}) collective-permute-start(bf16[512,768]{1,0:T(8,128)(2,1)} %slice_bitcast_fusion.2), channel_id=1, source_target_pairs={{0,8},{1,17},{2,10},{3,19},{4,12},{5,21},{6,14},{7,23},{8,0},{9,25... | collective-permute-start | bytes 2359304 | tf_op jit(solution)/shard_map/ppermute | solution.py:45
  11.1 4.3 %collective-permute-start.17 = (bf16[96,2048]{1,0:T(8,128)(2,1)}, bf16[96,2048]{1,0:T(8,128)(2,1)}, u32[]{:S(2)}, u32[]{:S(2)}) collective-permute-start(bf16[96,2048]{1,0:T(8,128)(2,1)} %convolution_convert_fusion.2), channel_id=1, source_target_pairs={{0,1},{1,0},{2,3},{3,2},{4,5},{5,4},{6,7},{7,6},{8,9},{9,8},{10,11... | collective-permute-start | bytes 1179656 | tf_op jit(solution)/shard_map/ppermute | solution.py:45
  11.8 1.2 copy-start.4
  13.0 1.0 copy-start.5
  16.6 12.9 %collective-permute-start.3 = (bf16[48,1024]{1,0:T(8,128)(2,1)S(1)}, bf16[48,1024]{1,0:T(8,128)(2,1)S(1)}, u32[]{:S(2)}, u32[]{:S(2)}) collective-permute-start(bf16[48,1024]{1,0:T(8,128)(2,1)S(1)} %get-tuple-element.33), channel_id=1, source_target_pairs={{0,6},{1,7},{2,4},{3,5},{4,2},{5,3},{6,0},{7,1},{8,14},{9,15},{10,... | collective-permute-start | bytes 294920 | tf_op jit(solution)/shard_map/ppermute | solution.py:45
  20.3 8.4 %collective-permute-start.2 = (bf16[48,1024]{1,0:T(8,128)(2,1)S(1)}, bf16[48,1024]{1,0:T(8,128)(2,1)S(1)}, u32[]{:S(2)}, u32[]{:S(2)}) collective-permute-start(bf16[48,1024]{1,0:T(8,128)(2,1)S(1)} %get-tuple-element.32), channel_id=1, source_target_pairs={{0,4},{1,5},{2,6},{3,7},{4,0},{5,1},{6,2},{7,3},{8,12},{9,13},{10,... | collective-permute-start | bytes 294920 | tf_op jit(solution)/shard_map/ppermute | solution.py:45
  20.3 6.5 %collective-permute-start.1 = (bf16[48,1024]{1,0:T(8,128)(2,1)S(1)}, bf16[48,1024]{1,0:T(8,128)(2,1)S(1)}, u32[]{:S(2)}, u32[]{:S(2)}) collective-permute-start(bf16[48,1024]{1,0:T(8,128)(2,1)S(1)} %get-tuple-element.31), channel_id=1, source_target_pairs={{0,2},{1,3},{2,0},{3,1},{4,6},{5,7},{6,4},{7,5},{8,10},{9,11},{10,... | collective-permute-start | bytes 294920 | tf_op jit(solution)/shard_map/ppermute | solution.py:45
  26.8 10.0 %collective-permute-start.5 = (bf16[192,1024]{1,0:T(8,128)(2,1)S(1)}, bf16[192,1024]{1,0:T(8,128)(2,1)S(1)}, u32[]{:S(2)}, u32[]{:S(2)}) collective-permute-start(bf16[192,1024]{1,0:T(8,128)(2,1)S(1)} %bitcast.175), channel_id=1, source_target_pairs={{0,16},{1,9},{2,18},{3,11},{4,20},{5,13},{6,22},{7,15},{8,24},{9,1... | collective-permute-start | bytes 1179656 | tf_op jit(solution)/shard_map/ppermute | solution.py:45
  28.7 12.3 %collective-permute-start.18 = (bf16[192,1024]{1,0:T(8,128)(2,1)S(1)}, bf16[192,1024]{1,0:T(8,128)(2,1)S(1)}, u32[]{:S(2)}, u32[]{:S(2)}) collective-permute-start(bf16[192,1024]{1,0:T(8,128)(2,1)S(1)} %bitcast.174), channel_id=1, source_target_pairs={{0,16},{1,9},{2,18},{3,11},{4,20},{5,13},{6,22},{7,15},{8,24},{9,1... | collective-permute-start | bytes 1179656 | tf_op jit(solution)/shard_map/ppermute | solution.py:45
  36.8 16.0 %collective-permute-start.8 = (bf16[48,1024]{1,0:T(8,128)(2,1)S(1)}, bf16[48,1024]{1,0:T(8,128)(2,1)S(1)}, u32[]{:S(2)}, u32[]{:S(2)}) collective-permute-start(bf16[48,1024]{1,0:T(8,128)(2,1)S(1)} %get-tuple-element.36), channel_id=1, source_target_pairs={{0,6},{1,7},{2,4},{3,5},{4,2},{5,3},{6,0},{7,1},{8,14},{9,15},{10,... | collective-permute-start | bytes 294920 | tf_op jit(solution)/shard_map/ppermute | solution.py:45
  40.7 9.4 %collective-permute-start.7 = (bf16[48,1024]{1,0:T(8,128)(2,1)S(1)}, bf16[48,1024]{1,0:T(8,128)(2,1)S(1)}, u32[]{:S(2)}, u32[]{:S(2)}) collective-permute-start(bf16[48,1024]{1,0:T(8,128)(2,1)S(1)} %get-tuple-element.35), channel_id=1, source_target_pairs={{0,4},{1,5},{2,6},{3,7},{4,0},{5,1},{6,2},{7,3},{8,12},{9,13},{10,... | collective-permute-start | bytes 294920 | tf_op jit(solution)/shard_map/ppermute | solution.py:45
  41.0 6.1 %collective-permute-start.6 = (bf16[48,1024]{1,0:T(8,128)(2,1)S(1)}, bf16[48,1024]{1,0:T(8,128)(2,1)S(1)}, u32[]{:S(2)}, u32[]{:S(2)}) collective-permute-start(bf16[48,1024]{1,0:T(8,128)(2,1)S(1)} %get-tuple-element.34), channel_id=1, source_target_pairs={{0,2},{1,3},{2,0},{3,1},{4,6},{5,7},{6,4},{7,5},{8,10},{9,11},{10,... | collective-permute-start | bytes 294920 | tf_op jit(solution)/shard_map/ppermute | solution.py:45
  47.1 10.6 %collective-permute-start.19 = (bf16[96,1024]{1,0:T(8,128)(2,1)S(1)}, bf16[96,1024]{1,0:T(8,128)(2,1)S(1)}, u32[]{:S(2)}, u32[]{:S(2)}) collective-permute-start(bf16[96,1024]{1,0:T(8,128)(2,1)S(1)} %pad_maximum_fusion.39), channel_id=1, source_target_pairs={{0,2},{1,3},{2,0},{3,1},{4,6},{5,7},{6,4},{7,5},{8,10},{9,11},{10,... | collective-permute-start | bytes 589832 | tf_op jit(solution)/shard_map/ppermute | solution.py:45
  50.1 17.1 %collective-permute-start.20 = (bf16[96,1024]{1,0:T(8,128)(2,1)S(1)}, bf16[96,1024]{1,0:T(8,128)(2,1)S(1)}, u32[]{:S(2)}, u32[]{:S(2)}) collective-permute-start(bf16[96,1024]{1,0:T(8,128)(2,1)S(1)} %pad_maximum_fusion.37), channel_id=1, source_target_pairs={{0,4},{1,5},{2,6},{3,7},{4,0},{5,1},{6,2},{7,3},{8,12},{9,13},{10,... | collective-permute-start | bytes 589832 | tf_op jit(solution)/shard_map/ppermute | solution.py:45
  52.8 14.4 %collective-permute-start.21 = (bf16[96,1024]{1,0:T(8,128)(2,1)S(1)}, bf16[96,1024]{1,0:T(8,128)(2,1)S(1)}, u32[]{:S(2)}, u32[]{:S(2)}) collective-permute-start(bf16[96,1024]{1,0:T(8,128)(2,1)S(1)} %pad_maximum_fusion.38), channel_id=1, source_target_pairs={{0,6},{1,7},{2,4},{3,5},{4,2},{5,3},{6,0},{7,1},{8,14},{9,15},{10,... | collective-permute-start | bytes 589832 | tf_op jit(solution)/shard_map/ppermute | solution.py:45
  71.1 26.7 %collective-permute-start.22 = (bf16[384,768]{1,0:T(8,128)(2,1)S(1)}, bf16[384,768]{1,0:T(8,128)(2,1)S(1)}, u32[]{:S(2)}, u32[]{:S(2)}) collective-permute-start(bf16[384,768]{1,0:T(8,128)(2,1)S(1)} %pad_maximum_fusion.3), channel_id=1, source_target_pairs={{0,16},{1,9},{2,18},{3,11},{4,20},{5,13},{6,22},{7,15},{8,24},{9,1... | collective-permute-start | bytes 1769480 | tf_op jit(solution)/shard_map/ppermute | solution.py:45
  76.1 11.3 %collective-permute-start.11 = (bf16[192,1536]{1,0:T(8,128)(2,1)S(1)}, bf16[192,1536]{1,0:T(8,128)(2,1)S(1)}, u32[]{:S(2)}, u32[]{:S(2)}) collective-permute-start(bf16[192,1536]{1,0:T(8,128)(2,1)S(1)} %fusion.15), channel_id=1, source_target_pairs={{0,16},{1,9},{2,18},{3,11},{4,20},{5,13},{6,22},{7,15},{8,24},{9,1... | collective-permute-start | bytes 1769480 | tf_op jit(solution)/shard_map/ppermute | solution.py:45
  80.6 13.1 %collective-permute-start.9 = (bf16[192,1536]{1,0:T(8,128)(2,1)S(1)}, bf16[192,1536]{1,0:T(8,128)(2,1)S(1)}, u32[]{:S(2)}, u32[]{:S(2)}) collective-permute-start(bf16[192,1536]{1,0:T(8,128)(2,1)S(1)} %fusion.14), channel_id=1, source_target_pairs={{0,16},{1,9},{2,18},{3,11},{4,20},{5,13},{6,22},{7,15},{8,24},{9,1... | collective-permute-start | bytes 1769480 | tf_op jit(solution)/shard_map/ppermute | solution.py:45
  102.2 39.3 %collective-permute-start.14 = (bf16[96,1024]{1,0:T(8,128)(2,1)S(1)}, bf16[96,1024]{1,0:T(8,128)(2,1)S(1)}, u32[]{:S(2)}, u32[]{:S(2)}) collective-permute-start(bf16[96,1024]{1,0:T(8,128)(2,1)S(1)} %pad_maximum_fusion.31), channel_id=1, source_target_pairs={{0,6},{1,7},{2,4},{3,5},{4,2},{5,3},{6,0},{7,1},{8,14},{9,15},{10,... | collective-permute-start | bytes 589832 | tf_op jit(solution)/shard_map/ppermute | solution.py:45
  104.5 38.9 %collective-permute-start.13 = (bf16[96,1024]{1,0:T(8,128)(2,1)S(1)}, bf16[96,1024]{1,0:T(8,128)(2,1)S(1)}, u32[]{:S(2)}, u32[]{:S(2)}) collective-permute-start(bf16[96,1024]{1,0:T(8,128)(2,1)S(1)} %pad_maximum_fusion.30), channel_id=1, source_target_pairs={{0,4},{1,5},{2,6},{3,7},{4,0},{5,1},{6,2},{7,3},{8,12},{9,13},{10,... | collective-permute-start | bytes 589832 | tf_op jit(solution)/shard_map/ppermute | solution.py:45
  107.7 10.7 %collective-permute-start.25 = (bf16[48,1024]{1,0:T(8,128)(2,1)S(1)}, bf16[48,1024]{1,0:T(8,128)(2,1)S(1)}, u32[]{:S(2)}, u32[]{:S(2)}) collective-permute-start(bf16[48,1024]{1,0:T(8,128)(2,1)S(1)} %get-tuple-element.53), channel_id=1, source_target_pairs={{0,6},{1,7},{2,4},{3,5},{4,2},{5,3},{6,0},{7,1},{8,14},{9,15},{10,... | collective-permute-start | bytes 294920 | tf_op jit(solution)/shard_map/ppermute | solution.py:45
  109.9 22.8 %collective-permute-start.24 = (bf16[48,1024]{1,0:T(8,128)(2,1)S(1)}, bf16[48,1024]{1,0:T(8,128)(2,1)S(1)}, u32[]{:S(2)}, u32[]{:S(2)}) collective-permute-start(bf16[48,1024]{1,0:T(8,128)(2,1)S(1)} %get-tuple-element.52), channel_id=1, source_target_pairs={{0,4},{1,5},{2,6},{3,7},{4,0},{5,1},{6,2},{7,3},{8,12},{9,13},{10,... | collective-permute-start | bytes 294920 | tf_op jit(solution)/shard_map/ppermute | solution.py:45
  109.9 22.9 %collective-permute-start.23 = (bf16[48,1024]{1,0:T(8,128)(2,1)S(1)}, bf16[48,1024]{1,0:T(8,128)(2,1)S(1)}, u32[]{:S(2)}, u32[]{:S(2)}) collective-permute-start(bf16[48,1024]{1,0:T(8,128)(2,1)S(1)} %get-tuple-element.51), channel_id=1, source_target_pairs={{0,2},{1,3},{2,0},{3,1},{4,6},{5,7},{6,4},{7,5},{8,10},{9,11},{10,... | collective-permute-start | bytes 294920 | tf_op jit(solution)/shard_map/ppermute | solution.py:45
  118.3 17.4 %collective-permute-start.28 = (bf16[48,1024]{1,0:T(8,128)(2,1)S(1)}, bf16[48,1024]{1,0:T(8,128)(2,1)S(1)}, u32[]{:S(2)}, u32[]{:S(2)}) collective-permute-start(bf16[48,1024]{1,0:T(8,128)(2,1)S(1)} %get-tuple-element.58), channel_id=1, source_target_pairs={{0,6},{1,7},{2,4},{3,5},{4,2},{5,3},{6,0},{7,1},{8,14},{9,15},{10,... | collective-permute-start | bytes 294920 | tf_op jit(solution)/shard_map/ppermute | solution.py:45
  132.7 6.4 %collective-permute-start.27 = (bf16[48,1024]{1,0:T(8,128)(2,1)S(1)}, bf16[48,1024]{1,0:T(8,128)(2,1)S(1)}, u32[]{:S(2)}, u32[]{:S(2)}) collective-permute-start(bf16[48,1024]{1,0:T(8,128)(2,1)S(1)} %get-tuple-element.57), channel_id=1, source_target_pairs={{0,4},{1,5},{2,6},{3,7},{4,0},{5,1},{6,2},{7,3},{8,12},{9,13},{10,... | collective-permute-start | bytes 294920 | tf_op jit(solution)/shard_map/ppermute | solution.py:45
  132.9 7.5 %collective-permute-start.26 = (bf16[48,1024]{1,0:T(8,128)(2,1)S(1)}, bf16[48,1024]{1,0:T(8,128)(2,1)S(1)}, u32[]{:S(2)}, u32[]{:S(2)}) collective-permute-start(bf16[48,1024]{1,0:T(8,128)(2,1)S(1)} %get-tuple-element.56), channel_id=1, source_target_pairs={{0,2},{1,3},{2,0},{3,1},{4,6},{5,7},{6,4},{7,5},{8,10},{9,11},{10,... | collective-permute-start | bytes 294920 | tf_op jit(solution)/shard_map/ppermute | solution.py:45
  135.7 7.7 %collective-permute-start.12 = (bf16[96,1024]{1,0:T(8,128)(2,1)S(1)}, bf16[96,1024]{1,0:T(8,128)(2,1)S(1)}, u32[]{:S(2)}, u32[]{:S(2)}) collective-permute-start(bf16[96,1024]{1,0:T(8,128)(2,1)S(1)} %pad_maximum_fusion.32), channel_id=1, source_target_pairs={{0,2},{1,3},{2,0},{3,1},{4,6},{5,7},{6,4},{7,5},{8,10},{9,11},{10,... | collective-permute-start | bytes 589832 | tf_op jit(solution)/shard_map/ppermute | solution.py:45
  139.1 23.2 %collective-permute-start.32 = (bf16[512,768]{1,0:T(8,128)(2,1)S(1)}, bf16[512,768]{1,0:T(8,128)(2,1)S(1)}, u32[]{:S(2)}, u32[]{:S(2)}) collective-permute-start(bf16[512,768]{1,0:T(8,128)(2,1)S(1)} %convolution_convert_fusion.6), channel_id=1, source_target_pairs={{0,8},{1,17},{2,10},{3,19},{4,12},{5,21},{6,14},{7,23},{8,0},{9,25... | collective-permute-start | bytes 2359304 | tf_op jit(solution)/shard_map/ppermute | solution.py:45
  140.4 34.2 %collective-permute-start.31 = (bf16[2,512,768]{2,1,0:T(8,128)(2,1)S(1)}, bf16[2,512,768]{2,1,0:T(8,128)(2,1)S(1)}, u32[]{:S(2)}, u32[]{:S(2)}) collective-permute-start(bf16[2,512,768]{2,1,0:T(8,128)(2,1)S(1)} %pad_maximum_fusion), channel_id=1, source_target_pairs={{0,8},{1,17},{2,10},{3,19},{4,12},{5,21},{6,14},{7,23},{8,0},{9,25... | collective-permute-start | bytes 4718600 | tf_op jit(solution)/shard_map/ppermute | solution.py:45
  141.6 12.1 %collective-permute-start.29 = (bf16[192,1024]{1,0:T(8,128)(2,1)S(1)}, bf16[192,1024]{1,0:T(8,128)(2,1)S(1)}, u32[]{:S(2)}, u32[]{:S(2)}) collective-permute-start(bf16[192,1024]{1,0:T(8,128)(2,1)S(1)} %pad_maximum_fusion.21), channel_id=1, source_target_pairs={{0,16},{1,9},{2,18},{3,11},{4,20},{5,13},{6,22},{7,15},{8,24},{9,1... | collective-permute-start | bytes 1179656 | tf_op jit(solution)/shard_map/ppermute | solution.py:45
  143.7 18.4 %collective-permute-start.15 = (bf16[192,1024]{1,0:T(8,128)(2,1)S(1)}, bf16[192,1024]{1,0:T(8,128)(2,1)S(1)}, u32[]{:S(2)}, u32[]{:S(2)}) collective-permute-start(bf16[192,1024]{1,0:T(8,128)(2,1)S(1)} %pad_maximum_fusion.16), channel_id=1, source_target_pairs={{0,16},{1,9},{2,18},{3,11},{4,20},{5,13},{6,22},{7,15},{8,24},{9,1... | collective-permute-start | bytes 1179656 | tf_op jit(solution)/shard_map/ppermute | solution.py:45
  153.7 9.2 %collective-permute-start.30 = (bf16[96,2048]{1,0:T(8,128)(2,1)S(1)}, bf16[96,2048]{1,0:T(8,128)(2,1)S(1)}, u32[]{:S(2)}, u32[]{:S(2)}) collective-permute-start(bf16[96,2048]{1,0:T(8,128)(2,1)S(1)} %slice_dynamic-update-slice_fusion), channel_id=1, source_target_pairs={{0,1},{1,0},{2,3},{3,2},{4,5},{5,4},{6,7},{7,6},{8,9},{9,8},{10,11... | collective-permute-start | bytes 1179656 | tf_op jit(solution)/shard_map/ppermute | solution.py:45
  162.1 2.2 %collective-permute-start.16 = (bf16[96,2048]{1,0:T(8,128)(2,1)S(1)}, bf16[96,2048]{1,0:T(8,128)(2,1)S(1)}, u32[]{:S(2)}, u32[]{:S(2)}) collective-permute-start(bf16[96,2048]{1,0:T(8,128)(2,1)S(1)} %slice_dynamic-update-slice_fusion.8), channel_id=1, source_target_pairs={{0,1},{1,0},{2,3},{3,2},{4,5},{5,4},{6,7},{7,6},{8,9},{9,8},{10,11... | collective-permute-start | bytes 1179656 | tf_op jit(solution)/shard_map/ppermute | solution.py:45
  175.2 2.3 %copy-start.1 = (bf16[256,2048]{1,0:T(8,128)(2,1)S(1)}, bf16[256,2048]{1,0:T(8,128)(2,1)}, u32[]{:S(2)}) copy-start(bf16[256,2048]{1,0:T(8,128)(2,1)} %param.5) | copy-start | bytes 3145732

commit v2 on v1

--- a/solution.py
+++ b/solution.py
@@ -79,12 +79,8 @@
     half = steps * CAP
 
     weights_own = expert_weights[0]
-    gates_far = moves.weight_pair(weights_own[:, :2])
-    down_far = moves.weight_pair(weights_own[:, 2])
-    pair = (
-        (weights_own[:, 0], weights_own[:, 1], weights_own[:, 2]),
-        (gates_far[:, 0], gates_far[:, 1], down_far),
-    )
+    weights_far = moves.weight_pair(weights_own)
+    pair = (weights_own, weights_far)
 
     slot = jnp.arange(2 * half, dtype=jnp.int32)
     slot_expert = ((slot % half // CAP) ^ own_z) * 2 + ((slot // half) ^ own_c)
@@ -115,9 +111,9 @@
         return whole
 
     def send_local(table, source):
-        other = contract(table[:, half:], source, 0, 0).astype(BF16)
-        came = moves.core(other)
-        same = contract(table[:, :half], source, 0, 0).astype(BF16)
+        both = contract(table, source, 0, 0).astype(BF16)
+        same = both[:half]
+        came = moves.core(both[half:])
         own = interleaved(taken(same, 0, 1), taken(came, 0, 1))
         out = interleaved(taken(same, 2, 3), taken(came, 2, 3))
         return own, moves.column_pair(out)
@@ -150,32 +146,41 @@
         rows = jnp.concatenate([placed(source(own, 0), source(out, 0)), came])
         return contract(table, rows, 1, 0).astype(BF16)
 
-    def inward(rows, which):
-        return contract(rows[:, :quarter_width], pair[0][which], 1, 0) + contract(
-            rows[:, quarter_width:], pair[1][which], 1, 0
+    def inward(rows, which, sides=(0, 1)):
+        return sum(
+            contract(
+                rows[:, i * quarter_width : (i + 1) * quarter_width], pair[i][:, which], 1, 0
+            )
+            for i in sides
         )
 
     def outward(terms):
         return jnp.concatenate(
             [
-                sum(contract(value, pair[i][which], 1, 1) for value, which in terms)
+                sum(contract(value, pair[i][:, which], 1, 1) for value, which in terms)
                 for i in (0, 1)
             ],
             axis=1,
         ).astype(BF16)
 
-    def wide(rows, *which):
-        return jnp.concatenate([inward(rows, i) for i in which], axis=1)
+    def base(rows):
+        return tuple(lax.optimization_barrier([inward(rows, i, (0,)) for i in (0, 1)]))
+
+    def added(start, rows):
+        both = [value + inward(rows, i, (1,)) for i, value in enumerate(start)]
+        return jnp.concatenate(both, axis=1)
 
     rows_own, rows_near = send_local(dispatch, tokens)
     (rows_own,) = by_z([rows_own])
     (rows_near,) = by_z([rows_near])
     scaled_own, scaled_near = by_z(send_local(combine, out_grad))
 
-    part_own = wide(rows_own, 0, 1)
+    base_own = base(rows_own)
+    base_near = base(rows_near)
+    part_own = added(base_own, rows_own)
     message = part_own.astype(BF16)
     near_extra = moves.column_pair(message)
-    part_near = wide(rows_near, 0, 1)
+    part_near = added(base_near, rows_near)
     message = part_near.astype(BF16)
     own_extra = moves.column_pair(message)
 
@@ -193,7 +198,7 @@
     out_own = outward([(act_own, 2)])
     back_near, back_own = by_z([out_near, out_own])
 
-    hid_own, hid_near = wide(scaled_own, 2), wide(scaled_near, 2)
+    hid_own, hid_near = inward(scaled_own, 2), inward(scaled_near, 2)
     message = jnp.concatenate([hid_near, hid_own]).astype(BF16)
     extra = moves.column_pair(message)
     hid_own = hid_own + extra[: 2 * half].astype(F32)

time: 178 us -> 148 us (0.83); the launches traced: 177 us -> 145 us
  waiting for transfers between devices: 84 us -> 56.9 us
  matrix products: 32.9 us -> 29.9 us
  local copies, waits for them, and re-layouts: 7.64 us -> 5.35 us
    ppermute x33 -> x32, waiting for transfers between devices: 84 us -> 56.9 us  [move(): return lax.ppermute(value, ALL, pairs)]
    dot_general x36 -> x34, matrix products: 32.6 us -> 29.7 us  [contract(): lax.dot_general(left, right, (((left_dim,), (right_dim,)), ((), ())), pre...]
    ppermute x33 -> x32, starting transfers between devices: 46.9 us -> 45.6 us  [move(): return lax.ppermute(value, ALL, pairs)]
  transfers between devices with their start and end apart: 33 -> 32, of which waited for: 15 -> 15; matrix products, arithmetic and copies ran while one was open for 19% -> 13% of each run, Pallas kernels for 0% -> 0%
where the time goes in v2:
time: 148 us; the launch traced here: 145 us
  waiting for transfers between devices  56.9 us (38%)
  starting transfers between devices  45.6 us (31%)
  matrix products  29.9 us (20%)
  other arithmetic  5.82 us (4%)
  local copies, waits for them, and re-layouts  5.35 us (4%)
  between operations  1.73 us (1%)
    ppermute x32, waiting for transfers between devices, move(): return lax.ppermute(value, ALL, pairs)  56.9 us
    ppermute x32, starting transfers between devices, move(): return lax.ppermute(value, ALL, pairs)  45.6 us
    dot_general x34, matrix products, contract(): lax.dot_general(left, right, (((left_dim,), (right_dim,)), ((), ())), pre...  29.7 us
  transfers between devices with their start and end apart: 32, of which 15 were waited for; matrix products, arithmetic and copies ran while one was open for 13% of the time, Pallas kernels for 0%

profile of v2, /device:TPU:0, one launch (start us, length us, event | category | flops | bytes accessed | tf_op | source)
XLA Modules:
  0.0 145.3 jit_solution(14396315385039042249)
XLA Ops:
  0.7 0.8 convert_element_type.105
  1.5 1.0 fusion.1
  3.2 0.8 fusion.73
  4.9 0.8 fusion.72
  6.3 2.5 %collective-permute-start.4 = (bf16[512,3,768]{2,0,1:T(8,128)(2,1)S(1)}, bf16[512,3,768]{2,0,1:T(8,128)(2,1)}, u32[]{:S(2)}, u32[]{:S(2)}) collective-permute-start(bf16[512,3,768]{2,0,1:T(8,128)(2,1)S(1)} %bitcast.123), channel_id=1, source_target_pairs={{0,8},{1,17},{2,10},{3,19},{4,12},{5,21},{6,14},{7,23},{8,0},{9,25... | collective-permute-start | bytes 7077896 | tf_op jit(solution)/shard_map/ppermute | solution.py:45
  9.0 1.1 constant_dynamic-slice_fusion.9
  10.1 1.1 constant_dynamic-slice_fusion.1
  11.4 1.6 %collective-permute-start.1 = (bf16[48,1024]{1,0:T(8,128)(2,1)S(1)}, bf16[48,1024]{1,0:T(8,128)(2,1)S(1)}, u32[]{:S(2)}, u32[]{:S(2)}) collective-permute-start(bf16[48,1024]{1,0:T(8,128)(2,1)S(1)} %get-tuple-element.35), channel_id=1, source_target_pairs={{0,2},{1,3},{2,0},{3,1},{4,6},{5,7},{6,4},{7,5},{8,10},{9,11},{10,... | collective-permute-start | bytes 294920 | tf_op jit(solution)/shard_map/ppermute | solution.py:45
  13.0 2.6 %collective-permute-start.2 = (bf16[48,1024]{1,0:T(8,128)(2,1)S(1)}, bf16[48,1024]{1,0:T(8,128)(2,1)S(1)}, u32[]{:S(2)}, u32[]{:S(2)}) collective-permute-start(bf16[48,1024]{1,0:T(8,128)(2,1)S(1)} %get-tuple-element.36), channel_id=1, source_target_pairs={{0,4},{1,5},{2,6},{3,7},{4,0},{5,1},{6,2},{7,3},{8,12},{9,13},{10,... | collective-permute-start | bytes 294920 | tf_op jit(solution)/shard_map/ppermute | solution.py:45
  15.9 1.6 %collective-permute-start.5 = (bf16[192,1024]{1,0:T(8,128)(2,1)S(1)}, bf16[192,1024]{1,0:T(8,128)(2,1)S(1)}, u32[]{:S(2)}, u32[]{:S(2)}) collective-permute-start(bf16[192,1024]{1,0:T(8,128)(2,1)S(1)} %bitcast.174), channel_id=1, source_target_pairs={{0,16},{1,9},{2,18},{3,11},{4,20},{5,13},{6,22},{7,15},{8,24},{9,1... | collective-permute-start | bytes 1179656 | tf_op jit(solution)/shard_map/ppermute | solution.py:45
  17.6 1.0 collective-permute-start.17
  18.5 5.1 %collective-permute-done.2 = bf16[48,1024]{1,0:T(8,128)(2,1)S(1)} collective-permute-done((bf16[48,1024]{1,0:T(8,128)(2,1)S(1)}, bf16[48,1024]{1,0:T(8,128)(2,1)S(1)}, u32[]{:S(2)}, u32[]{:S(2)}) %collective-permute-start.2) | collective-permute-done | bytes 98336 | tf_op jit(solution)/shard_map/ppermute | solution.py:45
  24.4 3.6 %collective-permute-done.5 = bf16[192,1024]{1,0:T(8,128)(2,1)S(1)} collective-permute-done((bf16[192,1024]{1,0:T(8,128)(2,1)S(1)}, bf16[192,1024]{1,0:T(8,128)(2,1)S(1)}, u32[]{:S(2)}, u32[]{:S(2)}) %collective-permute-start.5) | collective-permute-done | bytes 393248 | tf_op jit(solution)/shard_map/ppermute | solution.py:45
  28.0 0.7 collective-permute-start.6
  28.7 3.5 %collective-permute-start.7 = (bf16[48,1024]{1,0:T(8,128)(2,1)S(1)}, bf16[48,1024]{1,0:T(8,128)(2,1)S(1)}, u32[]{:S(2)}, u32[]{:S(2)}) collective-permute-start(bf16[48,1024]{1,0:T(8,128)(2,1)S(1)} %get-tuple-element.41), channel_id=1, source_target_pairs={{0,4},{1,5},{2,6},{3,7},{4,0},{5,1},{6,2},{7,3},{8,12},{9,13},{10,... | collective-permute-start | bytes 294920 | tf_op jit(solution)/shard_map/ppermute | solution.py:45
  32.4 3.9 %collective-permute-done.17 = bf16[192,1024]{1,0:T(8,128)(2,1)S(1)} collective-permute-done((bf16[192,1024]{1,0:T(8,128)(2,1)S(1)}, bf16[192,1024]{1,0:T(8,128)(2,1)S(1)}, u32[]{:S(2)}, u32[]{:S(2)}) %collective-permute-start.17) | collective-permute-done | bytes 393248 | tf_op jit(solution)/shard_map/ppermute | solution.py:45
  36.5 0.7 collective-permute-start.18
  37.3 3.6 %collective-permute-start.19 = (bf16[96,1024]{1,0:T(8,128)(2,1)S(1)}, bf16[96,1024]{1,0:T(8,128)(2,1)S(1)}, u32[]{:S(2)}, u32[]{:S(2)}) collective-permute-start(bf16[96,1024]{1,0:T(8,128)(2,1)S(1)} %pad_maximum_fusion.37), channel_id=1, source_target_pairs={{0,4},{1,5},{2,6},{3,7},{4,0},{5,1},{6,2},{7,3},{8,12},{9,13},{10,... | collective-permute-start | bytes 589832 | tf_op jit(solution)/shard_map/ppermute | solution.py:45
  42.0 4.1 %collective-permute-done.18 = bf16[96,1024]{1,0:T(8,128)(2,1)S(1)} collective-permute-done((bf16[96,1024]{1,0:T(8,128)(2,1)S(1)}, bf16[96,1024]{1,0:T(8,128)(2,1)S(1)}, u32[]{:S(2)}, u32[]{:S(2)}) %collective-permute-start.18) | collective-permute-done | bytes 196640 | tf_op jit(solution)/shard_map/ppermute | solution.py:45
  46.1 8.7 %collective-permute-done.19 = bf16[96,1024]{1,0:T(8,128)(2,1)S(1)} collective-permute-done((bf16[96,1024]{1,0:T(8,128)(2,1)S(1)}, bf16[96,1024]{1,0:T(8,128)(2,1)S(1)}, u32[]{:S(2)}, u32[]{:S(2)}) %collective-permute-start.19) | collective-permute-done | bytes 196640 | tf_op jit(solution)/shard_map/ppermute | solution.py:45
  55.0 1.5 %fusion.33 = f32[192,768]{1,0:T(8,128)S(1)} fusion(bf16[512,3,768]{2,0,1:T(8,128)(2,1)} %collective-permute-done.4, bf16[192,1024]{1,0:T(8,128)(2,1)S(1)} %pad_maximum_fusion.18), kind=kOutput, calls=%fused_computation.89 | convolution fusion | flops 150994944 | bytes 1572864 | tf_op jit(solution)/shard_map/dot_general | solution.py:28
  56.8 1.5 %fusion.32 = f32[192,768]{1,0:T(8,128)S(1)} fusion(bf16[512,3,768]{2,0,1:T(8,128)(2,1)} %collective-permute-done.4, bf16[192,1024]{1,0:T(8,128)(2,1)S(1)} %pad_maximum_fusion.19), kind=kOutput, calls=%fused_computation.88 | convolution fusion | flops 150994944 | bytes 1572864 | tf_op jit(solution)/shard_map/dot_general | solution.py:28
  59.2 1.5 %convolution_add_fusion.3 = f32[192,768]{1,0:T(8,128)S(1)} fusion(f32[192,768]{1,0:T(8,128)S(1)} %fusion.26, bf16[512,3,768]{2,0,1:T(8,128)(2,1)} %collective-permute-done.4, bf16[192,1024]{1,0:T(8,128)(2,1)S(1)} %pad_maximum_fusion.14), kind=kOutput, calls=%fused_computation.26 | convolution fusion | flops 151142400 | bytes 2162688 | tf_op jit(solution)/shard_map/dot_general | solution.py:28
  60.6 1.5 %convolution_add_fusion.2 = f32[192,768]{1,0:T(8,128)S(1)} fusion(f32[192,768]{1,0:T(8,128)S(1)} %fusion.28, bf16[512,3,768]{2,0,1:T(8,128)(2,1)} %collective-permute-done.4, bf16[192,1024]{1,0:T(8,128)(2,1)S(1)} %pad_maximum_fusion.14), kind=kOutput, calls=%fused_computation.25 | convolution fusion | flops 151142400 | bytes 2162688 | tf_op jit(solution)/shard_map/dot_general | solution.py:28
  62.2 1.6 %collective-permute-start.9 = (bf16[192,1536]{1,0:T(8,128)(2,1)S(1)}, bf16[192,1536]{1,0:T(8,128)(2,1)S(1)}, u32[]{:S(2)}, u32[]{:S(2)}) collective-permute-start(bf16[192,1536]{1,0:T(8,128)(2,1)S(1)} %fusion.14), channel_id=1, source_target_pairs={{0,16},{1,9},{2,18},{3,11},{4,20},{5,13},{6,22},{7,15},{8,24},{9,1... | collective-permute-start | bytes 1769480 | tf_op jit(solution)/shard_map/ppermute | solution.py:45
  63.8 1.5 %convolution_add_fusion.5 = f32[192,768]{1,0:T(8,128)S(1)} fusion(f32[192,768]{1,0:T(8,128)S(1)} %fusion.27, bf16[512,3,768]{2,0,1:T(8,128)(2,1)} %collective-permute-done.4, bf16[192,1024]{1,0:T(8,128)(2,1)S(1)} %pad_maximum_fusion.12), kind=kOutput, calls=%fused_computation.28 | convolution fusion | flops 151142400 | bytes 2162688 | tf_op jit(solution)/shard_map/dot_general | solution.py:28
  65.2 1.5 %convolution_add_fusion.4 = f32[192,768]{1,0:T(8,128)S(1)} fusion(f32[192,768]{1,0:T(8,128)S(1)} %fusion.29, bf16[512,3,768]{2,0,1:T(8,128)(2,1)} %collective-permute-done.4, bf16[192,1024]{1,0:T(8,128)(2,1)S(1)} %pad_maximum_fusion.12), kind=kOutput, calls=%fused_computation.27 | convolution fusion | flops 151142400 | bytes 2162688 | tf_op jit(solution)/shard_map/dot_general | solution.py:28
  67.3 7.5 %collective-permute-done.9 = bf16[192,1536]{1,0:T(8,128)(2,1)S(1)} collective-permute-done((bf16[192,1536]{1,0:T(8,128)(2,1)S(1)}, bf16[192,1536]{1,0:T(8,128)(2,1)S(1)}, u32[]{:S(2)}, u32[]{:S(2)}) %collective-permute-start.9) | collective-permute-done | bytes 589856 | tf_op jit(solution)/shard_map/ppermute | solution.py:45
  75.3 5.9 %collective-permute-done.10 = bf16[192,1536]{1,0:T(8,128)(2,1)S(1)} collective-permute-done((bf16[192,1536]{1,0:T(8,128)(2,1)S(1)}, bf16[192,1536]{1,0:T(8,128)(2,1)S(1)}, u32[]{:S(2)}, u32[]{:S(2)}) %collective-permute-start.10) | collective-permute-done | bytes 589856 | tf_op jit(solution)/shard_map/ppermute | solution.py:45
  82.8 1.5 %fusion.31 = f32[192,512]{1,0:T(8,128)S(1)} fusion(bf16[192,768]{1,0:T(8,128)(2,1)S(1)} %get-tuple-element.83, bf16[512,3,768]{2,0,1:T(8,128)(2,1)} %collective-permute-done.4), kind=kOutput, calls=%fused_computation.87 | convolution fusion | flops 150994944 | bytes 1474560 | tf_op jit(solution)/shard_map/dot_general | solution.py:28
  84.3 1.5 %fusion.10 = bf16[192,512]{1,0:T(8,128)(2,1)S(1)} fusion(f32[192,512]{1,0:T(8,128)S(1)} %fusion.31, bf16[192,768]{1,0:T(8,128)(2,1)S(1)} %get-tuple-element.84, bf16[512,3,768]{2,0,1:T(8,128)(2,1)} %collective-permute-done.4), kind=kOutput, calls=%fused_computation.38 | convolution fusion | flops 151191552 | bytes 1671168 | tf_op jit(solution)/shard_map/dot_general | solution.py:28
  86.4 0.6 fusion.4
  87.0 0.6 fusion.5
  88.0 1.5 %fusion.30 = f32[192,512]{1,0:T(8,128)S(1)} fusion(bf16[192,768]{1,0:T(8,128)(2,1)S(1)} %get-tuple-element.70, bf16[512,3,768]{2,0,1:T(8,128)(2,1)} %collective-permute-done.4), kind=kOutput, calls=%fused_computation.86 | convolution fusion | flops 150994944 | bytes 1474560 | tf_op jit(solution)/shard_map/dot_general | solution.py:28
  89.5 1.5 %fusion.12 = bf16[192,512]{1,0:T(8,128)(2,1)S(1)} fusion(f32[192,512]{1,0:T(8,128)S(1)} %fusion.30, bf16[192,768]{1,0:T(8,128)(2,1)S(1)} %get-tuple-element.69, bf16[512,3,768]{2,0,1:T(8,128)(2,1)} %collective-permute-done.4), kind=kOutput, calls=%fused_computation.40 | convolution fusion | flops 151191552 | bytes 1671168 | tf_op jit(solution)/shard_map/dot_general | solution.py:28
  91.6 1.5 %convolution_convert_fusion.9 = bf16[192,512]{1,0:T(8,128)(2,1)S(1)} fusion(bf16[192,768]{1,0:T(8,128)(2,1)S(1)} %get-tuple-element.45, bf16[512,3,768]{2,0,1:T(8,128)(2,1)} %collective-permute-done.4), kind=kOutput, calls=%fused_computation.43 | convolution fusion | flops 151093248 | bytes 1277952 | tf_op jit(solution)/shard_map/dot_general | solution.py:28
  93.4 0.9 collective-permute-start.30
  94.7 0.6 convolution_convert_fusion.4
  95.3 1.3 collective-permute-start.31
  96.6 3.0 %collective-permute-start.22 = (bf16[48,1024]{1,0:T(8,128)(2,1)S(1)}, bf16[48,1024]{1,0:T(8,128)(2,1)S(1)}, u32[]{:S(2)}, u32[]{:S(2)}) collective-permute-start(bf16[48,1024]{1,0:T(8,128)(2,1)S(1)} %get-tuple-element.59), channel_id=1, source_target_pairs={{0,2},{1,3},{2,0},{3,1},{4,6},{5,7},{6,4},{7,5},{8,10},{9,11},{10,... | collective-permute-start | bytes 294920 | tf_op jit(solution)/shard_map/ppermute | solution.py:45
  99.6 1.0 collective-permute-start.23
  100.6 1.4 collective-permute-start.24
  102.1 1.5 %convolution_convert_fusion.7 = bf16[192,512]{1,0:T(8,128)(2,1)S(1)} fusion(bf16[192,768]{1,0:T(8,128)(2,1)S(1)} %get-tuple-element.46, bf16[512,3,768]{2,0,1:T(8,128)(2,1)} %collective-permute-done.4), kind=kOutput, calls=%fused_computation.41 | convolution fusion | flops 151093248 | bytes 1277952 | tf_op jit(solution)/shard_map/dot_general | solution.py:28
  103.8 1.1 collective-permute-start.25
  104.9 0.8 collective-permute-done.23
  105.7 2.9 %collective-permute-start.26 = (bf16[48,1024]{1,0:T(8,128)(2,1)S(1)}, bf16[48,1024]{1,0:T(8,128)(2,1)S(1)}, u32[]{:S(2)}, u32[]{:S(2)}) collective-permute-start(bf16[48,1024]{1,0:T(8,128)(2,1)S(1)} %get-tuple-element.65), channel_id=1, source_target_pairs={{0,4},{1,5},{2,6},{3,7},{4,0},{5,1},{6,2},{7,3},{8,12},{9,13},{10,... | collective-permute-start | bytes 294920 | tf_op jit(solution)/shard_map/ppermute | solution.py:45
  108.6 0.7 collective-permute-done.24
  109.3 2.9 %collective-permute-start.27 = (bf16[48,1024]{1,0:T(8,128)(2,1)S(1)}, bf16[48,1024]{1,0:T(8,128)(2,1)S(1)}, u32[]{:S(2)}, u32[]{:S(2)}) collective-permute-start(bf16[48,1024]{1,0:T(8,128)(2,1)S(1)} %get-tuple-element.66), channel_id=1, source_target_pairs={{0,6},{1,7},{2,4},{3,5},{4,2},{5,3},{6,0},{7,1},{8,14},{9,15},{10,... | collective-permute-start | bytes 294920 | tf_op jit(solution)/shard_map/ppermute | solution.py:45
  112.4 0.9 collective-permute-done.25
  113.3 1.1 collective-permute-start.11
  114.4 1.1 collective-permute-start.12
  115.5 2.1 %collective-permute-done.27 = bf16[48,1024]{1,0:T(8,128)(2,1)S(1)} collective-permute-done((bf16[48,1024]{1,0:T(8,128)(2,1)S(1)}, bf16[48,1024]{1,0:T(8,128)(2,1)S(1)}, u32[]{:S(2)}, u32[]{:S(2)}) %collective-permute-start.27) | collective-permute-done | bytes 98336 | tf_op jit(solution)/shard_map/ppermute | solution.py:45
  117.7 5.7 %collective-permute-start.13 = (bf16[96,1024]{1,0:T(8,128)(2,1)S(1)}, bf16[96,1024]{1,0:T(8,128)(2,1)S(1)}, u32[]{:S(2)}, u32[]{:S(2)}) collective-permute-start(bf16[96,1024]{1,0:T(8,128)(2,1)S(1)} %pad_maximum_fusion.31), channel_id=1, source_target_pairs={{0,6},{1,7},{2,4},{3,5},{4,2},{5,3},{6,0},{7,1},{8,14},{9,15},{10,... | collective-permute-start | bytes 589832 | tf_op jit(solution)/shard_map/ppermute | solution.py:45
  123.4 1.5 %collective-permute-done.11 = bf16[96,1024]{1,0:T(8,128)(2,1)S(1)} collective-permute-done((bf16[96,1024]{1,0:T(8,128)(2,1)S(1)}, bf16[96,1024]{1,0:T(8,128)(2,1)S(1)}, u32[]{:S(2)}, u32[]{:S(2)}) %collective-permute-start.11) | collective-permute-done | bytes 196640 | tf_op jit(solution)/shard_map/ppermute | solution.py:45
  125.3 5.3 %collective-permute-done.12 = bf16[96,1024]{1,0:T(8,128)(2,1)S(1)} collective-permute-done((bf16[96,1024]{1,0:T(8,128)(2,1)S(1)}, bf16[96,1024]{1,0:T(8,128)(2,1)S(1)}, u32[]{:S(2)}, u32[]{:S(2)}) %collective-permute-start.12) | collective-permute-done | bytes 196640 | tf_op jit(solution)/shard_map/ppermute | solution.py:45
  130.8 0.6 collective-permute-start.14
  131.5 1.2 collective-permute-done.28
  132.9 5.8 %collective-permute-done.14 = bf16[192,1024]{1,0:T(8,128)(2,1)S(1)} collective-permute-done((bf16[192,1024]{1,0:T(8,128)(2,1)S(1)}, bf16[192,1024]{1,0:T(8,128)(2,1)S(1)}, u32[]{:S(2)}, u32[]{:S(2)}) %collective-permute-start.14) | collective-permute-done | bytes 393248 | tf_op jit(solution)/shard_map/ppermute | solution.py:45
  138.9 0.6 fusion.6
  139.5 1.5 %convolution_convert_fusion = bf16[256,2048]{1,0:T(8,128)(2,1)} fusion(pred[256,192]{0,1:T(32,128)(4,1)S(1)} %fusion.13, bf16[96,2048]{1,0:T(8,128)(2,1)S(1)} %collective-permute-done.29, bf16[96,2048]{1,0:T(8,128)(2,1)S(1)} %slice_dynamic-update-slice_fusion.4), kind=kOutput, calls=%fused_computation | convolution fusion | flops 203423744 | bytes 1884160 | tf_op jit(solution)/shard_map/dot_general | solution.py:28
  141.0 1.4 convolution_convert_fusion.1
  142.4 0.6 fusion.7
  143.0 0.6 fusion.8
  143.7 1.7 %maximum_bitcast_fusion = bf16[1,512,3,768]{3,1,2,0:T(8,128)(2,1)} fusion(bf16[512,1,768]{2,0,1:T(8,128)(2,1)S(1)} %fusion.6, bf16[512,1,768]{2,0,1:T(8,128)(2,1)S(1)} %fusion.8, bf16[512,1,768]{2,0,1:T(8,128)(2,1)S(1)} %fusion.7), kind=kLoop, calls=%fused_computation.4 | loop fusion | flops 2359296 | bytes 4718592 | tf_op jit(solution)/shard_map/broadcast_in_dim | solution.py:234
  (151 shorter events, 12.4 us)
Async XLA Ops:
  0.6 2.1 %copy-start = (bf16[256,2048]{1,0:T(8,128)(2,1)S(1)}, bf16[256,2048]{1,0:T(8,128)(2,1)}, u32[]{:S(2)}) copy-start(bf16[256,2048]{1,0:T(8,128)(2,1)} %param.5) | copy-start | bytes 3145732
  2.8 1.7 %copy-start.3 = (bf16[256,2048]{1,0:T(8,128)(2,1)S(1)}, bf16[256,2048]{1,0:T(8,128)(2,1)}, u32[]{:S(2)}) copy-start(bf16[256,2048]{1,0:T(8,128)(2,1)} %param.9) | copy-start | bytes 3145732
  4.0 5.0 %collective-permute-start = (bf16[96,2048]{1,0:T(8,128)(2,1)}, bf16[96,2048]{1,0:T(8,128)(2,1)}, u32[]{:S(2)}, u32[]{:S(2)}) collective-permute-start(bf16[96,2048]{1,0:T(8,128)(2,1)} %get-tuple-element.82), channel_id=1, source_target_pairs={{0,1},{1,0},{2,3},{3,2},{4,5},{5,4},{6,7},{7,6},{8,9},{9,8},{10,11... | collective-permute-start | bytes 1179656 | tf_op jit(solution)/shard_map/ppermute | solution.py:45
  4.5 1.8 %copy-start.2 = (bf16[1,512,3,768]{3,1,2,0:T(8,128)(2,1)S(1)}, bf16[1,512,3,768]{3,1,2,0:T(8,128)(2,1)}, u32[]{:S(2)}) copy-start(bf16[1,512,3,768]{3,1,2,0:T(8,128)(2,1)} %param.8) | copy-start | bytes 7077892
  5.7 4.5 %collective-permute-start.16 = (bf16[96,2048]{1,0:T(8,128)(2,1)}, bf16[96,2048]{1,0:T(8,128)(2,1)}, u32[]{:S(2)}, u32[]{:S(2)}) collective-permute-start(bf16[96,2048]{1,0:T(8,128)(2,1)} %get-tuple-element.80), channel_id=1, source_target_pairs={{0,1},{1,0},{2,3},{3,2},{4,5},{5,4},{6,7},{7,6},{8,9},{9,8},{10,11... | collective-permute-start | bytes 1179656 | tf_op jit(solution)/shard_map/ppermute | solution.py:45
  6.3 48.7 %collective-permute-start.4 = (bf16[512,3,768]{2,0,1:T(8,128)(2,1)S(1)}, bf16[512,3,768]{2,0,1:T(8,128)(2,1)}, u32[]{:S(2)}, u32[]{:S(2)}) collective-permute-start(bf16[512,3,768]{2,0,1:T(8,128)(2,1)S(1)} %bitcast.123), channel_id=1, source_target_pairs={{0,8},{1,17},{2,10},{3,19},{4,12},{5,21},{6,14},{7,23},{8,0},{9,25... | collective-permute-start | bytes 7077896 | tf_op jit(solution)/shard_map/ppermute | solution.py:45
  11.4 6.2 %collective-permute-start.1 = (bf16[48,1024]{1,0:T(8,128)(2,1)S(1)}, bf16[48,1024]{1,0:T(8,128)(2,1)S(1)}, u32[]{:S(2)}, u32[]{:S(2)}) collective-permute-start(bf16[48,1024]{1,0:T(8,128)(2,1)S(1)} %get-tuple-element.35), channel_id=1, source_target_pairs={{0,2},{1,3},{2,0},{3,1},{4,6},{5,7},{6,4},{7,5},{8,10},{9,11},{10,... | collective-permute-start | bytes 294920 | tf_op jit(solution)/shard_map/ppermute | solution.py:45
  13.0 10.6 %collective-permute-start.2 = (bf16[48,1024]{1,0:T(8,128)(2,1)S(1)}, bf16[48,1024]{1,0:T(8,128)(2,1)S(1)}, u32[]{:S(2)}, u32[]{:S(2)}) collective-permute-start(bf16[48,1024]{1,0:T(8,128)(2,1)S(1)} %get-tuple-element.36), channel_id=1, source_target_pairs={{0,4},{1,5},{2,6},{3,7},{4,0},{5,1},{6,2},{7,3},{8,12},{9,13},{10,... | collective-permute-start | bytes 294920 | tf_op jit(solution)/shard_map/ppermute | solution.py:45
  15.6 8.0 %collective-permute-start.3 = (bf16[48,1024]{1,0:T(8,128)(2,1)S(1)}, bf16[48,1024]{1,0:T(8,128)(2,1)S(1)}, u32[]{:S(2)}, u32[]{:S(2)}) collective-permute-start(bf16[48,1024]{1,0:T(8,128)(2,1)S(1)} %get-tuple-element.37), channel_id=1, source_target_pairs={{0,6},{1,7},{2,4},{3,5},{4,2},{5,3},{6,0},{7,1},{8,14},{9,15},{10,... | collective-permute-start | bytes 294920 | tf_op jit(solution)/shard_map/ppermute | solution.py:45
  15.9 12.1 %collective-permute-start.5 = (bf16[192,1024]{1,0:T(8,128)(2,1)S(1)}, bf16[192,1024]{1,0:T(8,128)(2,1)S(1)}, u32[]{:S(2)}, u32[]{:S(2)}) collective-permute-start(bf16[192,1024]{1,0:T(8,128)(2,1)S(1)} %bitcast.174), channel_id=1, source_target_pairs={{0,16},{1,9},{2,18},{3,11},{4,20},{5,13},{6,22},{7,15},{8,24},{9,1... | collective-permute-start | bytes 1179656 | tf_op jit(solution)/shard_map/ppermute | solution.py:45
  17.6 18.8 %collective-permute-start.17 = (bf16[192,1024]{1,0:T(8,128)(2,1)S(1)}, bf16[192,1024]{1,0:T(8,128)(2,1)S(1)}, u32[]{:S(2)}, u32[]{:S(2)}) collective-permute-start(bf16[192,1024]{1,0:T(8,128)(2,1)S(1)} %bitcast.173), channel_id=1, source_target_pairs={{0,16},{1,9},{2,18},{3,11},{4,20},{5,13},{6,22},{7,15},{8,24},{9,1... | collective-permute-start | bytes 1179656 | tf_op jit(solution)/shard_map/ppermute | solution.py:45
  28.0 9.3 %collective-permute-start.6 = (bf16[48,1024]{1,0:T(8,128)(2,1)S(1)}, bf16[48,1024]{1,0:T(8,128)(2,1)S(1)}, u32[]{:S(2)}, u32[]{:S(2)}) collective-permute-start(bf16[48,1024]{1,0:T(8,128)(2,1)S(1)} %get-tuple-element.40), channel_id=1, source_target_pairs={{0,2},{1,3},{2,0},{3,1},{4,6},{5,7},{6,4},{7,5},{8,10},{9,11},{10,... | collective-permute-start | bytes 294920 | tf_op jit(solution)/shard_map/ppermute | solution.py:45
  28.7 12.1 %collective-permute-start.7 = (bf16[48,1024]{1,0:T(8,128)(2,1)S(1)}, bf16[48,1024]{1,0:T(8,128)(2,1)S(1)}, u32[]{:S(2)}, u32[]{:S(2)}) collective-permute-start(bf16[48,1024]{1,0:T(8,128)(2,1)S(1)} %get-tuple-element.41), channel_id=1, source_target_pairs={{0,4},{1,5},{2,6},{3,7},{4,0},{5,1},{6,2},{7,3},{8,12},{9,13},{10,... | collective-permute-start | bytes 294920 | tf_op jit(solution)/shard_map/ppermute | solution.py:45
  32.2 9.1 %collective-permute-start.8 = (bf16[48,1024]{1,0:T(8,128)(2,1)S(1)}, bf16[48,1024]{1,0:T(8,128)(2,1)S(1)}, u32[]{:S(2)}, u32[]{:S(2)}) collective-permute-start(bf16[48,1024]{1,0:T(8,128)(2,1)S(1)} %get-tuple-element.42), channel_id=1, source_target_pairs={{0,6},{1,7},{2,4},{3,5},{4,2},{5,3},{6,0},{7,1},{8,14},{9,15},{10,... | collective-permute-start | bytes 294920 | tf_op jit(solution)/shard_map/ppermute | solution.py:45
  36.5 9.6 %collective-permute-start.18 = (bf16[96,1024]{1,0:T(8,128)(2,1)S(1)}, bf16[96,1024]{1,0:T(8,128)(2,1)S(1)}, u32[]{:S(2)}, u32[]{:S(2)}) collective-permute-start(bf16[96,1024]{1,0:T(8,128)(2,1)S(1)} %pad_maximum_fusion.39), channel_id=1, source_target_pairs={{0,2},{1,3},{2,0},{3,1},{4,6},{5,7},{6,4},{7,5},{8,10},{9,11},{10,... | collective-permute-start | bytes 589832 | tf_op jit(solution)/shard_map/ppermute | solution.py:45
  37.3 17.5 %collective-permute-start.19 = (bf16[96,1024]{1,0:T(8,128)(2,1)S(1)}, bf16[96,1024]{1,0:T(8,128)(2,1)S(1)}, u32[]{:S(2)}, u32[]{:S(2)}) collective-permute-start(bf16[96,1024]{1,0:T(8,128)(2,1)S(1)} %pad_maximum_fusion.37), channel_id=1, source_target_pairs={{0,4},{1,5},{2,6},{3,7},{4,0},{5,1},{6,2},{7,3},{8,12},{9,13},{10,... | collective-permute-start | bytes 589832 | tf_op jit(solution)/shard_map/ppermute | solution.py:45
  40.8 13.9 %collective-permute-start.20 = (bf16[96,1024]{1,0:T(8,128)(2,1)S(1)}, bf16[96,1024]{1,0:T(8,128)(2,1)S(1)}, u32[]{:S(2)}, u32[]{:S(2)}) collective-permute-start(bf16[96,1024]{1,0:T(8,128)(2,1)S(1)} %pad_maximum_fusion.38), channel_id=1, source_target_pairs={{0,6},{1,7},{2,4},{3,5},{4,2},{5,3},{6,0},{7,1},{8,14},{9,15},{10,... | collective-permute-start | bytes 589832 | tf_op jit(solution)/shard_map/ppermute | solution.py:45
  58.6 23.0 %collective-permute-start.21 = (bf16[384,768]{1,0:T(8,128)(2,1)S(1)}, bf16[384,768]{1,0:T(8,128)(2,1)S(1)}, u32[]{:S(2)}, u32[]{:S(2)}) collective-permute-start(bf16[384,768]{1,0:T(8,128)(2,1)S(1)} %pad_maximum_fusion.3), channel_id=1, source_target_pairs={{0,16},{1,9},{2,18},{3,11},{4,20},{5,13},{6,22},{7,15},{8,24},{9,1... | collective-permute-start | bytes 1769480 | tf_op jit(solution)/shard_map/ppermute | solution.py:45
  62.2 12.7 %collective-permute-start.9 = (bf16[192,1536]{1,0:T(8,128)(2,1)S(1)}, bf16[192,1536]{1,0:T(8,128)(2,1)S(1)}, u32[]{:S(2)}, u32[]{:S(2)}) collective-permute-start(bf16[192,1536]{1,0:T(8,128)(2,1)S(1)} %fusion.14), channel_id=1, source_target_pairs={{0,16},{1,9},{2,18},{3,11},{4,20},{5,13},{6,22},{7,15},{8,24},{9,1... | collective-permute-start | bytes 1769480 | tf_op jit(solution)/shard_map/ppermute | solution.py:45
  66.8 14.4 %collective-permute-start.10 = (bf16[192,1536]{1,0:T(8,128)(2,1)S(1)}, bf16[192,1536]{1,0:T(8,128)(2,1)S(1)}, u32[]{:S(2)}, u32[]{:S(2)}) collective-permute-start(bf16[192,1536]{1,0:T(8,128)(2,1)S(1)} %fusion.15), channel_id=1, source_target_pairs={{0,16},{1,9},{2,18},{3,11},{4,20},{5,13},{6,22},{7,15},{8,24},{9,1... | collective-permute-start | bytes 1769480 | tf_op jit(solution)/shard_map/ppermute | solution.py:45
  93.4 49.1 %collective-permute-start.30 = (bf16[2,512,768]{2,1,0:T(8,128)(2,1)S(1)}, bf16[2,512,768]{2,1,0:T(8,128)(2,1)S(1)}, u32[]{:S(2)}, u32[]{:S(2)}) collective-permute-start(bf16[2,512,768]{2,1,0:T(8,128)(2,1)S(1)} %pad_maximum_fusion), channel_id=1, source_target_pairs={{0,8},{1,17},{2,10},{3,19},{4,12},{5,21},{6,14},{7,23},{8,0},{9,25... | collective-permute-start | bytes 4718600 | tf_op jit(solution)/shard_map/ppermute | solution.py:45
  95.3 43.6 %collective-permute-start.31 = (bf16[512,768]{1,0:T(8,128)(2,1)S(1)}, bf16[512,768]{1,0:T(8,128)(2,1)S(1)}, u32[]{:S(2)}, u32[]{:S(2)}) collective-permute-start(bf16[512,768]{1,0:T(8,128)(2,1)S(1)} %convolution_convert_fusion.4), channel_id=1, source_target_pairs={{0,8},{1,17},{2,10},{3,19},{4,12},{5,21},{6,14},{7,23},{8,0},{9,25... | collective-permute-start | bytes 2359304 | tf_op jit(solution)/shard_map/ppermute | solution.py:45
  96.6 7.2 %collective-permute-start.22 = (bf16[48,1024]{1,0:T(8,128)(2,1)S(1)}, bf16[48,1024]{1,0:T(8,128)(2,1)S(1)}, u32[]{:S(2)}, u32[]{:S(2)}) collective-permute-start(bf16[48,1024]{1,0:T(8,128)(2,1)S(1)} %get-tuple-element.59), channel_id=1, source_target_pairs={{0,2},{1,3},{2,0},{3,1},{4,6},{5,7},{6,4},{7,5},{8,10},{9,11},{10,... | collective-permute-start | bytes 294920 | tf_op jit(solution)/shard_map/ppermute | solution.py:45
  99.6 6.1 %collective-permute-start.23 = (bf16[48,1024]{1,0:T(8,128)(2,1)S(1)}, bf16[48,1024]{1,0:T(8,128)(2,1)S(1)}, u32[]{:S(2)}, u32[]{:S(2)}) collective-permute-start(bf16[48,1024]{1,0:T(8,128)(2,1)S(1)} %get-tuple-element.60), channel_id=1, source_target_pairs={{0,4},{1,5},{2,6},{3,7},{4,0},{5,1},{6,2},{7,3},{8,12},{9,13},{10,... | collective-permute-start | bytes 294920 | tf_op jit(solution)/shard_map/ppermute | solution.py:45
  100.6 8.7 %collective-permute-start.24 = (bf16[48,1024]{1,0:T(8,128)(2,1)S(1)}, bf16[48,1024]{1,0:T(8,128)(2,1)S(1)}, u32[]{:S(2)}, u32[]{:S(2)}) collective-permute-start(bf16[48,1024]{1,0:T(8,128)(2,1)S(1)} %get-tuple-element.61), channel_id=1, source_target_pairs={{0,6},{1,7},{2,4},{3,5},{4,2},{5,3},{6,0},{7,1},{8,14},{9,15},{10,... | collective-permute-start | bytes 294920 | tf_op jit(solution)/shard_map/ppermute | solution.py:45
  103.8 9.5 %collective-permute-start.25 = (bf16[48,1024]{1,0:T(8,128)(2,1)S(1)}, bf16[48,1024]{1,0:T(8,128)(2,1)S(1)}, u32[]{:S(2)}, u32[]{:S(2)}) collective-permute-start(bf16[48,1024]{1,0:T(8,128)(2,1)S(1)} %get-tuple-element.64), channel_id=1, source_target_pairs={{0,2},{1,3},{2,0},{3,1},{4,6},{5,7},{6,4},{7,5},{8,10},{9,11},{10,... | collective-permute-start | bytes 294920 | tf_op jit(solution)/shard_map/ppermute | solution.py:45
  105.7 8.7 %collective-permute-start.26 = (bf16[48,1024]{1,0:T(8,128)(2,1)S(1)}, bf16[48,1024]{1,0:T(8,128)(2,1)S(1)}, u32[]{:S(2)}, u32[]{:S(2)}) collective-permute-start(bf16[48,1024]{1,0:T(8,128)(2,1)S(1)} %get-tuple-element.65), channel_id=1, source_target_pairs={{0,4},{1,5},{2,6},{3,7},{4,0},{5,1},{6,2},{7,3},{8,12},{9,13},{10,... | collective-permute-start | bytes 294920 | tf_op jit(solution)/shard_map/ppermute | solution.py:45
  109.3 8.4 %collective-permute-start.27 = (bf16[48,1024]{1,0:T(8,128)(2,1)S(1)}, bf16[48,1024]{1,0:T(8,128)(2,1)S(1)}, u32[]{:S(2)}, u32[]{:S(2)}) collective-permute-start(bf16[48,1024]{1,0:T(8,128)(2,1)S(1)} %get-tuple-element.66), channel_id=1, source_target_pairs={{0,6},{1,7},{2,4},{3,5},{4,2},{5,3},{6,0},{7,1},{8,14},{9,15},{10,... | collective-permute-start | bytes 294920 | tf_op jit(solution)/shard_map/ppermute | solution.py:45
  113.3 11.6 %collective-permute-start.11 = (bf16[96,1024]{1,0:T(8,128)(2,1)S(1)}, bf16[96,1024]{1,0:T(8,128)(2,1)S(1)}, u32[]{:S(2)}, u32[]{:S(2)}) collective-permute-start(bf16[96,1024]{1,0:T(8,128)(2,1)S(1)} %pad_maximum_fusion.32), channel_id=1, source_target_pairs={{0,2},{1,3},{2,0},{3,1},{4,6},{5,7},{6,4},{7,5},{8,10},{9,11},{10,... | collective-permute-start | bytes 589832 | tf_op jit(solution)/shard_map/ppermute | solution.py:45
  114.4 16.2 %collective-permute-start.12 = (bf16[96,1024]{1,0:T(8,128)(2,1)S(1)}, bf16[96,1024]{1,0:T(8,128)(2,1)S(1)}, u32[]{:S(2)}, u32[]{:S(2)}) collective-permute-start(bf16[96,1024]{1,0:T(8,128)(2,1)S(1)} %pad_maximum_fusion.30), channel_id=1, source_target_pairs={{0,4},{1,5},{2,6},{3,7},{4,0},{5,1},{6,2},{7,3},{8,12},{9,13},{10,... | collective-permute-start | bytes 589832 | tf_op jit(solution)/shard_map/ppermute | solution.py:45
  117.7 13.0 %collective-permute-start.13 = (bf16[96,1024]{1,0:T(8,128)(2,1)S(1)}, bf16[96,1024]{1,0:T(8,128)(2,1)S(1)}, u32[]{:S(2)}, u32[]{:S(2)}) collective-permute-start(bf16[96,1024]{1,0:T(8,128)(2,1)S(1)} %pad_maximum_fusion.31), channel_id=1, source_target_pairs={{0,6},{1,7},{2,4},{3,5},{4,2},{5,3},{6,0},{7,1},{8,14},{9,15},{10,... | collective-permute-start | bytes 589832 | tf_op jit(solution)/shard_map/ppermute | solution.py:45
  124.9 7.8 %collective-permute-start.28 = (bf16[192,1024]{1,0:T(8,128)(2,1)S(1)}, bf16[192,1024]{1,0:T(8,128)(2,1)S(1)}, u32[]{:S(2)}, u32[]{:S(2)}) collective-permute-start(bf16[192,1024]{1,0:T(8,128)(2,1)S(1)} %pad_maximum_fusion.21), channel_id=1, source_target_pairs={{0,16},{1,9},{2,18},{3,11},{4,20},{5,13},{6,22},{7,15},{8,24},{9,1... | collective-permute-start | bytes 1179656 | tf_op jit(solution)/shard_map/ppermute | solution.py:45
  130.8 7.8 %collective-permute-start.14 = (bf16[192,1024]{1,0:T(8,128)(2,1)S(1)}, bf16[192,1024]{1,0:T(8,128)(2,1)S(1)}, u32[]{:S(2)}, u32[]{:S(2)}) collective-permute-start(bf16[192,1024]{1,0:T(8,128)(2,1)S(1)} %pad_maximum_fusion.16), channel_id=1, source_target_pairs={{0,16},{1,9},{2,18},{3,11},{4,20},{5,13},{6,22},{7,15},{8,24},{9,1... | collective-permute-start | bytes 1179656 | tf_op jit(solution)/shard_map/ppermute | solution.py:45
  132.8 6.7 %collective-permute-start.29 = (bf16[96,2048]{1,0:T(8,128)(2,1)S(1)}, bf16[96,2048]{1,0:T(8,128)(2,1)S(1)}, u32[]{:S(2)}, u32[]{:S(2)}) collective-permute-start(bf16[96,2048]{1,0:T(8,128)(2,1)S(1)} %slice_dynamic-update-slice_fusion), channel_id=1, source_target_pairs={{0,1},{1,0},{2,3},{3,2},{4,5},{5,4},{6,7},{7,6},{8,9},{9,8},{10,11... | collective-permute-start | bytes 1179656 | tf_op jit(solution)/shard_map/ppermute | solution.py:45
  138.8 2.2 %collective-permute-start.15 = (bf16[96,2048]{1,0:T(8,128)(2,1)S(1)}, bf16[96,2048]{1,0:T(8,128)(2,1)S(1)}, u32[]{:S(2)}, u32[]{:S(2)}) collective-permute-start(bf16[96,2048]{1,0:T(8,128)(2,1)S(1)} %slice_dynamic-update-slice_fusion.8), channel_id=1, source_target_pairs={{0,1},{1,0},{2,3},{3,2},{4,5},{5,4},{6,7},{7,6},{8,9},{9,8},{10,11... | collective-permute-start | bytes 1179656 | tf_op jit(solution)/shard_map/ppermute | solution.py:45
  143.0 2.3 %copy-start.1 = (bf16[256,2048]{1,0:T(8,128)(2,1)S(1)}, bf16[256,2048]{1,0:T(8,128)(2,1)}, u32[]{:S(2)}) copy-start(bf16[256,2048]{1,0:T(8,128)(2,1)} %param.5) | copy-start | bytes 3145732

commit v3 on v2

--- a/solution.py
+++ b/solution.py
@@ -1,6 +1,8 @@
 import jax
 import jax.numpy as jnp
 from jax import lax
+from jax.experimental import pallas as pl
+from jax.experimental.pallas import tpu as pltpu
 from jax.sharding import PartitionSpec as P
 
 
@@ -30,6 +32,209 @@
     )
 
 
+VMEM = pl.BlockSpec(memory_space=pltpu.VMEM)
+HBM = pl.BlockSpec(memory_space=pltpu.HBM)
+PARAMS = pltpu.CompilerParams(vmem_limit_bytes=8 << 20)
+
+
+def where_am_i():
+    own_e = lax.axis_index("expert")
+    own_c = lax.rem(own_e, 2)
+    own_q = lax.axis_index("dp") * 2 + lax.axis_index("fsdp")
+    quarter = (
+        own_q,
+        jnp.bitwise_xor(own_q, 1 + own_c),
+        jnp.bitwise_xor(own_q, 2 - own_c),
+        jnp.bitwise_xor(own_q, 3),
+    )
+    return lax.div(own_e, 2), own_c, quarter
+
+
+def quarter_at(quarter, index, width):
+    return pl.ds(pl.multiple_of(quarter[index] * width, width), width)
+
+
+def write_rows(table, held, own, out, other):
+    half, width = own.shape[0], held.shape[1] // 4
+    _, _, quarter = where_am_i()
+    for index in range(4):
+        rows = jnp.dot(
+            table, held[:, quarter_at(quarter, index, width)], preferred_element_type=F32
+        ).astype(BF16)
+        low = index % 2 * width
+        (own, out)[index // 2][:, low : low + width] = rows[:half]
+        low = (0, 2, 1, 3)[index] * width
+        other[:, low : low + width] = rows[half:]
+
+
+def row_shapes(half, width):
+    return [
+        jax.ShapeDtypeStruct((half, width // 2), BF16),
+        jax.ShapeDtypeStruct((half, width // 2), BF16),
+        jax.ShapeDtypeStruct((half, width), BF16),
+    ]
+
+
+def front(ids, gates, source, steps):
+    top_count, tok_count = ids.shape
+    half, slots = steps * CAP, 2 * steps * CAP
+
+    def kernel(ids_hbm, gates_hbm, source_hbm, own, out, other, dispatch, combine, *scratch):
+        ids_ref, gates_ref, held, sem = scratch
+        fetches = [
+            pltpu.make_async_copy(ids_hbm, ids_ref, sem.at[0]),
+            pltpu.make_async_copy(gates_hbm, gates_ref, sem.at[1]),
+            pltpu.make_async_copy(source_hbm, held, sem.at[2]),
+        ]
+        for fetch in fetches:
+            fetch.start()
+        own_z, own_c, _ = where_am_i()
+        slot = lax.broadcasted_iota(jnp.int32, (slots, 1), 0)
+        expert, rank = jnp.zeros_like(slot), slot
+        for block in range(2 * steps):
+            inside = (slot >= block * CAP) & (slot < (block + 1) * CAP)
+            number = jnp.bitwise_xor(block % steps, own_z) * 2
+            number = number + jnp.bitwise_xor(block // steps, own_c)
+            expert = jnp.where(inside, number, expert)
+            rank = jnp.where(inside, slot - block * CAP, rank)
+        row = lax.broadcasted_iota(jnp.int32, (tok_count, tok_count), 0)
+        col = lax.broadcasted_iota(jnp.int32, (tok_count, tok_count), 1)
+        earlier = jnp.where(row < col, 1.0, 0.0).astype(BF16)
+        named = jnp.zeros((slots, tok_count), F32)
+        value = jnp.zeros((slots, tok_count), F32)
+        fetches[0].wait()
+        fetches[1].wait()
+        for k in range(top_count):
+            hit = ids_ref[k : k + 1, :] == expert
+            named = jnp.where(hit, 1.0, named)
+            value = jnp.where(hit, gates_ref[k : k + 1, :].astype(F32), value)
+        before = jnp.dot(named.astype(BF16), earlier, preferred_element_type=F32)
+        chosen = (named > 0.5) & (before == rank.astype(F32))
+        table = jnp.where(chosen, 1.0, 0.0).astype(BF16)
+        dispatch[...] = table
+        combine[...] = jnp.where(chosen, value * (1.0 / 256.0), 0.0).astype(BF16)
+        fetches[2].wait()
+        write_rows(table, held, own, out, other)
+
+    tables = [jax.ShapeDtypeStruct((slots, tok_count), BF16)] * 2
+    return pl.pallas_call(
+        kernel,
+        out_shape=(*row_shapes(half, source.shape[1]), *tables),
+        in_specs=[HBM] * 3,
+        out_specs=(VMEM,) * 5,
+        scratch_shapes=[
+            pltpu.VMEM(ids.shape, jnp.int32),
+            pltpu.VMEM(gates.shape, jnp.int32),
+            pltpu.VMEM(source.shape, BF16),
+            pltpu.SemaphoreType.DMA((3,)),
+        ],
+        compiler_params=PARAMS,
+        name="front",
+    )(ids, gates, source)
+
+
+def local_rows(table, source):
+    def kernel(table_ref, source_ref, own, out, other):
+        write_rows(table_ref[...], source_ref, own, out, other)
+
+    return pl.pallas_call(
+        kernel,
+        out_shape=row_shapes(table.shape[0] // 2, source.shape[1]),
+        in_specs=[VMEM] * 2,
+        out_specs=(VMEM,) * 3,
+        compiler_params=PARAMS,
+        name="local_rows",
+    )(table, source)
+
+
+def split_weights(weights):
+    parts, depth, hidden = weights.shape
+
+    def kernel(source, gates, down, sem):
+        copies = [
+            pltpu.make_async_copy(source.at[pl.ds(0, parts - 1)], gates, sem.at[0]),
+            pltpu.make_async_copy(source.at[parts - 1], down, sem.at[1]),
+        ]
+        for copy in copies:
+            copy.start()
+        for copy in copies:
+            copy.wait()
+
+    return pl.pallas_call(
+        kernel,
+        out_shape=(
+            jax.ShapeDtypeStruct((parts - 1, depth, hidden), weights.dtype),
+            jax.ShapeDtypeStruct((depth, hidden), weights.dtype),
+        ),
+        in_specs=[HBM],
+        out_specs=(VMEM,) * 2,
+        scratch_shapes=[pltpu.SemaphoreType.DMA((2,))],
+        compiler_params=PARAMS,
+        name="split_weights",
+    )(weights)
+
+
+def weight_terms(rows, grads, arrived, down):
+    parts, depth, hidden = arrived.shape
+
+    def kernel(rows_ref, gate_ref, up_ref, arrived_ref, down_ref, answer, held, sem):
+        writes = [pltpu.make_async_copy(down_ref, answer.at[parts], sem.at[parts])]
+        writes[0].start()
+        for part, grad in enumerate((gate_ref, up_ref)):
+            term = contract(rows_ref[:, :depth], grad[...], 0, 0)
+            held[part] = (term + arrived_ref[part].astype(F32)).astype(BF16)
+            writes.append(pltpu.make_async_copy(held.at[part], answer.at[part], sem.at[part]))
+            writes[-1].start()
+        for write in writes:
+            write.wait()
+
+    return pl.pallas_call(
+        kernel,
+        out_shape=jax.ShapeDtypeStruct((parts + 1, depth, hidden), BF16),
+        in_specs=[VMEM] * 5,
+        out_specs=HBM,
+        scratch_shapes=[
+            pltpu.VMEM(arrived.shape, BF16),
+            pltpu.SemaphoreType.DMA((parts + 1,)),
+        ],
+        compiler_params=PARAMS,
+        name="weight_terms",
+    )(rows, *grads, arrived, down)
+
+
+def fold(table, own, out, came):
+    tok_count, width = table.shape[1], came.shape[1] // 4
+
+    def kernel(table_ref, own_ref, out_ref, came_ref, answer, held, sem):
+        _, _, quarter = where_am_i()
+        writes = []
+        for index in range(4):
+            low = index % 2 * width
+            first = (own_ref, out_ref)[index // 2][:, low : low + width]
+            rows = jnp.concatenate([first, came_ref[:, index * width : (index + 1) * width]])
+            held[index] = contract(table_ref[...], rows, 0, 0).astype(BF16)
+            writes.append(
+                pltpu.make_async_copy(
+                    held.at[index],
+                    answer.at[:, quarter_at(quarter, index, width)],
+                    sem.at[index],
+                )
+            )
+            writes[-1].start()
+        for write in writes:
+            write.wait()
+
+    return pl.pallas_call(
+        kernel,
+        out_shape=jax.ShapeDtypeStruct((tok_count, came.shape[1]), BF16),
+        in_specs=[VMEM] * 4,
+        out_specs=HBM,
+        scratch_shapes=[pltpu.VMEM((4, tok_count, width), BF16), pltpu.SemaphoreType.DMA((4,))],
+        compiler_params=PARAMS,
+        name="fold",
+    )(table, own, out, came)
+
+
 class Moves:
     def __init__(self, dp, fsdp, experts):
         self.shape = (dp, fsdp, experts)
@@ -72,50 +277,26 @@
     quarter_width = model_width // 4
     half_width = model_width // 2
     hidden = expert_weights.shape[3]
-    own_e = lax.axis_index("expert")
-    own_z, own_c = own_e // 2, own_e % 2
-    own_q = lax.axis_index("dp") * 2 + lax.axis_index("fsdp")
-    quarter = (own_q, own_q ^ (1 + own_c), own_q ^ (2 - own_c), own_q ^ 3)
     half = steps * CAP
 
-    weights_own = expert_weights[0]
-    weights_far = moves.weight_pair(weights_own)
-    pair = (weights_own, weights_far)
-
-    slot = jnp.arange(2 * half, dtype=jnp.int32)
-    slot_expert = ((slot % half // CAP) ^ own_z) * 2 + ((slot // half) ^ own_c)
-    dispatch, combine = route_tables(expert_ids, gate_units, slot_expert, slot % CAP)
+    gates_own, down_own = split_weights(jnp.transpose(expert_weights[0], (1, 0, 2)))
+    gates_far = moves.weight_pair(gates_own)
+    pair = (
+        (gates_own[0], gates_own[1], down_own),
+        (gates_far[0], gates_far[1], moves.weight_pair(down_own)),
+    )
+
+    *token_parts, dispatch, combine = front(expert_ids.T, gate_units.T, tokens, steps)
 
     def interleaved(first, second):
         width = first.shape[1]
         both = (first.reshape(steps, CAP, width), second.reshape(steps, CAP, width))
         return jnp.stack(both, axis=1).reshape(2 * half, width)
 
-    def taken(array, *which):
-        return jnp.concatenate(
-            [
-                lax.dynamic_slice_in_dim(array, quarter[i] * quarter_width, quarter_width, 1)
-                for i in which
-            ],
-            axis=1,
-        )
-
-    def placed(own, out):
-        whole = jnp.zeros((own.shape[0], model_width), BF16)
-        for index in range(4):
-            part = (own, out)[index // 2]
-            low = index % 2 * quarter_width
-            whole = lax.dynamic_update_slice_in_dim(
-                whole, part[:, low : low + quarter_width], quarter[index] * quarter_width, 1
-            )
-        return whole
-
-    def send_local(table, source):
-        both = contract(table, source, 0, 0).astype(BF16)
-        same = both[:half]
-        came = moves.core(both[half:])
-        own = interleaved(taken(same, 0, 1), taken(came, 0, 1))
-        out = interleaved(taken(same, 2, 3), taken(came, 2, 3))
+    def send_local(own, out, other):
+        came = moves.core(other)
+        own = interleaved(own, came[:, :half_width])
+        out = interleaved(out, came[:, half_width:])
         return own, moves.column_pair(out)
 
     def by_z(rows):
@@ -142,14 +323,18 @@
         def source(array, index):
             return array.reshape(steps, 2, CAP, half_width)[:, index].reshape(half, half_width)
 
-        came = moves.core(placed(source(own, 1), source(out, 1)))
-        rows = jnp.concatenate([placed(source(own, 0), source(out, 0)), came])
-        return contract(table, rows, 1, 0).astype(BF16)
+        parts = [
+            side[:, i * quarter_width : (i + 1) * quarter_width]
+            for i in (0, 1)
+            for side in (source(own, 1), source(out, 1))
+        ]
+        came = moves.core(jnp.concatenate(parts, axis=1))
+        return fold(table, source(own, 0), source(out, 0), came)
 
     def inward(rows, which, sides=(0, 1)):
         return sum(
             contract(
-                rows[:, i * quarter_width : (i + 1) * quarter_width], pair[i][:, which], 1, 0
+                rows[:, i * quarter_width : (i + 1) * quarter_width], pair[i][which], 1, 0
             )
             for i in sides
         )
@@ -157,7 +342,7 @@
     def outward(terms):
         return jnp.concatenate(
             [
-                sum(contract(value, pair[i][:, which], 1, 1) for value, which in terms)
+                sum(contract(value, pair[i][which], 1, 1) for value, which in terms)
                 for i in (0, 1)
             ],
             axis=1,
@@ -170,10 +355,11 @@
         both = [value + inward(rows, i, (1,)) for i, value in enumerate(start)]
         return jnp.concatenate(both, axis=1)
 
-    rows_own, rows_near = send_local(dispatch, tokens)
+    rows_own, rows_near = send_local(*token_parts)
     (rows_own,) = by_z([rows_own])
     (rows_near,) = by_z([rows_near])
-    scaled_own, scaled_near = by_z(send_local(combine, out_grad))
+    grad_parts = local_rows(combine, out_grad)
+    scaled_own, scaled_near = by_z(send_local(*grad_parts))
 
     base_own = base(rows_own)
     base_near = base(rows_near)
@@ -196,7 +382,8 @@
     out_near = outward([(act_near, 2)])
     act_own, slope_own, swish_own = act(part_own, own_extra)
     out_own = outward([(act_own, 2)])
-    back_near, back_own = by_z([out_near, out_own])
+    (back_near,) = by_z([out_near])
+    (back_own,) = by_z([out_own])
 
     hid_own, hid_near = inward(scaled_own, 2), inward(scaled_near, 2)
     message = jnp.concatenate([hid_near, hid_own]).astype(BF16)
@@ -226,12 +413,8 @@
     token_grad = give_back_in(dispatch, grad_own, grad_near)
     term_down = contract(scaled[:, first], activation, 0, 0) + arrived_down.astype(F32)
     term_down = term_down.astype(BF16)
-    terms = [
-        contract(rows[:, first], value, 0, 0) + arrived_in[i].astype(F32)
-        for i, value in enumerate((gate_grad, up_grad))
-    ]
-    weight_grad = jnp.stack([*(term.astype(BF16) for term in terms), term_down], axis=1)
-    return moe_out, token_grad, weight_grad[None]
+    weight_grad = weight_terms(rows, (gate_grad, up_grad), arrived_in, term_down)
+    return moe_out, token_grad, jnp.transpose(weight_grad, (1, 0, 2))[None]
 
 
 def gathered(tokens, expert_ids, gate_units, expert_weights, out_grad):

time: 148 us -> 161 us (1.088); the launches traced: 145 us -> 160 us
  waiting for transfers between devices: 56.9 us -> 79.4 us
  matrix products: 29.9 us -> 11.2 us
  starting transfers between devices: 45.6 us -> 55.1 us
  Pallas kernels: 0 us -> 5.81 us
  other arithmetic: 5.82 us -> 2.28 us
    ppermute x32 -> x36, waiting for transfers between devices: 56.9 us -> 79.4 us  [move(): return lax.ppermute(value, ALL, pairs)]
    dot_general x34 -> x28, matrix products: 29.7 us -> 11.2 us  [contract(): lax.dot_general(left, right, (((left_dim,), (right_dim,)), ((), ())), pre...]
    ppermute x32 -> x36, starting transfers between devices: 45.6 us -> 55.1 us  [move(): return lax.ppermute(value, ALL, pairs)]
    pallas_call x0 -> x6, Pallas kernels: none -> 5.81 us  [the longest x2 2.55 us: fold(): pl.pallas_call(kernel, out_shape=jax.ShapeDtypeStruct((tok_count, came.sh...]
    unnamed x23 -> x25, local copies, waits for them, and re-layouts: 0.78 us -> 4.46 us
    dynamic_slice x4 -> x0, local copies, waits for them, and re-layouts: 2.22 us -> none  [taken(): lax.dynamic_slice_in_dim(array, quarter[i] * quarter_width, quarter_width...]
    broadcast_in_dim x1 -> x0, other arithmetic: 1.66 us -> none  [paired_body(): return (moe_out, token_grad, weight_grad[None])]
  transfers between devices with their start and end apart: 32 -> 36, of which waited for: 15 -> 17; matrix products, arithmetic and copies ran while one was open for 13% -> 7% of each run, Pallas kernels for 0% -> 2%
where the time goes in v3:
time: 161 us; the launch traced here: 160 us
  waiting for transfers between devices  79.4 us (49%)
  starting transfers between devices  55.1 us (34%)
  matrix products  11.2 us (7%)
  Pallas kernels  5.81 us (4%)
  local copies, waits for them, and re-layouts  4.91 us (3%)
  other arithmetic  2.28 us (1%)
  between operations  1.63 us (1%)
    ppermute x36, waiting for transfers between devices, move(): return lax.ppermute(value, ALL, pairs)  79.4 us
    ppermute x36, starting transfers between devices, move(): return lax.ppermute(value, ALL, pairs)  55.1 us
    dot_general x28, matrix products, contract(): lax.dot_general(left, right, (((left_dim,), (right_dim,)), ((), ())), pre...  11.2 us
    unnamed x25, local copies, waits for them, and re-layouts  4.46 us
  transfers between devices with their start and end apart: 36, of which 17 were waited for; matrix products, arithmetic and copies ran while one was open for 7% of the time, Pallas kernels for 2%

profile of v3, /device:TPU:0, one launch (start us, length us, event | category | flops | bytes accessed | tf_op | source)
XLA Modules:
  0.0 160.4 jit_solution(15675484582912865940)
XLA Ops:
  0.6 1.2 copy-done.1
  1.9 0.7 copy-done.3
  2.6 0.7 copy-done.4
  3.3 0.7 front.1
  4.0 0.6 collective-permute-start
  4.5 1.7 %copy-done = bf16[1,512,3,768]{3,1,2,0:T(8,128)(2,1)S(1)} copy-done((bf16[1,512,3,768]{3,1,2,0:T(8,128)(2,1)S(1)}, bf16[1,512,3,768]{3,1,2,0:T(8,128)(2,1)}, u32[]{:S(2)}) %copy-start) | copy-done | bytes 2359320
  6.4 2.6 %collective-permute-start.4 = (bf16[2,512,768]{2,1,0:T(8,128)(2,1)S(1)}, bf16[2,512,768]{2,1,0:T(8,128)(2,1)S(1)}, u32[]{:S(2)}, u32[]{:S(2)}) collective-permute-start(bf16[2,512,768]{2,1,0:T(8,128)(2,1)S(1)} %get-tuple-element.52), channel_id=1, source_target_pairs={{0,8},{1,17},{2,10},{3,19},{4,12},{5,21},{6,14},{7,23},{8,0},{9,25... | collective-permute-start | bytes 4718600 | tf_op jit(solution)/shard_map/ppermute | solution.py:250
  9.8 1.4 collective-permute-done.20
  11.4 2.1 %collective-permute-start.1 = (bf16[48,1024]{1,0:T(8,128)(2,1)S(1)}, bf16[48,1024]{1,0:T(8,128)(2,1)S(1)}, u32[]{:S(2)}, u32[]{:S(2)}) collective-permute-start(bf16[48,1024]{1,0:T(8,128)(2,1)S(1)} %get-tuple-element.49), channel_id=1, source_target_pairs={{0,2},{1,3},{2,0},{3,1},{4,6},{5,7},{6,4},{7,5},{8,10},{9,11},{10,... | collective-permute-start | bytes 294920 | tf_op jit(solution)/shard_map/ppermute | solution.py:250
  13.5 2.6 %collective-permute-start.2 = (bf16[48,1024]{1,0:T(8,128)(2,1)S(1)}, bf16[48,1024]{1,0:T(8,128)(2,1)S(1)}, u32[]{:S(2)}, u32[]{:S(2)}) collective-permute-start(bf16[48,1024]{1,0:T(8,128)(2,1)S(1)} %get-tuple-element.50), channel_id=1, source_target_pairs={{0,4},{1,5},{2,6},{3,7},{4,0},{5,1},{6,2},{7,3},{8,12},{9,13},{10,... | collective-permute-start | bytes 294920 | tf_op jit(solution)/shard_map/ppermute | solution.py:250
  16.2 0.4 collective-permute-done.1
  16.6 1.7 %collective-permute-start.5 = (bf16[192,1024]{1,0:T(8,128)(2,1)S(1)}, bf16[192,1024]{1,0:T(8,128)(2,1)S(1)}, u32[]{:S(2)}, u32[]{:S(2)}) collective-permute-start(bf16[192,1024]{1,0:T(8,128)(2,1)S(1)} %bitcast.156), channel_id=1, source_target_pairs={{0,16},{1,9},{2,18},{3,11},{4,20},{5,13},{6,22},{7,15},{8,24},{9,1... | collective-permute-start | bytes 1179656 | tf_op jit(solution)/shard_map/ppermute | solution.py:250
  18.2 5.9 %collective-permute-done.2 = bf16[48,1024]{1,0:T(8,128)(2,1)S(1)} collective-permute-done((bf16[48,1024]{1,0:T(8,128)(2,1)S(1)}, bf16[48,1024]{1,0:T(8,128)(2,1)S(1)}, u32[]{:S(2)}, u32[]{:S(2)}) %collective-permute-start.2) | collective-permute-done | bytes 98336 | tf_op jit(solution)/shard_map/ppermute | solution.py:250
  24.2 1.5 collective-permute-start.21
  26.4 2.2 %collective-permute-done.5 = bf16[192,1024]{1,0:T(8,128)(2,1)S(1)} collective-permute-done((bf16[192,1024]{1,0:T(8,128)(2,1)S(1)}, bf16[192,1024]{1,0:T(8,128)(2,1)S(1)}, u32[]{:S(2)}, u32[]{:S(2)}) %collective-permute-start.5) | collective-permute-done | bytes 393248 | tf_op jit(solution)/shard_map/ppermute | solution.py:250
  28.6 4.9 %collective-permute-start.8 = (bf16[48,1024]{1,0:T(8,128)(2,1)S(1)}, bf16[48,1024]{1,0:T(8,128)(2,1)S(1)}, u32[]{:S(2)}, u32[]{:S(2)}) collective-permute-start(bf16[48,1024]{1,0:T(8,128)(2,1)S(1)} %get-tuple-element.58), channel_id=1, source_target_pairs={{0,6},{1,7},{2,4},{3,5},{4,2},{5,3},{6,0},{7,1},{8,14},{9,15},{10,... | collective-permute-start | bytes 294920 | tf_op jit(solution)/shard_map/ppermute | solution.py:250
  33.5 3.5 %collective-permute-done.21 = bf16[192,1024]{1,0:T(8,128)(2,1)S(1)} collective-permute-done((bf16[192,1024]{1,0:T(8,128)(2,1)S(1)}, bf16[192,1024]{1,0:T(8,128)(2,1)S(1)}, u32[]{:S(2)}, u32[]{:S(2)}) %collective-permute-start.21) | collective-permute-done | bytes 393248 | tf_op jit(solution)/shard_map/ppermute | solution.py:250
  37.0 1.7 %collective-permute-start.6 = (bf16[48,1024]{1,0:T(8,128)(2,1)S(1)}, bf16[48,1024]{1,0:T(8,128)(2,1)S(1)}, u32[]{:S(2)}, u32[]{:S(2)}) collective-permute-start(bf16[48,1024]{1,0:T(8,128)(2,1)S(1)} %get-tuple-element.56), channel_id=1, source_target_pairs={{0,2},{1,3},{2,0},{3,1},{4,6},{5,7},{6,4},{7,5},{8,10},{9,11},{10,... | collective-permute-start | bytes 294920 | tf_op jit(solution)/shard_map/ppermute | solution.py:250
  38.9 0.6 collective-permute-start.22
  39.5 0.7 collective-permute-done.7
  40.2 2.6 %collective-permute-start.23 = (bf16[96,1024]{1,0:T(8,128)(2,1)S(1)}, bf16[96,1024]{1,0:T(8,128)(2,1)S(1)}, u32[]{:S(2)}, u32[]{:S(2)}) collective-permute-start(bf16[96,1024]{1,0:T(8,128)(2,1)S(1)} %pad_maximum_fusion.24), channel_id=1, source_target_pairs={{0,4},{1,5},{2,6},{3,7},{4,0},{5,1},{6,2},{7,3},{8,12},{9,13},{10,... | collective-permute-start | bytes 589832 | tf_op jit(solution)/shard_map/ppermute | solution.py:250
  42.8 5.9 %collective-permute-start.24 = (bf16[96,1024]{1,0:T(8,128)(2,1)S(1)}, bf16[96,1024]{1,0:T(8,128)(2,1)S(1)}, u32[]{:S(2)}, u32[]{:S(2)}) collective-permute-start(bf16[96,1024]{1,0:T(8,128)(2,1)S(1)} %pad_maximum_fusion.25), channel_id=1, source_target_pairs={{0,6},{1,7},{2,4},{3,5},{4,2},{5,3},{6,0},{7,1},{8,14},{9,15},{10,... | collective-permute-start | bytes 589832 | tf_op jit(solution)/shard_map/ppermute | solution.py:250
  49.4 0.5 collective-permute-done.22
  49.9 7.4 %collective-permute-done.23 = bf16[96,1024]{1,0:T(8,128)(2,1)S(1)} collective-permute-done((bf16[96,1024]{1,0:T(8,128)(2,1)S(1)}, bf16[96,1024]{1,0:T(8,128)(2,1)S(1)}, u32[]{:S(2)}, u32[]{:S(2)}) %collective-permute-start.23) | collective-permute-done | bytes 196640 | tf_op jit(solution)/shard_map/ppermute | solution.py:250
  58.9 1.6 collective-permute-start.25
  61.2 0.6 collective-permute-start.9
  62.5 1.6 collective-permute-start.14
  64.1 11.1 %collective-permute-done.9 = bf16[192,1536]{1,0:T(8,128)(2,1)S(1)} collective-permute-done((bf16[192,1536]{1,0:T(8,128)(2,1)S(1)}, bf16[192,1536]{1,0:T(8,128)(2,1)S(1)}, u32[]{:S(2)}, u32[]{:S(2)}) %collective-permute-start.9) | collective-permute-done | bytes 589856 | tf_op jit(solution)/shard_map/ppermute | solution.py:250
  75.6 0.4 convolution_convert_fusion.6
  76.1 5.5 %collective-permute-done.14 = bf16[192,1536]{1,0:T(8,128)(2,1)S(1)} collective-permute-done((bf16[192,1536]{1,0:T(8,128)(2,1)S(1)}, bf16[192,1536]{1,0:T(8,128)(2,1)S(1)}, u32[]{:S(2)}, u32[]{:S(2)}) %collective-permute-start.14) | collective-permute-done | bytes 589856 | tf_op jit(solution)/shard_map/ppermute | solution.py:250
  82.0 0.4 convolution_convert_fusion.4
  82.4 0.4 convolution_convert_fusion.5
  82.8 0.4 convolution_convert_fusion.3
  83.7 0.4 fusion.16
  84.1 0.4 fusion.2
  84.9 0.4 fusion.3
  85.9 2.3 %collective-permute-start.13 = (bf16[48,1024]{1,0:T(8,128)(2,1)S(1)}, bf16[48,1024]{1,0:T(8,128)(2,1)S(1)}, u32[]{:S(2)}, u32[]{:S(2)}) collective-permute-start(bf16[48,1024]{1,0:T(8,128)(2,1)S(1)} %get-tuple-element.65), channel_id=1, source_target_pairs={{0,6},{1,7},{2,4},{3,5},{4,2},{5,3},{6,0},{7,1},{8,14},{9,15},{10,... | collective-permute-start | bytes 294920 | tf_op jit(solution)/shard_map/ppermute | solution.py:250
  88.2 2.1 %collective-permute-start.12 = (bf16[48,1024]{1,0:T(8,128)(2,1)S(1)}, bf16[48,1024]{1,0:T(8,128)(2,1)S(1)}, u32[]{:S(2)}, u32[]{:S(2)}) collective-permute-start(bf16[48,1024]{1,0:T(8,128)(2,1)S(1)} %get-tuple-element.64), channel_id=1, source_target_pairs={{0,4},{1,5},{2,6},{3,7},{4,0},{5,1},{6,2},{7,3},{8,12},{9,13},{10,... | collective-permute-start | bytes 294920 | tf_op jit(solution)/shard_map/ppermute | solution.py:250
  90.4 2.6 %collective-permute-start.28 = (bf16[48,1024]{1,0:T(8,128)(2,1)S(1)}, bf16[48,1024]{1,0:T(8,128)(2,1)S(1)}, u32[]{:S(2)}, u32[]{:S(2)}) collective-permute-start(bf16[48,1024]{1,0:T(8,128)(2,1)S(1)} %get-tuple-element.83), channel_id=1, source_target_pairs={{0,6},{1,7},{2,4},{3,5},{4,2},{5,3},{6,0},{7,1},{8,14},{9,15},{10,... | collective-permute-start | bytes 294920 | tf_op jit(solution)/shard_map/ppermute | solution.py:250
  93.0 1.9 %collective-permute-start.26 = (bf16[48,1024]{1,0:T(8,128)(2,1)S(1)}, bf16[48,1024]{1,0:T(8,128)(2,1)S(1)}, u32[]{:S(2)}, u32[]{:S(2)}) collective-permute-start(bf16[48,1024]{1,0:T(8,128)(2,1)S(1)} %get-tuple-element.81), channel_id=1, source_target_pairs={{0,2},{1,3},{2,0},{3,1},{4,6},{5,7},{6,4},{7,5},{8,10},{9,11},{10,... | collective-permute-start | bytes 294920 | tf_op jit(solution)/shard_map/ppermute | solution.py:250
  94.9 0.6 fusion
  95.5 0.6 fusion.1
  96.1 0.4 fusion.4
  96.5 0.4 fusion.24
  96.9 0.4 fusion.5
  97.6 0.6 convolution_convert_fusion
  98.5 2.4 %collective-permute-start.17 = (bf16[48,1024]{1,0:T(8,128)(2,1)S(1)}, bf16[48,1024]{1,0:T(8,128)(2,1)S(1)}, u32[]{:S(2)}, u32[]{:S(2)}) collective-permute-start(bf16[48,1024]{1,0:T(8,128)(2,1)S(1)} %get-tuple-element.69), channel_id=1, source_target_pairs={{0,6},{1,7},{2,4},{3,5},{4,2},{5,3},{6,0},{7,1},{8,14},{9,15},{10,... | collective-permute-start | bytes 294920 | tf_op jit(solution)/shard_map/ppermute | solution.py:250
  100.8 7.1 %collective-permute-done.27 = bf16[48,1024]{1,0:T(8,128)(2,1)S(1)} collective-permute-done((bf16[48,1024]{1,0:T(8,128)(2,1)S(1)}, bf16[48,1024]{1,0:T(8,128)(2,1)S(1)}, u32[]{:S(2)}, u32[]{:S(2)}) %collective-permute-start.27) | collective-permute-done | bytes 98336 | tf_op jit(solution)/shard_map/ppermute | solution.py:250
  107.9 0.6 collective-permute-start.16
  108.5 3.5 %collective-permute-start.15 = (bf16[48,1024]{1,0:T(8,128)(2,1)S(1)}, bf16[48,1024]{1,0:T(8,128)(2,1)S(1)}, u32[]{:S(2)}, u32[]{:S(2)}) collective-permute-start(bf16[48,1024]{1,0:T(8,128)(2,1)S(1)} %get-tuple-element.67), channel_id=1, source_target_pairs={{0,2},{1,3},{2,0},{3,1},{4,6},{5,7},{6,4},{7,5},{8,10},{9,11},{10,... | collective-permute-start | bytes 294920 | tf_op jit(solution)/shard_map/ppermute | solution.py:250
  112.5 5.0 %collective-permute-done.16 = bf16[48,1024]{1,0:T(8,128)(2,1)S(1)} collective-permute-done((bf16[48,1024]{1,0:T(8,128)(2,1)S(1)}, bf16[48,1024]{1,0:T(8,128)(2,1)S(1)}, u32[]{:S(2)}, u32[]{:S(2)}) %collective-permute-start.16) | collective-permute-done | bytes 98336 | tf_op jit(solution)/shard_map/ppermute | solution.py:250
  117.5 4.3 %collective-permute-start.29 = (bf16[48,1024]{1,0:T(8,128)(2,1)S(1)}, bf16[48,1024]{1,0:T(8,128)(2,1)S(1)}, u32[]{:S(2)}, u32[]{:S(2)}) collective-permute-start(bf16[48,1024]{1,0:T(8,128)(2,1)S(1)} %get-tuple-element.86), channel_id=1, source_target_pairs={{0,2},{1,3},{2,0},{3,1},{4,6},{5,7},{6,4},{7,5},{8,10},{9,11},{10,... | collective-permute-start | bytes 294920 | tf_op jit(solution)/shard_map/ppermute | solution.py:250
  121.9 2.3 %collective-permute-done.30 = bf16[48,1024]{1,0:T(8,128)(2,1)S(1)} collective-permute-done((bf16[48,1024]{1,0:T(8,128)(2,1)S(1)}, bf16[48,1024]{1,0:T(8,128)(2,1)S(1)}, u32[]{:S(2)}, u32[]{:S(2)}) %collective-permute-start.30) | collective-permute-done | bytes 98336 | tf_op jit(solution)/shard_map/ppermute | solution.py:250
  124.2 1.5 collective-permute-start.34
  125.7 1.5 collective-permute-start.18
  127.3 0.5 collective-permute-start.35
  127.8 0.5 collective-permute-start.32
  128.4 9.3 %collective-permute-done.18 = bf16[192,1024]{1,0:T(8,128)(2,1)S(1)} collective-permute-done((bf16[192,1024]{1,0:T(8,128)(2,1)S(1)}, bf16[192,1024]{1,0:T(8,128)(2,1)S(1)}, u32[]{:S(2)}, u32[]{:S(2)}) %collective-permute-start.18) | collective-permute-done | bytes 393248 | tf_op jit(solution)/shard_map/ppermute | solution.py:250
  137.9 8.2 %collective-permute-done.32 = bf16[192,1024]{1,0:T(8,128)(2,1)S(1)} collective-permute-done((bf16[192,1024]{1,0:T(8,128)(2,1)S(1)}, bf16[192,1024]{1,0:T(8,128)(2,1)S(1)}, u32[]{:S(2)}, u32[]{:S(2)}) %collective-permute-start.32) | collective-permute-done | bytes 393248 | tf_op jit(solution)/shard_map/ppermute | solution.py:250
  146.3 8.7 %collective-permute-done.35 = bf16[512,768]{1,0:T(8,128)(2,1)S(1)} collective-permute-done((bf16[512,768]{1,0:T(8,128)(2,1)S(1)}, bf16[512,768]{1,0:T(8,128)(2,1)S(1)}, u32[]{:S(2)}, u32[]{:S(2)}) %collective-permute-start.35) | collective-permute-done | bytes 786464 | tf_op jit(solution)/shard_map/ppermute | solution.py:250
  155.1 0.6 add_convert_fusion.down_ref
  155.7 1.3 fold.2
  157.0 1.3 fold.3
  158.3 2.0 %weight_terms.1 = bf16[3,512,768]{2,1,0:T(8,128)(2,1)} custom-call(bf16[384,1024]{1,0:T(8,128)(2,1)S(1)} %constant_dynamic-update-slice_fusion.rows_ref, bf16[384,768]{1,0:T(8,128)(2,1)S(1)} %pad_maximum_fusion.4.gate_ref, bf16[384,768]{1,0:T(8,128)(2,1)S(1)} %pad_maximum_fusion.5.up_ref, bf16[2,512,768]{2,1,0:T(8,128)(2,1)S(1)} %collective-permute-done.34.arrived_ref, ...), custom_call_target="tpu_custom_call" | custom-call | tf_op jit(solution)/shard_map/weight_terms/pallas_call | solution.py:191
  (124 shorter events, 9.4 us)
Async XLA Ops:
  0.6 1.2 copy-start.1
  1.9 0.7 copy-start.3
  2.6 0.7 copy-start.4
  3.3 5.8 %copy-start.2 = (bf16[256,2048]{1,0:T(8,128)(2,1)S(1)}, bf16[256,2048]{1,0:T(8,128)(2,1)}, u32[]{:S(2)}) copy-start(bf16[256,2048]{1,0:T(8,128)(2,1)} %source_ref.1) | copy-start | bytes 3145732
  4.0 5.7 %collective-permute-start = (bf16[96,2048]{1,0:T(8,128)(2,1)S(1)}, bf16[96,2048]{1,0:T(8,128)(2,1)S(1)}, u32[]{:S(2)}, u32[]{:S(2)}) collective-permute-start(bf16[96,2048]{1,0:T(8,128)(2,1)S(1)} %get-tuple-element.48), channel_id=1, source_target_pairs={{0,1},{1,0},{2,3},{3,2},{4,5},{5,4},{6,7},{7,6},{8,9},{9,8},{10,11... | collective-permute-start | bytes 1179656 | tf_op jit(solution)/shard_map/ppermute | solution.py:250
  4.5 1.7 %copy-start = (bf16[1,512,3,768]{3,1,2,0:T(8,128)(2,1)S(1)}, bf16[1,512,3,768]{3,1,2,0:T(8,128)(2,1)}, u32[]{:S(2)}) copy-start(bf16[1,512,3,768]{3,1,2,0:T(8,128)(2,1)} %param.8) | copy-start | bytes 7077892
  6.4 54.1 %collective-permute-start.4 = (bf16[2,512,768]{2,1,0:T(8,128)(2,1)S(1)}, bf16[2,512,768]{2,1,0:T(8,128)(2,1)S(1)}, u32[]{:S(2)}, u32[]{:S(2)}) collective-permute-start(bf16[2,512,768]{2,1,0:T(8,128)(2,1)S(1)} %get-tuple-element.52), channel_id=1, source_target_pairs={{0,8},{1,17},{2,10},{3,19},{4,12},{5,21},{6,14},{7,23},{8,0},{9,25... | collective-permute-start | bytes 4718600 | tf_op jit(solution)/shard_map/ppermute | solution.py:250
  9.0 48.6 %collective-permute-start.10 = (bf16[512,768]{1,0:T(8,128)(2,1)S(1)}, bf16[512,768]{1,0:T(8,128)(2,1)S(1)}, u32[]{:S(2)}, u32[]{:S(2)}) collective-permute-start(bf16[512,768]{1,0:T(8,128)(2,1)S(1)} %get-tuple-element.62), channel_id=1, source_target_pairs={{0,8},{1,17},{2,10},{3,19},{4,12},{5,21},{6,14},{7,23},{8,0},{9,25... | collective-permute-start | bytes 2359304 | tf_op jit(solution)/shard_map/ppermute | solution.py:250
  9.4 1.8 %collective-permute-start.20 = (bf16[96,2048]{1,0:T(8,128)(2,1)S(1)}, bf16[96,2048]{1,0:T(8,128)(2,1)S(1)}, u32[]{:S(2)}, u32[]{:S(2)}) collective-permute-start(bf16[96,2048]{1,0:T(8,128)(2,1)S(1)} %get-tuple-element.72), channel_id=1, source_target_pairs={{0,1},{1,0},{2,3},{3,2},{4,5},{5,4},{6,7},{7,6},{8,9},{9,8},{10,11... | collective-permute-start | bytes 1179656 | tf_op jit(solution)/shard_map/ppermute | solution.py:250
  11.4 5.2 %collective-permute-start.1 = (bf16[48,1024]{1,0:T(8,128)(2,1)S(1)}, bf16[48,1024]{1,0:T(8,128)(2,1)S(1)}, u32[]{:S(2)}, u32[]{:S(2)}) collective-permute-start(bf16[48,1024]{1,0:T(8,128)(2,1)S(1)} %get-tuple-element.49), channel_id=1, source_target_pairs={{0,2},{1,3},{2,0},{3,1},{4,6},{5,7},{6,4},{7,5},{8,10},{9,11},{10,... | collective-permute-start | bytes 294920 | tf_op jit(solution)/shard_map/ppermute | solution.py:250
  13.5 10.7 %collective-permute-start.2 = (bf16[48,1024]{1,0:T(8,128)(2,1)S(1)}, bf16[48,1024]{1,0:T(8,128)(2,1)S(1)}, u32[]{:S(2)}, u32[]{:S(2)}) collective-permute-start(bf16[48,1024]{1,0:T(8,128)(2,1)S(1)} %get-tuple-element.50), channel_id=1, source_target_pairs={{0,4},{1,5},{2,6},{3,7},{4,0},{5,1},{6,2},{7,3},{8,12},{9,13},{10,... | collective-permute-start | bytes 294920 | tf_op jit(solution)/shard_map/ppermute | solution.py:250
  16.1 9.6 %collective-permute-start.3 = (bf16[48,1024]{1,0:T(8,128)(2,1)S(1)}, bf16[48,1024]{1,0:T(8,128)(2,1)S(1)}, u32[]{:S(2)}, u32[]{:S(2)}) collective-permute-start(bf16[48,1024]{1,0:T(8,128)(2,1)S(1)} %get-tuple-element.51), channel_id=1, source_target_pairs={{0,6},{1,7},{2,4},{3,5},{4,2},{5,3},{6,0},{7,1},{8,14},{9,15},{10,... | collective-permute-start | bytes 294920 | tf_op jit(solution)/shard_map/ppermute | solution.py:250
  16.6 12.0 %collective-permute-start.5 = (bf16[192,1024]{1,0:T(8,128)(2,1)S(1)}, bf16[192,1024]{1,0:T(8,128)(2,1)S(1)}, u32[]{:S(2)}, u32[]{:S(2)}) collective-permute-start(bf16[192,1024]{1,0:T(8,128)(2,1)S(1)} %bitcast.156), channel_id=1, source_target_pairs={{0,16},{1,9},{2,18},{3,11},{4,20},{5,13},{6,22},{7,15},{8,24},{9,1... | collective-permute-start | bytes 1179656 | tf_op jit(solution)/shard_map/ppermute | solution.py:250
  24.2 12.8 %collective-permute-start.21 = (bf16[192,1024]{1,0:T(8,128)(2,1)S(1)}, bf16[192,1024]{1,0:T(8,128)(2,1)S(1)}, u32[]{:S(2)}, u32[]{:S(2)}) collective-permute-start(bf16[192,1024]{1,0:T(8,128)(2,1)S(1)} %bitcast.154), channel_id=1, source_target_pairs={{0,16},{1,9},{2,18},{3,11},{4,20},{5,13},{6,22},{7,15},{8,24},{9,1... | collective-permute-start | bytes 1179656 | tf_op jit(solution)/shard_map/ppermute | solution.py:250
  28.6 10.3 %collective-permute-start.8 = (bf16[48,1024]{1,0:T(8,128)(2,1)S(1)}, bf16[48,1024]{1,0:T(8,128)(2,1)S(1)}, u32[]{:S(2)}, u32[]{:S(2)}) collective-permute-start(bf16[48,1024]{1,0:T(8,128)(2,1)S(1)} %get-tuple-element.58), channel_id=1, source_target_pairs={{0,6},{1,7},{2,4},{3,5},{4,2},{5,3},{6,0},{7,1},{8,14},{9,15},{10,... | collective-permute-start | bytes 294920 | tf_op jit(solution)/shard_map/ppermute | solution.py:250
  33.5 6.8 %collective-permute-start.7 = (bf16[48,1024]{1,0:T(8,128)(2,1)S(1)}, bf16[48,1024]{1,0:T(8,128)(2,1)S(1)}, u32[]{:S(2)}, u32[]{:S(2)}) collective-permute-start(bf16[48,1024]{1,0:T(8,128)(2,1)S(1)} %get-tuple-element.57), channel_id=1, source_target_pairs={{0,4},{1,5},{2,6},{3,7},{4,0},{5,1},{6,2},{7,3},{8,12},{9,13},{10,... | collective-permute-start | bytes 294920 | tf_op jit(solution)/shard_map/ppermute | solution.py:250
  37.0 5.8 %collective-permute-start.6 = (bf16[48,1024]{1,0:T(8,128)(2,1)S(1)}, bf16[48,1024]{1,0:T(8,128)(2,1)S(1)}, u32[]{:S(2)}, u32[]{:S(2)}) collective-permute-start(bf16[48,1024]{1,0:T(8,128)(2,1)S(1)} %get-tuple-element.56), channel_id=1, source_target_pairs={{0,2},{1,3},{2,0},{3,1},{4,6},{5,7},{6,4},{7,5},{8,10},{9,11},{10,... | collective-permute-start | bytes 294920 | tf_op jit(solution)/shard_map/ppermute | solution.py:250
  38.9 11.0 %collective-permute-start.22 = (bf16[96,1024]{1,0:T(8,128)(2,1)S(1)}, bf16[96,1024]{1,0:T(8,128)(2,1)S(1)}, u32[]{:S(2)}, u32[]{:S(2)}) collective-permute-start(bf16[96,1024]{1,0:T(8,128)(2,1)S(1)} %pad_maximum_fusion.26), channel_id=1, source_target_pairs={{0,2},{1,3},{2,0},{3,1},{4,6},{5,7},{6,4},{7,5},{8,10},{9,11},{10,... | collective-permute-start | bytes 589832 | tf_op jit(solution)/shard_map/ppermute | solution.py:250
  40.2 17.1 %collective-permute-start.23 = (bf16[96,1024]{1,0:T(8,128)(2,1)S(1)}, bf16[96,1024]{1,0:T(8,128)(2,1)S(1)}, u32[]{:S(2)}, u32[]{:S(2)}) collective-permute-start(bf16[96,1024]{1,0:T(8,128)(2,1)S(1)} %pad_maximum_fusion.24), channel_id=1, source_target_pairs={{0,4},{1,5},{2,6},{3,7},{4,0},{5,1},{6,2},{7,3},{8,12},{9,13},{10,... | collective-permute-start | bytes 589832 | tf_op jit(solution)/shard_map/ppermute | solution.py:250
  42.8 14.5 %collective-permute-start.24 = (bf16[96,1024]{1,0:T(8,128)(2,1)S(1)}, bf16[96,1024]{1,0:T(8,128)(2,1)S(1)}, u32[]{:S(2)}, u32[]{:S(2)}) collective-permute-start(bf16[96,1024]{1,0:T(8,128)(2,1)S(1)} %pad_maximum_fusion.25), channel_id=1, source_target_pairs={{0,6},{1,7},{2,4},{3,5},{4,2},{5,3},{6,0},{7,1},{8,14},{9,15},{10,... | collective-permute-start | bytes 589832 | tf_op jit(solution)/shard_map/ppermute | solution.py:250
  58.9 24.4 %collective-permute-start.25 = (bf16[384,768]{1,0:T(8,128)(2,1)S(1)}, bf16[384,768]{1,0:T(8,128)(2,1)S(1)}, u32[]{:S(2)}, u32[]{:S(2)}) collective-permute-start(bf16[384,768]{1,0:T(8,128)(2,1)S(1)} %pad_maximum_fusion.3), channel_id=1, source_target_pairs={{0,16},{1,9},{2,18},{3,11},{4,20},{5,13},{6,22},{7,15},{8,24},{9,1... | collective-permute-start | bytes 1769480 | tf_op jit(solution)/shard_map/ppermute | solution.py:250
  61.2 13.9 %collective-permute-start.9 = (bf16[192,1536]{1,0:T(8,128)(2,1)S(1)}, bf16[192,1536]{1,0:T(8,128)(2,1)S(1)}, u32[]{:S(2)}, u32[]{:S(2)}) collective-permute-start(bf16[192,1536]{1,0:T(8,128)(2,1)S(1)} %fusion.6), channel_id=1, source_target_pairs={{0,16},{1,9},{2,18},{3,11},{4,20},{5,13},{6,22},{7,15},{8,24},{9,1... | collective-permute-start | bytes 1769480 | tf_op jit(solution)/shard_map/ppermute | solution.py:250
  62.5 19.0 %collective-permute-start.14 = (bf16[192,1536]{1,0:T(8,128)(2,1)S(1)}, bf16[192,1536]{1,0:T(8,128)(2,1)S(1)}, u32[]{:S(2)}, u32[]{:S(2)}) collective-permute-start(bf16[192,1536]{1,0:T(8,128)(2,1)S(1)} %fusion.7), channel_id=1, source_target_pairs={{0,16},{1,9},{2,18},{3,11},{4,20},{5,13},{6,22},{7,15},{8,24},{9,1... | collective-permute-start | bytes 1769480 | tf_op jit(solution)/shard_map/ppermute | solution.py:250
  85.9 41.4 %collective-permute-start.13 = (bf16[48,1024]{1,0:T(8,128)(2,1)S(1)}, bf16[48,1024]{1,0:T(8,128)(2,1)S(1)}, u32[]{:S(2)}, u32[]{:S(2)}) collective-permute-start(bf16[48,1024]{1,0:T(8,128)(2,1)S(1)} %get-tuple-element.65), channel_id=1, source_target_pairs={{0,6},{1,7},{2,4},{3,5},{4,2},{5,3},{6,0},{7,1},{8,14},{9,15},{10,... | collective-permute-start | bytes 294920 | tf_op jit(solution)/shard_map/ppermute | solution.py:250
  88.2 39.6 %collective-permute-start.12 = (bf16[48,1024]{1,0:T(8,128)(2,1)S(1)}, bf16[48,1024]{1,0:T(8,128)(2,1)S(1)}, u32[]{:S(2)}, u32[]{:S(2)}) collective-permute-start(bf16[48,1024]{1,0:T(8,128)(2,1)S(1)} %get-tuple-element.64), channel_id=1, source_target_pairs={{0,4},{1,5},{2,6},{3,7},{4,0},{5,1},{6,2},{7,3},{8,12},{9,13},{10,... | collective-permute-start | bytes 294920 | tf_op jit(solution)/shard_map/ppermute | solution.py:250
  90.4 8.0 %collective-permute-start.28 = (bf16[48,1024]{1,0:T(8,128)(2,1)S(1)}, bf16[48,1024]{1,0:T(8,128)(2,1)S(1)}, u32[]{:S(2)}, u32[]{:S(2)}) collective-permute-start(bf16[48,1024]{1,0:T(8,128)(2,1)S(1)} %get-tuple-element.83), channel_id=1, source_target_pairs={{0,6},{1,7},{2,4},{3,5},{4,2},{5,3},{6,0},{7,1},{8,14},{9,15},{10,... | collective-permute-start | bytes 294920 | tf_op jit(solution)/shard_map/ppermute | solution.py:250
  93.0 14.9 %collective-permute-start.27 = (bf16[48,1024]{1,0:T(8,128)(2,1)S(1)}, bf16[48,1024]{1,0:T(8,128)(2,1)S(1)}, u32[]{:S(2)}, u32[]{:S(2)}) collective-permute-start(bf16[48,1024]{1,0:T(8,128)(2,1)S(1)} %get-tuple-element.82), channel_id=1, source_target_pairs={{0,4},{1,5},{2,6},{3,7},{4,0},{5,1},{6,2},{7,3},{8,12},{9,13},{10,... | collective-permute-start | bytes 294920 | tf_op jit(solution)/shard_map/ppermute | solution.py:250
  93.0 15.5 %collective-permute-start.26 = (bf16[48,1024]{1,0:T(8,128)(2,1)S(1)}, bf16[48,1024]{1,0:T(8,128)(2,1)S(1)}, u32[]{:S(2)}, u32[]{:S(2)}) collective-permute-start(bf16[48,1024]{1,0:T(8,128)(2,1)S(1)} %get-tuple-element.81), channel_id=1, source_target_pairs={{0,2},{1,3},{2,0},{3,1},{4,6},{5,7},{6,4},{7,5},{8,10},{9,11},{10,... | collective-permute-start | bytes 294920 | tf_op jit(solution)/shard_map/ppermute | solution.py:250
  98.5 13.7 %collective-permute-start.17 = (bf16[48,1024]{1,0:T(8,128)(2,1)S(1)}, bf16[48,1024]{1,0:T(8,128)(2,1)S(1)}, u32[]{:S(2)}, u32[]{:S(2)}) collective-permute-start(bf16[48,1024]{1,0:T(8,128)(2,1)S(1)} %get-tuple-element.69), channel_id=1, source_target_pairs={{0,6},{1,7},{2,4},{3,5},{4,2},{5,3},{6,0},{7,1},{8,14},{9,15},{10,... | collective-permute-start | bytes 294920 | tf_op jit(solution)/shard_map/ppermute | solution.py:250
  107.9 9.6 %collective-permute-start.16 = (bf16[48,1024]{1,0:T(8,128)(2,1)S(1)}, bf16[48,1024]{1,0:T(8,128)(2,1)S(1)}, u32[]{:S(2)}, u32[]{:S(2)}) collective-permute-start(bf16[48,1024]{1,0:T(8,128)(2,1)S(1)} %get-tuple-element.68), channel_id=1, source_target_pairs={{0,4},{1,5},{2,6},{3,7},{4,0},{5,1},{6,2},{7,3},{8,12},{9,13},{10,... | collective-permute-start | bytes 294920 | tf_op jit(solution)/shard_map/ppermute | solution.py:250
  108.5 9.0 %collective-permute-start.15 = (bf16[48,1024]{1,0:T(8,128)(2,1)S(1)}, bf16[48,1024]{1,0:T(8,128)(2,1)S(1)}, u32[]{:S(2)}, u32[]{:S(2)}) collective-permute-start(bf16[48,1024]{1,0:T(8,128)(2,1)S(1)} %get-tuple-element.67), channel_id=1, source_target_pairs={{0,2},{1,3},{2,0},{3,1},{4,6},{5,7},{6,4},{7,5},{8,10},{9,11},{10,... | collective-permute-start | bytes 294920 | tf_op jit(solution)/shard_map/ppermute | solution.py:250
  112.1 9.7 %collective-permute-start.31 = (bf16[48,1024]{1,0:T(8,128)(2,1)S(1)}, bf16[48,1024]{1,0:T(8,128)(2,1)S(1)}, u32[]{:S(2)}, u32[]{:S(2)}) collective-permute-start(bf16[48,1024]{1,0:T(8,128)(2,1)S(1)} %get-tuple-element.88), channel_id=1, source_target_pairs={{0,6},{1,7},{2,4},{3,5},{4,2},{5,3},{6,0},{7,1},{8,14},{9,15},{10,... | collective-permute-start | bytes 294920 | tf_op jit(solution)/shard_map/ppermute | solution.py:250
  117.5 6.7 %collective-permute-start.30 = (bf16[48,1024]{1,0:T(8,128)(2,1)S(1)}, bf16[48,1024]{1,0:T(8,128)(2,1)S(1)}, u32[]{:S(2)}, u32[]{:S(2)}) collective-permute-start(bf16[48,1024]{1,0:T(8,128)(2,1)S(1)} %get-tuple-element.87), channel_id=1, source_target_pairs={{0,4},{1,5},{2,6},{3,7},{4,0},{5,1},{6,2},{7,3},{8,12},{9,13},{10,... | collective-permute-start | bytes 294920 | tf_op jit(solution)/shard_map/ppermute | solution.py:250
  117.5 8.2 %collective-permute-start.29 = (bf16[48,1024]{1,0:T(8,128)(2,1)S(1)}, bf16[48,1024]{1,0:T(8,128)(2,1)S(1)}, u32[]{:S(2)}, u32[]{:S(2)}) collective-permute-start(bf16[48,1024]{1,0:T(8,128)(2,1)S(1)} %get-tuple-element.86), channel_id=1, source_target_pairs={{0,2},{1,3},{2,0},{3,1},{4,6},{5,7},{6,4},{7,5},{8,10},{9,11},{10,... | collective-permute-start | bytes 294920 | tf_op jit(solution)/shard_map/ppermute | solution.py:250
  121.8 6.5 %collective-permute-start.11 = (bf16[48,1024]{1,0:T(8,128)(2,1)S(1)}, bf16[48,1024]{1,0:T(8,128)(2,1)S(1)}, u32[]{:S(2)}, u32[]{:S(2)}) collective-permute-start(bf16[48,1024]{1,0:T(8,128)(2,1)S(1)} %get-tuple-element.63), channel_id=1, source_target_pairs={{0,2},{1,3},{2,0},{3,1},{4,6},{5,7},{6,4},{7,5},{8,10},{9,11},{10,... | collective-permute-start | bytes 294920 | tf_op jit(solution)/shard_map/ppermute | solution.py:250
  124.2 34.1 %collective-permute-start.34 = (bf16[2,512,768]{2,1,0:T(8,128)(2,1)S(1)}, bf16[2,512,768]{2,1,0:T(8,128)(2,1)S(1)}, u32[]{:S(2)}, u32[]{:S(2)}) collective-permute-start(bf16[2,512,768]{2,1,0:T(8,128)(2,1)S(1)} %pad_maximum_fusion), channel_id=1, source_target_pairs={{0,8},{1,17},{2,10},{3,19},{4,12},{5,21},{6,14},{7,23},{8,0},{9,25... | collective-permute-start | bytes 4718600 | tf_op jit(solution)/shard_map/ppermute | solution.py:250
  125.7 12.0 %collective-permute-start.18 = (bf16[192,1024]{1,0:T(8,128)(2,1)S(1)}, bf16[192,1024]{1,0:T(8,128)(2,1)S(1)}, u32[]{:S(2)}, u32[]{:S(2)}) collective-permute-start(bf16[192,1024]{1,0:T(8,128)(2,1)S(1)} %pad_maximum_fusion.16), channel_id=1, source_target_pairs={{0,16},{1,9},{2,18},{3,11},{4,20},{5,13},{6,22},{7,15},{8,24},{9,1... | collective-permute-start | bytes 1179656 | tf_op jit(solution)/shard_map/ppermute | solution.py:250
  127.3 27.8 %collective-permute-start.35 = (bf16[512,768]{1,0:T(8,128)(2,1)S(1)}, bf16[512,768]{1,0:T(8,128)(2,1)S(1)}, u32[]{:S(2)}, u32[]{:S(2)}) collective-permute-start(bf16[512,768]{1,0:T(8,128)(2,1)S(1)} %convolution_convert_fusion), channel_id=1, source_target_pairs={{0,8},{1,17},{2,10},{3,19},{4,12},{5,21},{6,14},{7,23},{8,0},{9,25... | collective-permute-start | bytes 2359304 | tf_op jit(solution)/shard_map/ppermute | solution.py:250
  127.8 18.3 %collective-permute-start.32 = (bf16[192,1024]{1,0:T(8,128)(2,1)S(1)}, bf16[192,1024]{1,0:T(8,128)(2,1)S(1)}, u32[]{:S(2)}, u32[]{:S(2)}) collective-permute-start(bf16[192,1024]{1,0:T(8,128)(2,1)S(1)} %pad_maximum_fusion.22), channel_id=1, source_target_pairs={{0,16},{1,9},{2,18},{3,11},{4,20},{5,13},{6,22},{7,15},{8,24},{9,1... | collective-permute-start | bytes 1179656 | tf_op jit(solution)/shard_map/ppermute | solution.py:250
  137.8 17.9 %collective-permute-start.19 = (bf16[96,2048]{1,0:T(8,128)(2,1)S(1)}, bf16[96,2048]{1,0:T(8,128)(2,1)S(1)}, u32[]{:S(2)}, u32[]{:S(2)}) collective-permute-start(bf16[96,2048]{1,0:T(8,128)(2,1)S(1)} %pad_maximum_fusion.17), channel_id=1, source_target_pairs={{0,1},{1,0},{2,3},{3,2},{4,5},{5,4},{6,7},{7,6},{8,9},{9,8},{10,11... | collective-permute-start | bytes 1179656 | tf_op jit(solution)/shard_map/ppermute | solution.py:250
  146.2 10.8 %collective-permute-start.33 = (bf16[96,2048]{1,0:T(8,128)(2,1)S(1)}, bf16[96,2048]{1,0:T(8,128)(2,1)S(1)}, u32[]{:S(2)}, u32[]{:S(2)}) collective-permute-start(bf16[96,2048]{1,0:T(8,128)(2,1)S(1)} %pad_maximum_fusion.23), channel_id=1, source_target_pairs={{0,1},{1,0},{2,3},{3,2},{4,5},{5,4},{6,7},{7,6},{8,9},{9,8},{10,11... | collective-permute-start | bytes 1179656 | tf_op jit(solution)/shard_map/ppermute | solution.py:250

commit v4 on v3

--- a/solution.py
+++ b/solution.py
@@ -174,44 +174,71 @@
     )(weights)
 
 
-def weight_terms(rows, grads, arrived, down):
-    parts, depth, hidden = arrived.shape
-
-    def kernel(rows_ref, gate_ref, up_ref, arrived_ref, down_ref, answer, held, sem):
-        writes = [pltpu.make_async_copy(down_ref, answer.at[parts], sem.at[parts])]
-        writes[0].start()
-        for part, grad in enumerate((gate_ref, up_ref)):
-            term = contract(rows_ref[:, :depth], grad[...], 0, 0)
-            held[part] = (term + arrived_ref[part].astype(F32)).astype(BF16)
-            writes.append(pltpu.make_async_copy(held.at[part], answer.at[part], sem.at[part]))
-            writes[-1].start()
-        for write in writes:
-            write.wait()
+def first_terms(own, arrived, down):
+    depth, hidden = own.shape
+
+    def kernel(own_ref, arrived_ref, down_ref, answer, held, sem):
+        copies = [pltpu.make_async_copy(down_ref, answer.at[2], sem.at[0])]
+        copies[0].start()
+        held[...] = (own_ref[...] + arrived_ref[...].astype(F32)).astype(BF16)
+        copies.append(pltpu.make_async_copy(held, answer.at[0], sem.at[1]))
+        copies[1].start()
+        for copy in copies:
+            copy.wait()
 
     return pl.pallas_call(
         kernel,
-        out_shape=jax.ShapeDtypeStruct((parts + 1, depth, hidden), BF16),
-        in_specs=[VMEM] * 5,
+        out_shape=jax.ShapeDtypeStruct((3, depth, hidden), BF16),
+        in_specs=[VMEM] * 3,
         out_specs=HBM,
-        scratch_shapes=[
-            pltpu.VMEM(arrived.shape, BF16),
-            pltpu.SemaphoreType.DMA((parts + 1,)),
-        ],
+        scratch_shapes=[pltpu.VMEM((depth, hidden), BF16), pltpu.SemaphoreType.DMA((2,))],
         compiler_params=PARAMS,
-        name="weight_terms",
-    )(rows, *grads, arrived, down)
-
-
-def fold(table, own, out, came):
-    tok_count, width = table.shape[1], came.shape[1] // 4
-
-    def kernel(table_ref, own_ref, out_ref, came_ref, answer, held, sem):
+        name="first_terms",
+    )(own, arrived, down)
+
+
+def last_term(whole, own, arrived):
+    depth, hidden = own.shape
+    pieces = 4
+    rows = depth // pieces
+
+    def kernel(whole_ref, own_ref, arrived_ref, answer, held, sem):
+        copies = []
+        for i in range(pieces):
+            span = pl.ds(i * rows, rows)
+            held[span] = (own_ref[span, :] + arrived_ref[span, :].astype(F32)).astype(BF16)
+            copies.append(pltpu.make_async_copy(held.at[span], answer.at[1, span], sem.at[i]))
+            copies[i].start()
+        for copy in copies:
+            copy.wait()
+
+    return pl.pallas_call(
+        kernel,
+        out_shape=jax.ShapeDtypeStruct(whole.shape, BF16),
+        in_specs=[HBM, VMEM, VMEM],
+        out_specs=HBM,
+        scratch_shapes=[pltpu.VMEM((depth, hidden), BF16), pltpu.SemaphoreType.DMA((pieces,))],
+        input_output_aliases={0: 0},
+        compiler_params=PARAMS,
+        name="last_term",
+    )(whole, own, arrived)
+
+
+def fold(table, same, other):
+    tok_count, width = table.shape[1], same[0][0].shape[1] // 2
+    arrays = list({id(array): array for array, _ in (*same, *other)}.values())
+    number = {id(array): i for i, array in enumerate(arrays)}
+    spots = [[(number[id(array)], block) for array, block in side] for side in (same, other)]
+
+    def kernel(table_ref, *refs):
+        sources, (answer, held, sem) = refs[: len(arrays)], refs[len(arrays) :]
         _, _, quarter = where_am_i()
         writes = []
         for index in range(4):
-            low = index % 2 * width
-            first = (own_ref, out_ref)[index // 2][:, low : low + width]
-            rows = jnp.concatenate([first, came_ref[:, index * width : (index + 1) * width]])
+            parts = [side[index] for side in spots]
+            rows = jnp.concatenate(
+                [sources[i][:, block * width : (block + 1) * width] for i, block in parts]
+            )
             held[index] = contract(table_ref[...], rows, 0, 0).astype(BF16)
             writes.append(
                 pltpu.make_async_copy(
@@ -226,13 +253,13 @@
 
     return pl.pallas_call(
         kernel,
-        out_shape=jax.ShapeDtypeStruct((tok_count, came.shape[1]), BF16),
-        in_specs=[VMEM] * 4,
+        out_shape=jax.ShapeDtypeStruct((tok_count, 4 * width), BF16),
+        in_specs=[VMEM] * (1 + len(arrays)),
         out_specs=HBM,
         scratch_shapes=[pltpu.VMEM((4, tok_count, width), BF16), pltpu.SemaphoreType.DMA((4,))],
         compiler_params=PARAMS,
         name="fold",
-    )(table, own, out, came)
+    )(table, *arrays)
 
 
 class Moves:
@@ -257,6 +284,11 @@
 
     def column_pair(self, value):
         return self.move(value, lambda d, f, e: (1 - d, f, e) if e % 2 == 0 else (d, 1 - f, e))
+
+    def cross_pair(self, value):
+        return self.move(
+            value, lambda d, f, e: (1 - d, f, e ^ 1) if e % 2 == 0 else (d, 1 - f, e ^ 1)
+        )
 
     def along_z(self, value, step):
         return self.move(value, lambda d, f, e: (d, f, e ^ (2 * step)))
@@ -317,19 +349,28 @@
             low += n
         return whole
 
-    def give_back_in(table, own, near):
+    def source(array, index):
+        return array.reshape(steps, 2, CAP, half_width)[:, index].reshape(half, half_width)
+
+    def give_back(table, own, near):
         out = moves.column_pair(near)
-
-        def source(array, index):
-            return array.reshape(steps, 2, CAP, half_width)[:, index].reshape(half, half_width)
-
         parts = [
             side[:, i * quarter_width : (i + 1) * quarter_width]
             for i in (0, 1)
             for side in (source(own, 1), source(out, 1))
         ]
         came = moves.core(jnp.concatenate(parts, axis=1))
-        return fold(table, source(own, 0), source(out, 0), came)
+        own, out = source(own, 0), source(out, 0)
+        other = [(came, i) for i in range(4)]
+        return fold(table, [(own, 0), (own, 1), (out, 0), (out, 1)], other)
+
+    def give_back_crossed(table, own, near):
+        out = moves.column_pair(source(near, 0))
+        cross = moves.cross_pair(source(near, 1))
+        came = moves.core(source(own, 1))
+        own = source(own, 0)
+        same = [(own, 0), (own, 1), (out, 0), (out, 1)]
+        return fold(table, same, [(came, 0), (cross, 0), (came, 1), (cross, 1)])
 
     def inward(rows, which, sides=(0, 1)):
         return sum(
@@ -403,17 +444,20 @@
     arrived_down = moves.weight_pair(term_far)
     grad_near = outward([(gg_near, 0), (ug_near, 1)])
     (grad_near,) = by_z([grad_near])
-    terms_far = jnp.stack(
-        [contract(rows[:, second], value, 0, 0) for value in (gate_grad, up_grad)]
-    ).astype(BF16)
-    arrived_in = moves.weight_pair(terms_far)
+    gate_far = contract(rows[:, second], gate_grad, 0, 0).astype(BF16)
+    arrived_gate = moves.weight_pair(gate_far)
+    up_far = contract(rows[:, second], up_grad, 0, 0).astype(BF16)
+    arrived_up = moves.weight_pair(up_far)
     grad_own = outward([(gg_own, 0), (ug_own, 1)])
     (grad_own,) = by_z([grad_own])
-    moe_out = give_back_in(combine, back_own, back_near)
-    token_grad = give_back_in(dispatch, grad_own, grad_near)
+    moe_out = give_back(combine, back_own, back_near)
+    token_grad = give_back_crossed(dispatch, grad_own, grad_near)
     term_down = contract(scaled[:, first], activation, 0, 0) + arrived_down.astype(F32)
     term_down = term_down.astype(BF16)
-    weight_grad = weight_terms(rows, (gate_grad, up_grad), arrived_in, term_down)
+    own_gate = contract(rows[:, first], gate_grad, 0, 0)
+    own_up = contract(rows[:, first], up_grad, 0, 0)
+    weight_grad = first_terms(own_gate, arrived_gate, term_down)
+    weight_grad = last_term(weight_grad, own_up, arrived_up)
     return moe_out, token_grad, jnp.transpose(weight_grad, (1, 0, 2))[None]
 
 

time: 161 us -> 161 us (level)
  waiting for transfers between devices: 79.4 us -> 73.9 us
  starting transfers between devices: 55.1 us -> 59.8 us
    ppermute x36 -> x38, waiting for transfers between devices: 79.4 us -> 73.9 us  [move(): return lax.ppermute(value, ALL, pairs)]
    ppermute x36 -> x38, starting transfers between devices: 55.1 us -> 59.8 us  [move(): return lax.ppermute(value, ALL, pairs)]
    dot_general x28 -> x30, matrix products: 11.2 us -> 12.4 us  [contract(): lax.dot_general(left, right, (((left_dim,), (right_dim,)), ((), ())), pre...]
    pallas_call x3 -> x4, Pallas kernels: 4.51 us -> 4.62 us  [the longest x2 2.53 us: fold(): pl.pallas_call(kernel, out_shape=jax.ShapeDtypeStruct((tok_count, 4 * wid...]
  transfers between devices with their start and end apart: 36 -> 38, of which waited for: 17 -> 19; matrix products, arithmetic and copies ran while one was open for 7% -> 7% of each run, Pallas kernels for 2% -> 2%
where the time goes in v4:
time: 161 us
  waiting for transfers between devices  73.9 us (46%)
  starting transfers between devices  59.8 us (37%)
  matrix products  12.4 us (8%)
  Pallas kernels  5.92 us (4%)
  local copies, waits for them, and re-layouts  4.87 us (3%)
  other arithmetic  2.01 us (1%)
    ppermute x38, waiting for transfers between devices, move(): return lax.ppermute(value, ALL, pairs)  73.9 us
    ppermute x38, starting transfers between devices, move(): return lax.ppermute(value, ALL, pairs)  59.8 us
    dot_general x30, matrix products, contract(): lax.dot_general(left, right, (((left_dim,), (right_dim,)), ((), ())), pre...  12.4 us
    unnamed x25, local copies, waits for them, and re-layouts  4.46 us
  transfers between devices with their start and end apart: 38, of which 19 were waited for; matrix products, arithmetic and copies ran while one was open for 7% of the time, Pallas kernels for 2%

profile of v4, /device:TPU:0, one launch (start us, length us, event | category | flops | bytes accessed | tf_op | source)
XLA Modules:
  0.0 160.6 jit_solution(3791142950541357524)
XLA Ops:
  0.6 1.2 copy-done.1
  1.9 0.7 copy-done.3
  2.6 0.7 copy-done.4
  3.3 0.7 front.1
  4.0 0.6 collective-permute-start
  4.5 1.7 %copy-done = bf16[1,512,3,768]{3,1,2,0:T(8,128)(2,1)S(1)} copy-done((bf16[1,512,3,768]{3,1,2,0:T(8,128)(2,1)S(1)}, bf16[1,512,3,768]{3,1,2,0:T(8,128)(2,1)}, u32[]{:S(2)}) %copy-start) | copy-done | bytes 2359320
  6.4 2.6 %collective-permute-start.4 = (bf16[2,512,768]{2,1,0:T(8,128)(2,1)S(1)}, bf16[2,512,768]{2,1,0:T(8,128)(2,1)S(1)}, u32[]{:S(2)}, u32[]{:S(2)}) collective-permute-start(bf16[2,512,768]{2,1,0:T(8,128)(2,1)S(1)} %get-tuple-element.52), channel_id=1, source_target_pairs={{0,8},{1,17},{2,10},{3,19},{4,12},{5,21},{6,14},{7,23},{8,0},{9,25... | collective-permute-start | bytes 4718600 | tf_op jit(solution)/shard_map/ppermute | solution.py:277
  9.8 1.4 collective-permute-done.20
  11.4 2.1 %collective-permute-start.1 = (bf16[48,1024]{1,0:T(8,128)(2,1)S(1)}, bf16[48,1024]{1,0:T(8,128)(2,1)S(1)}, u32[]{:S(2)}, u32[]{:S(2)}) collective-permute-start(bf16[48,1024]{1,0:T(8,128)(2,1)S(1)} %get-tuple-element.49), channel_id=1, source_target_pairs={{0,2},{1,3},{2,0},{3,1},{4,6},{5,7},{6,4},{7,5},{8,10},{9,11},{10,... | collective-permute-start | bytes 294920 | tf_op jit(solution)/shard_map/ppermute | solution.py:277
  13.5 2.6 %collective-permute-start.2 = (bf16[48,1024]{1,0:T(8,128)(2,1)S(1)}, bf16[48,1024]{1,0:T(8,128)(2,1)S(1)}, u32[]{:S(2)}, u32[]{:S(2)}) collective-permute-start(bf16[48,1024]{1,0:T(8,128)(2,1)S(1)} %get-tuple-element.50), channel_id=1, source_target_pairs={{0,4},{1,5},{2,6},{3,7},{4,0},{5,1},{6,2},{7,3},{8,12},{9,13},{10,... | collective-permute-start | bytes 294920 | tf_op jit(solution)/shard_map/ppermute | solution.py:277
  16.6 1.7 %collective-permute-start.5 = (bf16[192,1024]{1,0:T(8,128)(2,1)S(1)}, bf16[192,1024]{1,0:T(8,128)(2,1)S(1)}, u32[]{:S(2)}, u32[]{:S(2)}) collective-permute-start(bf16[192,1024]{1,0:T(8,128)(2,1)S(1)} %bitcast.150), channel_id=1, source_target_pairs={{0,16},{1,9},{2,18},{3,11},{4,20},{5,13},{6,22},{7,15},{8,24},{9,1... | collective-permute-start | bytes 1179656 | tf_op jit(solution)/shard_map/ppermute | solution.py:277
  18.2 5.9 %collective-permute-done.2 = bf16[48,1024]{1,0:T(8,128)(2,1)S(1)} collective-permute-done((bf16[48,1024]{1,0:T(8,128)(2,1)S(1)}, bf16[48,1024]{1,0:T(8,128)(2,1)S(1)}, u32[]{:S(2)}, u32[]{:S(2)}) %collective-permute-start.2) | collective-permute-done | bytes 98336 | tf_op jit(solution)/shard_map/ppermute | solution.py:277
  24.2 1.5 collective-permute-start.21
  26.4 2.2 %collective-permute-done.5 = bf16[192,1024]{1,0:T(8,128)(2,1)S(1)} collective-permute-done((bf16[192,1024]{1,0:T(8,128)(2,1)S(1)}, bf16[192,1024]{1,0:T(8,128)(2,1)S(1)}, u32[]{:S(2)}, u32[]{:S(2)}) %collective-permute-start.5) | collective-permute-done | bytes 393248 | tf_op jit(solution)/shard_map/ppermute | solution.py:277
  28.6 4.9 %collective-permute-start.8 = (bf16[48,1024]{1,0:T(8,128)(2,1)S(1)}, bf16[48,1024]{1,0:T(8,128)(2,1)S(1)}, u32[]{:S(2)}, u32[]{:S(2)}) collective-permute-start(bf16[48,1024]{1,0:T(8,128)(2,1)S(1)} %get-tuple-element.58), channel_id=1, source_target_pairs={{0,6},{1,7},{2,4},{3,5},{4,2},{5,3},{6,0},{7,1},{8,14},{9,15},{10,... | collective-permute-start | bytes 294920 | tf_op jit(solution)/shard_map/ppermute | solution.py:277
  33.5 3.5 %collective-permute-done.21 = bf16[192,1024]{1,0:T(8,128)(2,1)S(1)} collective-permute-done((bf16[192,1024]{1,0:T(8,128)(2,1)S(1)}, bf16[192,1024]{1,0:T(8,128)(2,1)S(1)}, u32[]{:S(2)}, u32[]{:S(2)}) %collective-permute-start.21) | collective-permute-done | bytes 393248 | tf_op jit(solution)/shard_map/ppermute | solution.py:277
  37.0 1.7 %collective-permute-start.6 = (bf16[48,1024]{1,0:T(8,128)(2,1)S(1)}, bf16[48,1024]{1,0:T(8,128)(2,1)S(1)}, u32[]{:S(2)}, u32[]{:S(2)}) collective-permute-start(bf16[48,1024]{1,0:T(8,128)(2,1)S(1)} %get-tuple-element.56), channel_id=1, source_target_pairs={{0,2},{1,3},{2,0},{3,1},{4,6},{5,7},{6,4},{7,5},{8,10},{9,11},{10,... | collective-permute-start | bytes 294920 | tf_op jit(solution)/shard_map/ppermute | solution.py:277
  38.9 0.6 collective-permute-start.22
  39.5 0.7 collective-permute-done.7
  40.2 2.6 %collective-permute-start.23 = (bf16[96,1024]{1,0:T(8,128)(2,1)S(1)}, bf16[96,1024]{1,0:T(8,128)(2,1)S(1)}, u32[]{:S(2)}, u32[]{:S(2)}) collective-permute-start(bf16[96,1024]{1,0:T(8,128)(2,1)S(1)} %pad_maximum_fusion.26), channel_id=1, source_target_pairs={{0,4},{1,5},{2,6},{3,7},{4,0},{5,1},{6,2},{7,3},{8,12},{9,13},{10,... | collective-permute-start | bytes 589832 | tf_op jit(solution)/shard_map/ppermute | solution.py:277
  42.8 5.9 %collective-permute-start.24 = (bf16[96,1024]{1,0:T(8,128)(2,1)S(1)}, bf16[96,1024]{1,0:T(8,128)(2,1)S(1)}, u32[]{:S(2)}, u32[]{:S(2)}) collective-permute-start(bf16[96,1024]{1,0:T(8,128)(2,1)S(1)} %pad_maximum_fusion.27), channel_id=1, source_target_pairs={{0,6},{1,7},{2,4},{3,5},{4,2},{5,3},{6,0},{7,1},{8,14},{9,15},{10,... | collective-permute-start | bytes 589832 | tf_op jit(solution)/shard_map/ppermute | solution.py:277
  49.4 0.5 collective-permute-done.22
  49.9 7.4 %collective-permute-done.23 = bf16[96,1024]{1,0:T(8,128)(2,1)S(1)} collective-permute-done((bf16[96,1024]{1,0:T(8,128)(2,1)S(1)}, bf16[96,1024]{1,0:T(8,128)(2,1)S(1)}, u32[]{:S(2)}, u32[]{:S(2)}) %collective-permute-start.23) | collective-permute-done | bytes 196640 | tf_op jit(solution)/shard_map/ppermute | solution.py:277
  58.9 1.6 collective-permute-start.25
  61.2 0.6 collective-permute-start.9
  62.5 1.6 collective-permute-start.14
  64.1 11.1 %collective-permute-done.9 = bf16[192,1536]{1,0:T(8,128)(2,1)S(1)} collective-permute-done((bf16[192,1536]{1,0:T(8,128)(2,1)S(1)}, bf16[192,1536]{1,0:T(8,128)(2,1)S(1)}, u32[]{:S(2)}, u32[]{:S(2)}) %collective-permute-start.9) | collective-permute-done | bytes 589856 | tf_op jit(solution)/shard_map/ppermute | solution.py:277
  76.1 5.5 %collective-permute-done.14 = bf16[192,1536]{1,0:T(8,128)(2,1)S(1)} collective-permute-done((bf16[192,1536]{1,0:T(8,128)(2,1)S(1)}, bf16[192,1536]{1,0:T(8,128)(2,1)S(1)}, u32[]{:S(2)}, u32[]{:S(2)}) %collective-permute-start.14) | collective-permute-done | bytes 589856 | tf_op jit(solution)/shard_map/ppermute | solution.py:277
  82.0 0.4 convolution_convert_fusion.4
  85.8 0.6 fusion.35.own_ref
  86.4 0.6 convolution_convert_fusion.2
  87.1 2.4 %collective-permute-start.13 = (bf16[48,1024]{1,0:T(8,128)(2,1)S(1)}, bf16[48,1024]{1,0:T(8,128)(2,1)S(1)}, u32[]{:S(2)}, u32[]{:S(2)}) collective-permute-start(bf16[48,1024]{1,0:T(8,128)(2,1)S(1)} %get-tuple-element.65), channel_id=1, source_target_pairs={{0,6},{1,7},{2,4},{3,5},{4,2},{5,3},{6,0},{7,1},{8,14},{9,15},{10,... | collective-permute-start | bytes 294920 | tf_op jit(solution)/shard_map/ppermute | solution.py:277
  89.4 2.1 %collective-permute-start.12 = (bf16[48,1024]{1,0:T(8,128)(2,1)S(1)}, bf16[48,1024]{1,0:T(8,128)(2,1)S(1)}, u32[]{:S(2)}, u32[]{:S(2)}) collective-permute-start(bf16[48,1024]{1,0:T(8,128)(2,1)S(1)} %get-tuple-element.64), channel_id=1, source_target_pairs={{0,4},{1,5},{2,6},{3,7},{4,0},{5,1},{6,2},{7,3},{8,12},{9,13},{10,... | collective-permute-start | bytes 294920 | tf_op jit(solution)/shard_map/ppermute | solution.py:277
  91.7 2.4 %collective-permute-start.17 = (bf16[48,1024]{1,0:T(8,128)(2,1)S(1)}, bf16[48,1024]{1,0:T(8,128)(2,1)S(1)}, u32[]{:S(2)}, u32[]{:S(2)}) collective-permute-start(bf16[48,1024]{1,0:T(8,128)(2,1)S(1)} %get-tuple-element.69), channel_id=1, source_target_pairs={{0,6},{1,7},{2,4},{3,5},{4,2},{5,3},{6,0},{7,1},{8,14},{9,15},{10,... | collective-permute-start | bytes 294920 | tf_op jit(solution)/shard_map/ppermute | solution.py:277
  94.2 1.0 collective-permute-start.16
  95.2 0.6 convolution_convert_fusion
  96.6 0.4 fusion.3
  97.1 0.6 convolution_convert_fusion.1
  97.8 2.3 %collective-permute-start.15 = (bf16[48,1024]{1,0:T(8,128)(2,1)S(1)}, bf16[48,1024]{1,0:T(8,128)(2,1)S(1)}, u32[]{:S(2)}, u32[]{:S(2)}) collective-permute-start(bf16[48,1024]{1,0:T(8,128)(2,1)S(1)} %get-tuple-element.67), channel_id=1, source_target_pairs={{0,2},{1,3},{2,0},{3,1},{4,6},{5,7},{6,4},{7,5},{8,10},{9,11},{10,... | collective-permute-start | bytes 294920 | tf_op jit(solution)/shard_map/ppermute | solution.py:277
  100.0 6.1 %collective-permute-done.12 = bf16[48,1024]{1,0:T(8,128)(2,1)S(1)} collective-permute-done((bf16[48,1024]{1,0:T(8,128)(2,1)S(1)}, bf16[48,1024]{1,0:T(8,128)(2,1)S(1)}, u32[]{:S(2)}, u32[]{:S(2)}) %collective-permute-start.12) | collective-permute-done | bytes 98336 | tf_op jit(solution)/shard_map/ppermute | solution.py:277
  106.2 2.8 %collective-permute-start.28 = (bf16[48,1024]{1,0:T(8,128)(2,1)S(1)}, bf16[48,1024]{1,0:T(8,128)(2,1)S(1)}, u32[]{:S(2)}, u32[]{:S(2)}) collective-permute-start(bf16[48,1024]{1,0:T(8,128)(2,1)S(1)} %get-tuple-element.83), channel_id=1, source_target_pairs={{0,6},{1,7},{2,4},{3,5},{4,2},{5,3},{6,0},{7,1},{8,14},{9,15},{10,... | collective-permute-start | bytes 294920 | tf_op jit(solution)/shard_map/ppermute | solution.py:277
  109.0 1.1 collective-permute-start.31
  110.1 2.7 %collective-permute-done.16 = bf16[48,1024]{1,0:T(8,128)(2,1)S(1)} collective-permute-done((bf16[48,1024]{1,0:T(8,128)(2,1)S(1)}, bf16[48,1024]{1,0:T(8,128)(2,1)S(1)}, u32[]{:S(2)}, u32[]{:S(2)}) %collective-permute-start.16) | collective-permute-done | bytes 98336 | tf_op jit(solution)/shard_map/ppermute | solution.py:277
  112.8 2.0 %collective-permute-start.29 = (bf16[48,1024]{1,0:T(8,128)(2,1)S(1)}, bf16[48,1024]{1,0:T(8,128)(2,1)S(1)}, u32[]{:S(2)}, u32[]{:S(2)}) collective-permute-start(bf16[48,1024]{1,0:T(8,128)(2,1)S(1)} %get-tuple-element.86), channel_id=1, source_target_pairs={{0,2},{1,3},{2,0},{3,1},{4,6},{5,7},{6,4},{7,5},{8,10},{9,11},{10,... | collective-permute-start | bytes 294920 | tf_op jit(solution)/shard_map/ppermute | solution.py:277
  114.9 0.7 collective-permute-done.31
  115.6 6.6 %collective-permute-start.26 = (bf16[48,1024]{1,0:T(8,128)(2,1)S(1)}, bf16[48,1024]{1,0:T(8,128)(2,1)S(1)}, u32[]{:S(2)}, u32[]{:S(2)}) collective-permute-start(bf16[48,1024]{1,0:T(8,128)(2,1)S(1)} %get-tuple-element.81), channel_id=1, source_target_pairs={{0,2},{1,3},{2,0},{3,1},{4,6},{5,7},{6,4},{7,5},{8,10},{9,11},{10,... | collective-permute-start | bytes 294920 | tf_op jit(solution)/shard_map/ppermute | solution.py:277
  122.2 0.5 collective-permute-done.30
  122.6 1.5 collective-permute-start.35
  124.1 1.5 collective-permute-start.18
  125.7 0.6 collective-permute-start.36
  126.4 1.5 collective-permute-start.37
  127.8 0.5 collective-permute-start.32
  128.4 7.7 %collective-permute-done.18 = bf16[192,1024]{1,0:T(8,128)(2,1)S(1)} collective-permute-done((bf16[192,1024]{1,0:T(8,128)(2,1)S(1)}, bf16[192,1024]{1,0:T(8,128)(2,1)S(1)}, u32[]{:S(2)}, u32[]{:S(2)}) %collective-permute-start.18) | collective-permute-done | bytes 393248 | tf_op jit(solution)/shard_map/ppermute | solution.py:277
  136.2 4.1 %collective-permute-done.32.refs_1_ = bf16[96,1024]{1,0:T(8,128)(2,1)S(1)} collective-permute-done((bf16[96,1024]{1,0:T(8,128)(2,1)S(1)}, bf16[96,1024]{1,0:T(8,128)(2,1)S(1)}, u32[]{:S(2)}, u32[]{:S(2)}) %collective-permute-start.32) | collective-permute-done | bytes 196640 | tf_op jit(solution)/shard_map/ppermute | solution.py:277
  140.3 0.6 collective-permute-start.19
  141.0 0.6 fusion.34.own_ref
  141.6 5.9 %collective-permute-done.34.refs_3_ = bf16[96,1024]{1,0:T(8,128)(2,1)S(1)} collective-permute-done((bf16[96,1024]{1,0:T(8,128)(2,1)S(1)}, bf16[96,1024]{1,0:T(8,128)(2,1)S(1)}, u32[]{:S(2)}, u32[]{:S(2)}) %collective-permute-start.34) | collective-permute-done | bytes 196640 | tf_op jit(solution)/shard_map/ppermute | solution.py:277
  147.5 1.3 fold.3
  148.8 0.9 collective-permute-done.36
  149.8 0.6 add_convert_fusion.down_ref
  150.4 1.2 first_terms.1.whole_ref
  151.5 6.6 %collective-permute-done.37.arrived_ref = bf16[512,768]{1,0:T(8,128)(2,1)S(1)} collective-permute-done((bf16[512,768]{1,0:T(8,128)(2,1)S(1)}, bf16[512,768]{1,0:T(8,128)(2,1)S(1)}, u32[]{:S(2)}, u32[]{:S(2)}) %collective-permute-start.37) | collective-permute-done | bytes 786464 | tf_op jit(solution)/shard_map/ppermute | solution.py:277
  158.2 0.9 last_term.1
  159.1 1.3 fold.2
  (125 shorter events, 12.2 us)
Async XLA Ops:
  0.6 1.2 copy-start.1
  1.9 0.7 copy-start.3
  2.6 0.7 copy-start.4
  3.3 5.8 %copy-start.2 = (bf16[256,2048]{1,0:T(8,128)(2,1)S(1)}, bf16[256,2048]{1,0:T(8,128)(2,1)}, u32[]{:S(2)}) copy-start(bf16[256,2048]{1,0:T(8,128)(2,1)} %source_ref.1) | copy-start | bytes 3145732
  4.0 5.7 %collective-permute-start = (bf16[96,2048]{1,0:T(8,128)(2,1)S(1)}, bf16[96,2048]{1,0:T(8,128)(2,1)S(1)}, u32[]{:S(2)}, u32[]{:S(2)}) collective-permute-start(bf16[96,2048]{1,0:T(8,128)(2,1)S(1)} %get-tuple-element.48), channel_id=1, source_target_pairs={{0,1},{1,0},{2,3},{3,2},{4,5},{5,4},{6,7},{7,6},{8,9},{9,8},{10,11... | collective-permute-start | bytes 1179656 | tf_op jit(solution)/shard_map/ppermute | solution.py:277
  4.5 1.7 %copy-start = (bf16[1,512,3,768]{3,1,2,0:T(8,128)(2,1)S(1)}, bf16[1,512,3,768]{3,1,2,0:T(8,128)(2,1)}, u32[]{:S(2)}) copy-start(bf16[1,512,3,768]{3,1,2,0:T(8,128)(2,1)} %param.8) | copy-start | bytes 7077892
  6.4 54.1 %collective-permute-start.4 = (bf16[2,512,768]{2,1,0:T(8,128)(2,1)S(1)}, bf16[2,512,768]{2,1,0:T(8,128)(2,1)S(1)}, u32[]{:S(2)}, u32[]{:S(2)}) collective-permute-start(bf16[2,512,768]{2,1,0:T(8,128)(2,1)S(1)} %get-tuple-element.52), channel_id=1, source_target_pairs={{0,8},{1,17},{2,10},{3,19},{4,12},{5,21},{6,14},{7,23},{8,0},{9,25... | collective-permute-start | bytes 4718600 | tf_op jit(solution)/shard_map/ppermute | solution.py:277
  9.0 48.6 %collective-permute-start.10 = (bf16[512,768]{1,0:T(8,128)(2,1)S(1)}, bf16[512,768]{1,0:T(8,128)(2,1)S(1)}, u32[]{:S(2)}, u32[]{:S(2)}) collective-permute-start(bf16[512,768]{1,0:T(8,128)(2,1)S(1)} %get-tuple-element.62), channel_id=1, source_target_pairs={{0,8},{1,17},{2,10},{3,19},{4,12},{5,21},{6,14},{7,23},{8,0},{9,25... | collective-permute-start | bytes 2359304 | tf_op jit(solution)/shard_map/ppermute | solution.py:277
  9.4 1.8 %collective-permute-start.20 = (bf16[96,2048]{1,0:T(8,128)(2,1)S(1)}, bf16[96,2048]{1,0:T(8,128)(2,1)S(1)}, u32[]{:S(2)}, u32[]{:S(2)}) collective-permute-start(bf16[96,2048]{1,0:T(8,128)(2,1)S(1)} %get-tuple-element.72), channel_id=1, source_target_pairs={{0,1},{1,0},{2,3},{3,2},{4,5},{5,4},{6,7},{7,6},{8,9},{9,8},{10,11... | collective-permute-start | bytes 1179656 | tf_op jit(solution)/shard_map/ppermute | solution.py:277
  11.4 5.2 %collective-permute-start.1 = (bf16[48,1024]{1,0:T(8,128)(2,1)S(1)}, bf16[48,1024]{1,0:T(8,128)(2,1)S(1)}, u32[]{:S(2)}, u32[]{:S(2)}) collective-permute-start(bf16[48,1024]{1,0:T(8,128)(2,1)S(1)} %get-tuple-element.49), channel_id=1, source_target_pairs={{0,2},{1,3},{2,0},{3,1},{4,6},{5,7},{6,4},{7,5},{8,10},{9,11},{10,... | collective-permute-start | bytes 294920 | tf_op jit(solution)/shard_map/ppermute | solution.py:277
  13.5 10.7 %collective-permute-start.2 = (bf16[48,1024]{1,0:T(8,128)(2,1)S(1)}, bf16[48,1024]{1,0:T(8,128)(2,1)S(1)}, u32[]{:S(2)}, u32[]{:S(2)}) collective-permute-start(bf16[48,1024]{1,0:T(8,128)(2,1)S(1)} %get-tuple-element.50), channel_id=1, source_target_pairs={{0,4},{1,5},{2,6},{3,7},{4,0},{5,1},{6,2},{7,3},{8,12},{9,13},{10,... | collective-permute-start | bytes 294920 | tf_op jit(solution)/shard_map/ppermute | solution.py:277
  16.1 9.6 %collective-permute-start.3 = (bf16[48,1024]{1,0:T(8,128)(2,1)S(1)}, bf16[48,1024]{1,0:T(8,128)(2,1)S(1)}, u32[]{:S(2)}, u32[]{:S(2)}) collective-permute-start(bf16[48,1024]{1,0:T(8,128)(2,1)S(1)} %get-tuple-element.51), channel_id=1, source_target_pairs={{0,6},{1,7},{2,4},{3,5},{4,2},{5,3},{6,0},{7,1},{8,14},{9,15},{10,... | collective-permute-start | bytes 294920 | tf_op jit(solution)/shard_map/ppermute | solution.py:277
  16.6 12.0 %collective-permute-start.5 = (bf16[192,1024]{1,0:T(8,128)(2,1)S(1)}, bf16[192,1024]{1,0:T(8,128)(2,1)S(1)}, u32[]{:S(2)}, u32[]{:S(2)}) collective-permute-start(bf16[192,1024]{1,0:T(8,128)(2,1)S(1)} %bitcast.150), channel_id=1, source_target_pairs={{0,16},{1,9},{2,18},{3,11},{4,20},{5,13},{6,22},{7,15},{8,24},{9,1... | collective-permute-start | bytes 1179656 | tf_op jit(solution)/shard_map/ppermute | solution.py:277
  24.2 12.8 %collective-permute-start.21 = (bf16[192,1024]{1,0:T(8,128)(2,1)S(1)}, bf16[192,1024]{1,0:T(8,128)(2,1)S(1)}, u32[]{:S(2)}, u32[]{:S(2)}) collective-permute-start(bf16[192,1024]{1,0:T(8,128)(2,1)S(1)} %bitcast.148), channel_id=1, source_target_pairs={{0,16},{1,9},{2,18},{3,11},{4,20},{5,13},{6,22},{7,15},{8,24},{9,1... | collective-permute-start | bytes 1179656 | tf_op jit(solution)/shard_map/ppermute | solution.py:277
  28.6 10.3 %collective-permute-start.8 = (bf16[48,1024]{1,0:T(8,128)(2,1)S(1)}, bf16[48,1024]{1,0:T(8,128)(2,1)S(1)}, u32[]{:S(2)}, u32[]{:S(2)}) collective-permute-start(bf16[48,1024]{1,0:T(8,128)(2,1)S(1)} %get-tuple-element.58), channel_id=1, source_target_pairs={{0,6},{1,7},{2,4},{3,5},{4,2},{5,3},{6,0},{7,1},{8,14},{9,15},{10,... | collective-permute-start | bytes 294920 | tf_op jit(solution)/shard_map/ppermute | solution.py:277
  33.5 6.8 %collective-permute-start.7 = (bf16[48,1024]{1,0:T(8,128)(2,1)S(1)}, bf16[48,1024]{1,0:T(8,128)(2,1)S(1)}, u32[]{:S(2)}, u32[]{:S(2)}) collective-permute-start(bf16[48,1024]{1,0:T(8,128)(2,1)S(1)} %get-tuple-element.57), channel_id=1, source_target_pairs={{0,4},{1,5},{2,6},{3,7},{4,0},{5,1},{6,2},{7,3},{8,12},{9,13},{10,... | collective-permute-start | bytes 294920 | tf_op jit(solution)/shard_map/ppermute | solution.py:277
  37.0 5.8 %collective-permute-start.6 = (bf16[48,1024]{1,0:T(8,128)(2,1)S(1)}, bf16[48,1024]{1,0:T(8,128)(2,1)S(1)}, u32[]{:S(2)}, u32[]{:S(2)}) collective-permute-start(bf16[48,1024]{1,0:T(8,128)(2,1)S(1)} %get-tuple-element.56), channel_id=1, source_target_pairs={{0,2},{1,3},{2,0},{3,1},{4,6},{5,7},{6,4},{7,5},{8,10},{9,11},{10,... | collective-permute-start | bytes 294920 | tf_op jit(solution)/shard_map/ppermute | solution.py:277
  38.9 11.0 %collective-permute-start.22 = (bf16[96,1024]{1,0:T(8,128)(2,1)S(1)}, bf16[96,1024]{1,0:T(8,128)(2,1)S(1)}, u32[]{:S(2)}, u32[]{:S(2)}) collective-permute-start(bf16[96,1024]{1,0:T(8,128)(2,1)S(1)} %pad_maximum_fusion.28), channel_id=1, source_target_pairs={{0,2},{1,3},{2,0},{3,1},{4,6},{5,7},{6,4},{7,5},{8,10},{9,11},{10,... | collective-permute-start | bytes 589832 | tf_op jit(solution)/shard_map/ppermute | solution.py:277
  40.2 17.1 %collective-permute-start.23 = (bf16[96,1024]{1,0:T(8,128)(2,1)S(1)}, bf16[96,1024]{1,0:T(8,128)(2,1)S(1)}, u32[]{:S(2)}, u32[]{:S(2)}) collective-permute-start(bf16[96,1024]{1,0:T(8,128)(2,1)S(1)} %pad_maximum_fusion.26), channel_id=1, source_target_pairs={{0,4},{1,5},{2,6},{3,7},{4,0},{5,1},{6,2},{7,3},{8,12},{9,13},{10,... | collective-permute-start | bytes 589832 | tf_op jit(solution)/shard_map/ppermute | solution.py:277
  42.8 14.5 %collective-permute-start.24 = (bf16[96,1024]{1,0:T(8,128)(2,1)S(1)}, bf16[96,1024]{1,0:T(8,128)(2,1)S(1)}, u32[]{:S(2)}, u32[]{:S(2)}) collective-permute-start(bf16[96,1024]{1,0:T(8,128)(2,1)S(1)} %pad_maximum_fusion.27), channel_id=1, source_target_pairs={{0,6},{1,7},{2,4},{3,5},{4,2},{5,3},{6,0},{7,1},{8,14},{9,15},{10,... | collective-permute-start | bytes 589832 | tf_op jit(solution)/shard_map/ppermute | solution.py:277
  58.9 24.4 %collective-permute-start.25 = (bf16[384,768]{1,0:T(8,128)(2,1)S(1)}, bf16[384,768]{1,0:T(8,128)(2,1)S(1)}, u32[]{:S(2)}, u32[]{:S(2)}) collective-permute-start(bf16[384,768]{1,0:T(8,128)(2,1)S(1)} %pad_maximum_fusion.2), channel_id=1, source_target_pairs={{0,16},{1,9},{2,18},{3,11},{4,20},{5,13},{6,22},{7,15},{8,24},{9,1... | collective-permute-start | bytes 1769480 | tf_op jit(solution)/shard_map/ppermute | solution.py:277
  61.2 13.9 %collective-permute-start.9 = (bf16[192,1536]{1,0:T(8,128)(2,1)S(1)}, bf16[192,1536]{1,0:T(8,128)(2,1)S(1)}, u32[]{:S(2)}, u32[]{:S(2)}) collective-permute-start(bf16[192,1536]{1,0:T(8,128)(2,1)S(1)} %fusion.4), channel_id=1, source_target_pairs={{0,16},{1,9},{2,18},{3,11},{4,20},{5,13},{6,22},{7,15},{8,24},{9,1... | collective-permute-start | bytes 1769480 | tf_op jit(solution)/shard_map/ppermute | solution.py:277
  62.5 19.0 %collective-permute-start.14 = (bf16[192,1536]{1,0:T(8,128)(2,1)S(1)}, bf16[192,1536]{1,0:T(8,128)(2,1)S(1)}, u32[]{:S(2)}, u32[]{:S(2)}) collective-permute-start(bf16[192,1536]{1,0:T(8,128)(2,1)S(1)} %fusion.5), channel_id=1, source_target_pairs={{0,16},{1,9},{2,18},{3,11},{4,20},{5,13},{6,22},{7,15},{8,24},{9,1... | collective-permute-start | bytes 1769480 | tf_op jit(solution)/shard_map/ppermute | solution.py:277
  87.1 10.7 %collective-permute-start.13 = (bf16[48,1024]{1,0:T(8,128)(2,1)S(1)}, bf16[48,1024]{1,0:T(8,128)(2,1)S(1)}, u32[]{:S(2)}, u32[]{:S(2)}) collective-permute-start(bf16[48,1024]{1,0:T(8,128)(2,1)S(1)} %get-tuple-element.65), channel_id=1, source_target_pairs={{0,6},{1,7},{2,4},{3,5},{4,2},{5,3},{6,0},{7,1},{8,14},{9,15},{10,... | collective-permute-start | bytes 294920 | tf_op jit(solution)/shard_map/ppermute | solution.py:277
  89.4 16.7 %collective-permute-start.12 = (bf16[48,1024]{1,0:T(8,128)(2,1)S(1)}, bf16[48,1024]{1,0:T(8,128)(2,1)S(1)}, u32[]{:S(2)}, u32[]{:S(2)}) collective-permute-start(bf16[48,1024]{1,0:T(8,128)(2,1)S(1)} %get-tuple-element.64), channel_id=1, source_target_pairs={{0,4},{1,5},{2,6},{3,7},{4,0},{5,1},{6,2},{7,3},{8,12},{9,13},{10,... | collective-permute-start | bytes 294920 | tf_op jit(solution)/shard_map/ppermute | solution.py:277
  91.6 17.4 %collective-permute-start.11 = (bf16[48,1024]{1,0:T(8,128)(2,1)S(1)}, bf16[48,1024]{1,0:T(8,128)(2,1)S(1)}, u32[]{:S(2)}, u32[]{:S(2)}) collective-permute-start(bf16[48,1024]{1,0:T(8,128)(2,1)S(1)} %get-tuple-element.63), channel_id=1, source_target_pairs={{0,2},{1,3},{2,0},{3,1},{4,6},{5,7},{6,4},{7,5},{8,10},{9,11},{10,... | collective-permute-start | bytes 294920 | tf_op jit(solution)/shard_map/ppermute | solution.py:277
  91.7 17.3 %collective-permute-start.17 = (bf16[48,1024]{1,0:T(8,128)(2,1)S(1)}, bf16[48,1024]{1,0:T(8,128)(2,1)S(1)}, u32[]{:S(2)}, u32[]{:S(2)}) collective-permute-start(bf16[48,1024]{1,0:T(8,128)(2,1)S(1)} %get-tuple-element.69), channel_id=1, source_target_pairs={{0,6},{1,7},{2,4},{3,5},{4,2},{5,3},{6,0},{7,1},{8,14},{9,15},{10,... | collective-permute-start | bytes 294920 | tf_op jit(solution)/shard_map/ppermute | solution.py:277
  94.2 18.7 %collective-permute-start.16 = (bf16[48,1024]{1,0:T(8,128)(2,1)S(1)}, bf16[48,1024]{1,0:T(8,128)(2,1)S(1)}, u32[]{:S(2)}, u32[]{:S(2)}) collective-permute-start(bf16[48,1024]{1,0:T(8,128)(2,1)S(1)} %get-tuple-element.68), channel_id=1, source_target_pairs={{0,4},{1,5},{2,6},{3,7},{4,0},{5,1},{6,2},{7,3},{8,12},{9,13},{10,... | collective-permute-start | bytes 294920 | tf_op jit(solution)/shard_map/ppermute | solution.py:277
  97.8 15.1 %collective-permute-start.15 = (bf16[48,1024]{1,0:T(8,128)(2,1)S(1)}, bf16[48,1024]{1,0:T(8,128)(2,1)S(1)}, u32[]{:S(2)}, u32[]{:S(2)}) collective-permute-start(bf16[48,1024]{1,0:T(8,128)(2,1)S(1)} %get-tuple-element.67), channel_id=1, source_target_pairs={{0,2},{1,3},{2,0},{3,1},{4,6},{5,7},{6,4},{7,5},{8,10},{9,11},{10,... | collective-permute-start | bytes 294920 | tf_op jit(solution)/shard_map/ppermute | solution.py:277
  106.2 19.6 %collective-permute-start.28 = (bf16[48,1024]{1,0:T(8,128)(2,1)S(1)}, bf16[48,1024]{1,0:T(8,128)(2,1)S(1)}, u32[]{:S(2)}, u32[]{:S(2)}) collective-permute-start(bf16[48,1024]{1,0:T(8,128)(2,1)S(1)} %get-tuple-element.83), channel_id=1, source_target_pairs={{0,6},{1,7},{2,4},{3,5},{4,2},{5,3},{6,0},{7,1},{8,14},{9,15},{10,... | collective-permute-start | bytes 294920 | tf_op jit(solution)/shard_map/ppermute | solution.py:277
  108.9 17.4 %collective-permute-start.27 = (bf16[48,1024]{1,0:T(8,128)(2,1)S(1)}, bf16[48,1024]{1,0:T(8,128)(2,1)S(1)}, u32[]{:S(2)}, u32[]{:S(2)}) collective-permute-start(bf16[48,1024]{1,0:T(8,128)(2,1)S(1)} %get-tuple-element.82), channel_id=1, source_target_pairs={{0,4},{1,5},{2,6},{3,7},{4,0},{5,1},{6,2},{7,3},{8,12},{9,13},{10,... | collective-permute-start | bytes 294920 | tf_op jit(solution)/shard_map/ppermute | solution.py:277
  109.0 6.6 %collective-permute-start.31 = (bf16[48,1024]{1,0:T(8,128)(2,1)S(1)}, bf16[48,1024]{1,0:T(8,128)(2,1)S(1)}, u32[]{:S(2)}, u32[]{:S(2)}) collective-permute-start(bf16[48,1024]{1,0:T(8,128)(2,1)S(1)} %get-tuple-element.88), channel_id=1, source_target_pairs={{0,6},{1,7},{2,4},{3,5},{4,2},{5,3},{6,0},{7,1},{8,14},{9,15},{10,... | collective-permute-start | bytes 294920 | tf_op jit(solution)/shard_map/ppermute | solution.py:277
  112.8 9.8 %collective-permute-start.30 = (bf16[48,1024]{1,0:T(8,128)(2,1)S(1)}, bf16[48,1024]{1,0:T(8,128)(2,1)S(1)}, u32[]{:S(2)}, u32[]{:S(2)}) collective-permute-start(bf16[48,1024]{1,0:T(8,128)(2,1)S(1)} %get-tuple-element.87), channel_id=1, source_target_pairs={{0,4},{1,5},{2,6},{3,7},{4,0},{5,1},{6,2},{7,3},{8,12},{9,13},{10,... | collective-permute-start | bytes 294920 | tf_op jit(solution)/shard_map/ppermute | solution.py:277
  112.8 11.3 %collective-permute-start.29 = (bf16[48,1024]{1,0:T(8,128)(2,1)S(1)}, bf16[48,1024]{1,0:T(8,128)(2,1)S(1)}, u32[]{:S(2)}, u32[]{:S(2)}) collective-permute-start(bf16[48,1024]{1,0:T(8,128)(2,1)S(1)} %get-tuple-element.86), channel_id=1, source_target_pairs={{0,2},{1,3},{2,0},{3,1},{4,6},{5,7},{6,4},{7,5},{8,10},{9,11},{10,... | collective-permute-start | bytes 294920 | tf_op jit(solution)/shard_map/ppermute | solution.py:277
  115.6 12.3 %collective-permute-start.26 = (bf16[48,1024]{1,0:T(8,128)(2,1)S(1)}, bf16[48,1024]{1,0:T(8,128)(2,1)S(1)}, u32[]{:S(2)}, u32[]{:S(2)}) collective-permute-start(bf16[48,1024]{1,0:T(8,128)(2,1)S(1)} %get-tuple-element.81), channel_id=1, source_target_pairs={{0,2},{1,3},{2,0},{3,1},{4,6},{5,7},{6,4},{7,5},{8,10},{9,11},{10,... | collective-permute-start | bytes 294920 | tf_op jit(solution)/shard_map/ppermute | solution.py:277
  122.6 27.7 %collective-permute-start.35 = (bf16[512,768]{1,0:T(8,128)(2,1)S(1)}, bf16[512,768]{1,0:T(8,128)(2,1)S(1)}, u32[]{:S(2)}, u32[]{:S(2)}) collective-permute-start(bf16[512,768]{1,0:T(8,128)(2,1)S(1)} %convolution_convert_fusion.2), channel_id=1, source_target_pairs={{0,8},{1,17},{2,10},{3,19},{4,12},{5,21},{6,14},{7,23},{8,0},{9,25... | collective-permute-start | bytes 2359304 | tf_op jit(solution)/shard_map/ppermute | solution.py:277
  124.1 12.0 %collective-permute-start.18 = (bf16[192,1024]{1,0:T(8,128)(2,1)S(1)}, bf16[192,1024]{1,0:T(8,128)(2,1)S(1)}, u32[]{:S(2)}, u32[]{:S(2)}) collective-permute-start(bf16[192,1024]{1,0:T(8,128)(2,1)S(1)} %pad_maximum_fusion.15), channel_id=1, source_target_pairs={{0,16},{1,9},{2,18},{3,11},{4,20},{5,13},{6,22},{7,15},{8,24},{9,1... | collective-permute-start | bytes 1179656 | tf_op jit(solution)/shard_map/ppermute | solution.py:277
  125.7 24.0 %collective-permute-start.36 = (bf16[512,768]{1,0:T(8,128)(2,1)S(1)}, bf16[512,768]{1,0:T(8,128)(2,1)S(1)}, u32[]{:S(2)}, u32[]{:S(2)}) collective-permute-start(bf16[512,768]{1,0:T(8,128)(2,1)S(1)} %convolution_convert_fusion.1), channel_id=1, source_target_pairs={{0,8},{1,17},{2,10},{3,19},{4,12},{5,21},{6,14},{7,23},{8,0},{9,25... | collective-permute-start | bytes 2359304 | tf_op jit(solution)/shard_map/ppermute | solution.py:277
  126.4 31.8 %collective-permute-start.37 = (bf16[512,768]{1,0:T(8,128)(2,1)S(1)}, bf16[512,768]{1,0:T(8,128)(2,1)S(1)}, u32[]{:S(2)}, u32[]{:S(2)}) collective-permute-start(bf16[512,768]{1,0:T(8,128)(2,1)S(1)} %convolution_convert_fusion), channel_id=1, source_target_pairs={{0,8},{1,17},{2,10},{3,19},{4,12},{5,21},{6,14},{7,23},{8,0},{9,25... | collective-permute-start | bytes 2359304 | tf_op jit(solution)/shard_map/ppermute | solution.py:277
  127.8 12.5 %collective-permute-start.32 = (bf16[96,1024]{1,0:T(8,128)(2,1)S(1)}, bf16[96,1024]{1,0:T(8,128)(2,1)S(1)}, u32[]{:S(2)}, u32[]{:S(2)}) collective-permute-start(bf16[96,1024]{1,0:T(8,128)(2,1)S(1)} %bitcast.152), channel_id=1, source_target_pairs={{0,16},{1,9},{2,18},{3,11},{4,20},{5,13},{6,22},{7,15},{8,24},{9,1... | collective-permute-start | bytes 589832 | tf_op jit(solution)/shard_map/ppermute | solution.py:277
  136.1 4.2 %collective-permute-start.33 = (bf16[96,1024]{1,0:T(8,128)(2,1)S(1)}, bf16[96,1024]{1,0:T(8,128)(2,1)S(1)}, u32[]{:S(2)}, u32[]{:S(2)}) collective-permute-start(bf16[96,1024]{1,0:T(8,128)(2,1)S(1)} %bitcast.153), channel_id=1, source_target_pairs={{0,1},{1,0},{2,3},{3,2},{4,5},{5,4},{6,7},{7,6},{8,9},{9,8},{10,11... | collective-permute-start | bytes 589832 | tf_op jit(solution)/shard_map/ppermute | solution.py:277
  140.3 7.2 %collective-permute-start.34 = (bf16[96,1024]{1,0:T(8,128)(2,1)S(1)}, bf16[96,1024]{1,0:T(8,128)(2,1)S(1)}, u32[]{:S(2)}, u32[]{:S(2)}) collective-permute-start(bf16[96,1024]{1,0:T(8,128)(2,1)S(1)} %bitcast.151), channel_id=1, source_target_pairs={{0,17},{1,8},{2,19},{3,10},{4,21},{5,12},{6,23},{7,14},{8,25},{9,0... | collective-permute-start | bytes 589832 | tf_op jit(solution)/shard_map/ppermute | solution.py:277
  140.3 18.8 %collective-permute-start.19 = (bf16[96,2048]{1,0:T(8,128)(2,1)S(1)}, bf16[96,2048]{1,0:T(8,128)(2,1)S(1)}, u32[]{:S(2)}, u32[]{:S(2)}) collective-permute-start(bf16[96,2048]{1,0:T(8,128)(2,1)S(1)} %pad_maximum_fusion.16), channel_id=1, source_target_pairs={{0,1},{1,0},{2,3},{3,2},{4,5},{5,4},{6,7},{7,6},{8,9},{9,8},{10,11... | collective-permute-start | bytes 1179656 | tf_op jit(solution)/shard_map/ppermute | solution.py:277
